TPU v7x, 256 devices: a whole 4x4x8 slice. The times are simulated.
256 devices in a mesh: sweep: 16 (over z, y_hi), cross: 16 (over y_lo, x, core).
Axes of the slice: x: 4, y: 4 (y_hi: 2, y_lo: 2; y = y_hi * 2 + y_lo), z: 8, core: 2. Of those that a mesh axis runs over, the one named last changes fastest.
Arguments:
- right_side: bfloat16 [32, 64, 320, 128], P('sweep', 'cross'), may hold values from -6 to 6
- diag_inv: bfloat16 [32, 64, 320, 320], P('sweep', 'cross')
- diag_blk: bfloat16 [32, 64, 320, 320], P('sweep', 'cross')
- lower_blk: bfloat16 [32, 64, 320, 320], P('sweep', 'cross')
- upper_blk: bfloat16 [32, 64, 320, 320], P('sweep', 'cross')
- cross_minus: bfloat16 [32, 64, 320, 320], P('sweep', 'cross')
- cross_plus: bfloat16 [32, 64, 320, 320], P('sweep', 'cross')
- elem_slot: int32 [32, 64], P('sweep', 'cross'), may hold values from 0 to 7, as said below
Outputs:
- precond: bfloat16 [32, 64, 320, 128], P('sweep', 'cross')
- jacobian_prod: bfloat16 [32, 64, 320, 128], P('sweep', 'cross')
Inputs may be any that keep to these rules, and one draw needn't show every extreme that they name: `elem_slot`: within each aligned block of 2 slabs by 4 pencils the entries are a permutation of 0 to 7.
All inputs are finite; a program needn't handle non-finite values.
Results may differ from a plain program's by a relative error of at most 0.0083.
Values may be sent and summed in bfloat16 or wider, within the bound.
No kernel may reach another device: no remote copies, remote signals or barrier semaphores. Data moves between devices by JAX's collectives and lax.ppermute only.
A program may use at most 256 MiB of HBM per device.

v0:
```python
import jax
import jax.numpy as jnp
from jax import lax
from jax.sharding import PartitionSpec as P


def passed_along(value, axis, steps):
    count = lax.axis_size(axis)
    leading, last = (max(0, -steps), min(count, count - steps))
    return lax.ppermute(value, axis, [(source, source + steps) for source in range(leading, last)])


def with_halo(cells, sides, width):
    for axis, dim in sides:
        count = lax.axis_size(axis)
        ends = count - 1
        head = lax.slice_in_dim(cells, 0, width, axis=dim)
        tail = lax.slice_in_dim(cells, cells.shape[dim] - width, cells.shape[dim], axis=dim)
        cells = jnp.concatenate(
            [
                lax.ppermute(tail, axis, [(i, (i + 1) % count) for i in range(ends)]),
                cells,
                lax.ppermute(head, axis, [((i + 1) % count, i) for i in range(ends)]),
            ],
            axis=dim,
        )
    return cells


def apply_blocks(blocks, vectors):
    return jnp.einsum(
        "pij,pjr->pir", blocks.astype(jnp.float32), vectors, precision=lax.Precision.HIGHEST
    )


def apply_native(blocks, vectors):
    return jnp.einsum("spij,spjr->spir", blocks, vectors, preferred_element_type=jnp.float32)


def forward_slabs(inverse, lower_blocks, source, front_in):
    values = []
    current = front_in
    for slab in range(inverse.shape[0]):
        current = apply_blocks(
            inverse[slab],
            source[slab].astype(jnp.float32) - apply_blocks(lower_blocks[slab], current),
        )
        values.append(current)
    return (jnp.stack(values), current)


def backward_slabs(inverse, upper_blocks, forward_part, front_in):
    values = [None] * inverse.shape[0]
    current = front_in
    for slab in reversed(range(inverse.shape[0])):
        current = forward_part[slab] - apply_blocks(
            inverse[slab], apply_blocks(upper_blocks[slab], current)
        )
        values[slab] = current
    return (jnp.stack(values), current)


def local(right_side, diag_inv, diag_blk, lower_blk, upper_blk, cross_minus, cross_plus, elem_slot):
    slab_count, pencil_count = elem_slot.shape
    block_size = right_side.shape[2]
    column_total = right_side.shape[3]
    slot_order = elem_slot.reshape(-1)

    def to_sweep(values):
        flattened = values.reshape((slab_count * pencil_count,) + values.shape[2:])
        return jnp.take(flattened, slot_order, axis=0).reshape(values.shape)

    def to_store(values):
        flattened = values.reshape((slab_count * pencil_count,) + values.shape[2:])
        placed = jnp.zeros_like(flattened).at[slot_order].set(flattened)
        return placed.reshape(values.shape)

    source = to_sweep(right_side)
    inverse = to_sweep(diag_inv)
    diagonal_sorted = to_sweep(diag_blk)
    lower_sorted = to_sweep(lower_blk)
    upper_sorted = to_sweep(upper_blk)
    minus_sorted = to_sweep(cross_minus)
    plus_sorted = to_sweep(cross_plus)
    piece_count = 1
    piece_width = column_total // piece_count
    devices = lax.axis_size("sweep")
    position = lax.axis_index("sweep")
    zero_piece = jnp.zeros((pencil_count, block_size, piece_width), jnp.float32)
    zero_all = jnp.zeros((slab_count, pencil_count, block_size, column_total), jnp.float32)

    def turn_forward(step_no, carry):
        forward_all, incoming = carry
        piece = step_no - position
        active = jnp.logical_and(piece >= 0, piece < piece_count)
        col_start = jnp.clip(piece, 0, piece_count - 1) * piece_width

        def working(forward_all, incoming):
            values, front_out = forward_slabs(inverse, lower_sorted, source, incoming)
            return (lax.dynamic_update_slice_in_dim(forward_all, values, col_start, 3), front_out)

        def waiting(forward_all, incoming):
            return (forward_all, jnp.zeros_like(incoming))

        forward_all, front_out = lax.cond(active, working, waiting, forward_all, incoming)
        incoming = passed_along(front_out, "sweep", 1)
        return (forward_all, incoming)

    forward_vals, _ = lax.fori_loop(
        0, devices - 1 + piece_count, turn_forward, (zero_all, zero_piece)
    )

    def turn_backward(step_no, carry):
        solved_all, incoming = carry
        piece = step_no - (devices - 1 - position)
        active = jnp.logical_and(piece >= 0, piece < piece_count)
        col_start = jnp.clip(piece, 0, piece_count - 1) * piece_width

        def working(solved_all, incoming):
            values, front_out = backward_slabs(inverse, upper_sorted, forward_vals, incoming)
            return (lax.dynamic_update_slice_in_dim(solved_all, values, col_start, 3), front_out)

        def waiting(solved_all, incoming):
            return (solved_all, jnp.zeros_like(incoming))

        solved_all, front_out = lax.cond(active, working, waiting, solved_all, incoming)
        incoming = passed_along(front_out, "sweep", -1)
        return (solved_all, incoming)

    solved_vals, _ = lax.fori_loop(
        0, devices - 1 + piece_count, turn_backward, (zero_all, zero_piece)
    )
    precond_sorted = solved_vals.astype(jnp.bfloat16)
    padded = with_halo(precond_sorted, (("sweep", 0), ("cross", 1)), 1)
    center = padded[1:-1]
    total = apply_native(diagonal_sorted, precond_sorted)
    total = total + apply_native(lower_sorted, padded[:-2, 1:-1])
    total = total + apply_native(upper_sorted, padded[2:, 1:-1])
    total = total + apply_native(minus_sorted, center[:, :-2])
    total = total + apply_native(plus_sorted, center[:, 2:])
    jacobian_sorted = total.astype(jnp.bfloat16)
    return (to_store(precond_sorted), to_store(jacobian_sorted))


def solution(mesh):
    in_specs = (
        P("sweep", "cross", None, None),
        P("sweep", "cross", None, None),
        P("sweep", "cross", None, None),
        P("sweep", "cross", None, None),
        P("sweep", "cross", None, None),
        P("sweep", "cross", None, None),
        P("sweep", "cross", None, None),
        P("sweep", "cross"),
    )
    out_specs = (P("sweep", "cross", None, None), P("sweep", "cross", None, None))
    return jax.shard_map(local, mesh=mesh, in_specs=in_specs, out_specs=out_specs, check_vma=False)
```

profile of v0, /device:TPU:8, one launch (start us, length us, event | category | flops | bytes accessed | tf_op | source)
XLA Modules:
  0.0 803.3 jit_solution(6338139744823519513)
XLA Ops:
  36.9 319.2 %while.38 = (s32[]{:T(128)}, f32[2,4,320,128]{3,2,1,0:T(8,128)}, f32[4,320,128]{2,1,0:T(8,128)}, s32[]{:T(128)}, bf16[2,4,320,128]{3,2,1,0:T(8,128)(2,1)S(1)}, /...) while((s32[]{:T(128)}, f32[2,4,320,128]{3,2,1,0:T(8,128)}, ...), condition=%wide.region_3.5_spmd, body=%wide.region_0.4_spmd.sunk | while | flops 2517565440 | bytes 28180756 | solution.py:109
  47.5 13.8 %collective-permute-done = f32[4,320,128]{2,1,0:T(8,128)} collective-permute-done((f32[4,320,128]{2,1,0:T(8,128)}, f32[4,320,128]{2,1,0:T(8,128)}, u32[]{:S(2)}, u32[]{:S(2)}) %collective-permute-start) | collective-permute-done | bytes 655392 | tf_op jit(solution)/shard_map/while/body/eval_jaxpr/ppermute | solution.py:10
  62.1 14.3 %collective-permute-start = (f32[4,320,128]{2,1,0:T(8,128)}, f32[4,320,128]{2,1,0:T(8,128)}, u32[]{:S(2)}, u32[]{:S(2)}) collective-permute-start(f32[4,320,128]{2,1,0:T(8,128)} %get-tuple-element.477), channel_id=1, source_target_pairs={{0,16},{16,32},{32,48},{48,64},{64,80},{80,96},{96,112},{112,128},... | collective-permute-start | bytes 1966088 | tf_op jit(solution)/shard_map/while/body/eval_jaxpr/ppermute | solution.py:10
  76.4 12.9 %collective-permute-done = f32[4,320,128]{2,1,0:T(8,128)} collective-permute-done((f32[4,320,128]{2,1,0:T(8,128)}, f32[4,320,128]{2,1,0:T(8,128)}, u32[]{:S(2)}, u32[]{:S(2)}) %collective-permute-start) | collective-permute-done | bytes 655392 | tf_op jit(solution)/shard_map/while/body/eval_jaxpr/ppermute | solution.py:10
  96.9 12.0 %collective-permute-done = f32[4,320,128]{2,1,0:T(8,128)} collective-permute-done((f32[4,320,128]{2,1,0:T(8,128)}, f32[4,320,128]{2,1,0:T(8,128)}, u32[]{:S(2)}, u32[]{:S(2)}) %collective-permute-start) | collective-permute-done | bytes 655392 | tf_op jit(solution)/shard_map/while/body/eval_jaxpr/ppermute | solution.py:10
  109.8 11.8 %collective-permute-start = (f32[4,320,128]{2,1,0:T(8,128)}, f32[4,320,128]{2,1,0:T(8,128)}, u32[]{:S(2)}, u32[]{:S(2)}) collective-permute-start(f32[4,320,128]{2,1,0:T(8,128)} %get-tuple-element.477), channel_id=1, source_target_pairs={{0,16},{16,32},{32,48},{48,64},{64,80},{80,96},{96,112},{112,128},... | collective-permute-start | bytes 1966088 | tf_op jit(solution)/shard_map/while/body/eval_jaxpr/ppermute | solution.py:10
  299.1 12.2 %collective-permute-start = (f32[4,320,128]{2,1,0:T(8,128)}, f32[4,320,128]{2,1,0:T(8,128)}, u32[]{:S(2)}, u32[]{:S(2)}) collective-permute-start(f32[4,320,128]{2,1,0:T(8,128)} %get-tuple-element.477), channel_id=1, source_target_pairs={{0,16},{16,32},{32,48},{48,64},{64,80},{80,96},{96,112},{112,128},... | collective-permute-start | bytes 1966088 | tf_op jit(solution)/shard_map/while/body/eval_jaxpr/ppermute | solution.py:10
  356.1 415.5 %while.39 = (s32[]{:T(128)}, bf16[2,4,320,128]{3,2,1,0:T(8,128)(2,1)S(1)}, f32[4,320,128]{2,1,0:T(8,128)S(1)}, s32[]{:T(128)}, f32[2,4,320,128]{3,2,1,0:T(8,128)...) while((s32[]{:T(128)}, ...), condition=%wide.region_7.9_spmd, body=%wide.region_4.0_spmd.sunk | while | flops 2517237760 | bytes 33423664 | solution.py:130
  358.3 18.0 %collective-permute-done.1 = f32[4,320,128]{2,1,0:T(8,128)S(1)} collective-permute-done((f32[4,320,128]{2,1,0:T(8,128)}, f32[4,320,128]{2,1,0:T(8,128)S(1)}, u32[]{:S(2)}, u32[]{:S(2)}) %collective-permute-start.1) | collective-permute-done | bytes 655392 | tf_op jit(solution)/shard_map/while/body/eval_jaxpr/ppermute | solution.py:10
  378.5 27.9 %collective-permute-done.1 = f32[4,320,128]{2,1,0:T(8,128)S(1)} collective-permute-done((f32[4,320,128]{2,1,0:T(8,128)}, f32[4,320,128]{2,1,0:T(8,128)S(1)}, u32[]{:S(2)}, u32[]{:S(2)}) %collective-permute-start.1) | collective-permute-done | bytes 655392 | tf_op jit(solution)/shard_map/while/body/eval_jaxpr/ppermute | solution.py:10
  408.6 18.2 %collective-permute-done.1 = f32[4,320,128]{2,1,0:T(8,128)S(1)} collective-permute-done((f32[4,320,128]{2,1,0:T(8,128)}, f32[4,320,128]{2,1,0:T(8,128)S(1)}, u32[]{:S(2)}, u32[]{:S(2)}) %collective-permute-start.1) | collective-permute-done | bytes 655392 | tf_op jit(solution)/shard_map/while/body/eval_jaxpr/ppermute | solution.py:10
  428.9 26.5 %collective-permute-done.1 = f32[4,320,128]{2,1,0:T(8,128)S(1)} collective-permute-done((f32[4,320,128]{2,1,0:T(8,128)}, f32[4,320,128]{2,1,0:T(8,128)S(1)}, u32[]{:S(2)}, u32[]{:S(2)}) %collective-permute-start.1) | collective-permute-done | bytes 655392 | tf_op jit(solution)/shard_map/while/body/eval_jaxpr/ppermute | solution.py:10
  457.7 19.0 %collective-permute-done.1 = f32[4,320,128]{2,1,0:T(8,128)S(1)} collective-permute-done((f32[4,320,128]{2,1,0:T(8,128)}, f32[4,320,128]{2,1,0:T(8,128)S(1)}, u32[]{:S(2)}, u32[]{:S(2)}) %collective-permute-start.1) | collective-permute-done | bytes 655392 | tf_op jit(solution)/shard_map/while/body/eval_jaxpr/ppermute | solution.py:10
  478.8 18.0 %collective-permute-done.1 = f32[4,320,128]{2,1,0:T(8,128)S(1)} collective-permute-done((f32[4,320,128]{2,1,0:T(8,128)}, f32[4,320,128]{2,1,0:T(8,128)S(1)}, u32[]{:S(2)}, u32[]{:S(2)}) %collective-permute-start.1) | collective-permute-done | bytes 655392 | tf_op jit(solution)/shard_map/while/body/eval_jaxpr/ppermute | solution.py:10
  499.0 17.0 %collective-permute-done.1 = f32[4,320,128]{2,1,0:T(8,128)S(1)} collective-permute-done((f32[4,320,128]{2,1,0:T(8,128)}, f32[4,320,128]{2,1,0:T(8,128)S(1)}, u32[]{:S(2)}, u32[]{:S(2)}) %collective-permute-start.1) | collective-permute-done | bytes 655392 | tf_op jit(solution)/shard_map/while/body/eval_jaxpr/ppermute | solution.py:10
  518.2 34.2 %collective-permute-done.1 = f32[4,320,128]{2,1,0:T(8,128)S(1)} collective-permute-done((f32[4,320,128]{2,1,0:T(8,128)}, f32[4,320,128]{2,1,0:T(8,128)S(1)}, u32[]{:S(2)}, u32[]{:S(2)}) %collective-permute-start.1) | collective-permute-done | bytes 655392 | tf_op jit(solution)/shard_map/while/body/eval_jaxpr/ppermute | solution.py:10
  554.6 16.4 %collective-permute-done.1 = f32[4,320,128]{2,1,0:T(8,128)S(1)} collective-permute-done((f32[4,320,128]{2,1,0:T(8,128)}, f32[4,320,128]{2,1,0:T(8,128)S(1)}, u32[]{:S(2)}, u32[]{:S(2)}) %collective-permute-start.1) | collective-permute-done | bytes 655392 | tf_op jit(solution)/shard_map/while/body/eval_jaxpr/ppermute | solution.py:10
  573.2 15.5 %collective-permute-done.1 = f32[4,320,128]{2,1,0:T(8,128)S(1)} collective-permute-done((f32[4,320,128]{2,1,0:T(8,128)}, f32[4,320,128]{2,1,0:T(8,128)S(1)}, u32[]{:S(2)}, u32[]{:S(2)}) %collective-permute-start.1) | collective-permute-done | bytes 655392 | tf_op jit(solution)/shard_map/while/body/eval_jaxpr/ppermute | solution.py:10
  590.8 14.5 %collective-permute-done.1 = f32[4,320,128]{2,1,0:T(8,128)S(1)} collective-permute-done((f32[4,320,128]{2,1,0:T(8,128)}, f32[4,320,128]{2,1,0:T(8,128)S(1)}, u32[]{:S(2)}, u32[]{:S(2)}) %collective-permute-start.1) | collective-permute-done | bytes 655392 | tf_op jit(solution)/shard_map/while/body/eval_jaxpr/ppermute | solution.py:10
  607.5 13.6 %collective-permute-done.1 = f32[4,320,128]{2,1,0:T(8,128)S(1)} collective-permute-done((f32[4,320,128]{2,1,0:T(8,128)}, f32[4,320,128]{2,1,0:T(8,128)S(1)}, u32[]{:S(2)}, u32[]{:S(2)}) %collective-permute-start.1) | collective-permute-done | bytes 655392 | tf_op jit(solution)/shard_map/while/body/eval_jaxpr/ppermute | solution.py:10
  623.3 13.7 %collective-permute-done.1 = f32[4,320,128]{2,1,0:T(8,128)S(1)} collective-permute-done((f32[4,320,128]{2,1,0:T(8,128)}, f32[4,320,128]{2,1,0:T(8,128)S(1)}, u32[]{:S(2)}, u32[]{:S(2)}) %collective-permute-start.1) | collective-permute-done | bytes 655392 | tf_op jit(solution)/shard_map/while/body/eval_jaxpr/ppermute | solution.py:10
  639.1 13.8 %collective-permute-done.1 = f32[4,320,128]{2,1,0:T(8,128)S(1)} collective-permute-done((f32[4,320,128]{2,1,0:T(8,128)}, f32[4,320,128]{2,1,0:T(8,128)S(1)}, u32[]{:S(2)}, u32[]{:S(2)}) %collective-permute-start.1) | collective-permute-done | bytes 655392 | tf_op jit(solution)/shard_map/while/body/eval_jaxpr/ppermute | solution.py:10
  655.1 94.0 %collective-permute-done.1 = f32[4,320,128]{2,1,0:T(8,128)S(1)} collective-permute-done((f32[4,320,128]{2,1,0:T(8,128)}, f32[4,320,128]{2,1,0:T(8,128)S(1)}, u32[]{:S(2)}, u32[]{:S(2)}) %collective-permute-start.1) | collective-permute-done | bytes 655392 | tf_op jit(solution)/shard_map/while/body/eval_jaxpr/ppermute | solution.py:10
  758.7 12.9 %collective-permute-done.1 = f32[4,320,128]{2,1,0:T(8,128)S(1)} collective-permute-done((f32[4,320,128]{2,1,0:T(8,128)}, f32[4,320,128]{2,1,0:T(8,128)S(1)}, u32[]{:S(2)}, u32[]{:S(2)}) %collective-permute-start.1) | collective-permute-done | bytes 655392 | tf_op jit(solution)/shard_map/while/body/eval_jaxpr/ppermute | solution.py:10
  (178 shorter events, 395.2 us)
Async XLA Ops:
  45.4 15.9 %collective-permute-start = (f32[4,320,128]{2,1,0:T(8,128)}, f32[4,320,128]{2,1,0:T(8,128)}, u32[]{:S(2)}, u32[]{:S(2)}) collective-permute-start(f32[4,320,128]{2,1,0:T(8,128)} %get-tuple-element.477), channel_id=1, source_target_pairs={{0,16},{16,32},{32,48},{48,64},{64,80},{80,96},{96,112},{112,128},... | collective-permute-start | bytes 1966088 | tf_op jit(solution)/shard_map/while/body/eval_jaxpr/ppermute | solution.py:10
  62.1 27.2 %collective-permute-start = (f32[4,320,128]{2,1,0:T(8,128)}, f32[4,320,128]{2,1,0:T(8,128)}, u32[]{:S(2)}, u32[]{:S(2)}) collective-permute-start(f32[4,320,128]{2,1,0:T(8,128)} %get-tuple-element.477), channel_id=1, source_target_pairs={{0,16},{16,32},{32,48},{48,64},{64,80},{80,96},{96,112},{112,128},... | collective-permute-start | bytes 1966088 | tf_op jit(solution)/shard_map/while/body/eval_jaxpr/ppermute | solution.py:10
  90.2 18.7 %collective-permute-start = (f32[4,320,128]{2,1,0:T(8,128)}, f32[4,320,128]{2,1,0:T(8,128)}, u32[]{:S(2)}, u32[]{:S(2)}) collective-permute-start(f32[4,320,128]{2,1,0:T(8,128)} %get-tuple-element.477), channel_id=1, source_target_pairs={{0,16},{16,32},{32,48},{48,64},{64,80},{80,96},{96,112},{112,128},... | collective-permute-start | bytes 1966088 | tf_op jit(solution)/shard_map/while/body/eval_jaxpr/ppermute | solution.py:10
  109.8 23.1 %collective-permute-start = (f32[4,320,128]{2,1,0:T(8,128)}, f32[4,320,128]{2,1,0:T(8,128)}, u32[]{:S(2)}, u32[]{:S(2)}) collective-permute-start(f32[4,320,128]{2,1,0:T(8,128)} %get-tuple-element.477), channel_id=1, source_target_pairs={{0,16},{16,32},{32,48},{48,64},{64,80},{80,96},{96,112},{112,128},... | collective-permute-start | bytes 1966088 | tf_op jit(solution)/shard_map/while/body/eval_jaxpr/ppermute | solution.py:10
  133.8 18.0 %collective-permute-start = (f32[4,320,128]{2,1,0:T(8,128)}, f32[4,320,128]{2,1,0:T(8,128)}, u32[]{:S(2)}, u32[]{:S(2)}) collective-permute-start(f32[4,320,128]{2,1,0:T(8,128)} %get-tuple-element.477), channel_id=1, source_target_pairs={{0,16},{16,32},{32,48},{48,64},{64,80},{80,96},{96,112},{112,128},... | collective-permute-start | bytes 1966088 | tf_op jit(solution)/shard_map/while/body/eval_jaxpr/ppermute | solution.py:10
  152.8 20.0 %collective-permute-start = (f32[4,320,128]{2,1,0:T(8,128)}, f32[4,320,128]{2,1,0:T(8,128)}, u32[]{:S(2)}, u32[]{:S(2)}) collective-permute-start(f32[4,320,128]{2,1,0:T(8,128)} %get-tuple-element.477), channel_id=1, source_target_pairs={{0,16},{16,32},{32,48},{48,64},{64,80},{80,96},{96,112},{112,128},... | collective-permute-start | bytes 1966088 | tf_op jit(solution)/shard_map/while/body/eval_jaxpr/ppermute | solution.py:10
  173.7 16.5 %collective-permute-start = (f32[4,320,128]{2,1,0:T(8,128)}, f32[4,320,128]{2,1,0:T(8,128)}, u32[]{:S(2)}, u32[]{:S(2)}) collective-permute-start(f32[4,320,128]{2,1,0:T(8,128)} %get-tuple-element.477), channel_id=1, source_target_pairs={{0,16},{16,32},{32,48},{48,64},{64,80},{80,96},{96,112},{112,128},... | collective-permute-start | bytes 1966088 | tf_op jit(solution)/shard_map/while/body/eval_jaxpr/ppermute | solution.py:10
  191.0 19.7 %collective-permute-start = (f32[4,320,128]{2,1,0:T(8,128)}, f32[4,320,128]{2,1,0:T(8,128)}, u32[]{:S(2)}, u32[]{:S(2)}) collective-permute-start(f32[4,320,128]{2,1,0:T(8,128)} %get-tuple-element.477), channel_id=1, source_target_pairs={{0,16},{16,32},{32,48},{48,64},{64,80},{80,96},{96,112},{112,128},... | collective-permute-start | bytes 1966088 | tf_op jit(solution)/shard_map/while/body/eval_jaxpr/ppermute | solution.py:10
  227.7 18.1 %collective-permute-start = (f32[4,320,128]{2,1,0:T(8,128)}, f32[4,320,128]{2,1,0:T(8,128)}, u32[]{:S(2)}, u32[]{:S(2)}) collective-permute-start(f32[4,320,128]{2,1,0:T(8,128)} %get-tuple-element.477), channel_id=1, source_target_pairs={{0,16},{16,32},{32,48},{48,64},{64,80},{80,96},{96,112},{112,128},... | collective-permute-start | bytes 1966088 | tf_op jit(solution)/shard_map/while/body/eval_jaxpr/ppermute | solution.py:10
  262.7 20.3 %collective-permute-start = (f32[4,320,128]{2,1,0:T(8,128)}, f32[4,320,128]{2,1,0:T(8,128)}, u32[]{:S(2)}, u32[]{:S(2)}) collective-permute-start(f32[4,320,128]{2,1,0:T(8,128)} %get-tuple-element.477), channel_id=1, source_target_pairs={{0,16},{16,32},{32,48},{48,64},{64,80},{80,96},{96,112},{112,128},... | collective-permute-start | bytes 1966088 | tf_op jit(solution)/shard_map/while/body/eval_jaxpr/ppermute | solution.py:10
  299.1 22.2 %collective-permute-start = (f32[4,320,128]{2,1,0:T(8,128)}, f32[4,320,128]{2,1,0:T(8,128)}, u32[]{:S(2)}, u32[]{:S(2)}) collective-permute-start(f32[4,320,128]{2,1,0:T(8,128)} %get-tuple-element.477), channel_id=1, source_target_pairs={{0,16},{16,32},{32,48},{48,64},{64,80},{80,96},{96,112},{112,128},... | collective-permute-start | bytes 1966088 | tf_op jit(solution)/shard_map/while/body/eval_jaxpr/ppermute | solution.py:10
  322.1 16.5 %collective-permute-start = (f32[4,320,128]{2,1,0:T(8,128)}, f32[4,320,128]{2,1,0:T(8,128)}, u32[]{:S(2)}, u32[]{:S(2)}) collective-permute-start(f32[4,320,128]{2,1,0:T(8,128)} %get-tuple-element.477), channel_id=1, source_target_pairs={{0,16},{16,32},{32,48},{48,64},{64,80},{80,96},{96,112},{112,128},... | collective-permute-start | bytes 1966088 | tf_op jit(solution)/shard_map/while/body/eval_jaxpr/ppermute | solution.py:10
  339.5 16.5 %collective-permute-start = (f32[4,320,128]{2,1,0:T(8,128)}, f32[4,320,128]{2,1,0:T(8,128)}, u32[]{:S(2)}, u32[]{:S(2)}) collective-permute-start(f32[4,320,128]{2,1,0:T(8,128)} %get-tuple-element.477), channel_id=1, source_target_pairs={{0,16},{16,32},{32,48},{48,64},{64,80},{80,96},{96,112},{112,128},... | collective-permute-start | bytes 1966088 | tf_op jit(solution)/shard_map/while/body/eval_jaxpr/ppermute | solution.py:10
  357.1 19.2 %collective-permute-start.1 = (f32[4,320,128]{2,1,0:T(8,128)}, f32[4,320,128]{2,1,0:T(8,128)S(1)}, u32[]{:S(2)}, u32[]{:S(2)}) collective-permute-start(f32[4,320,128]{2,1,0:T(8,128)} %get-tuple-element.486), channel_id=1, source_target_pairs={{16,0},{32,16},{48,32},{64,48},{80,64},{96,80},{112,96},{128,112},... | collective-permute-start | bytes 1966088 | tf_op jit(solution)/shard_map/while/body/eval_jaxpr/ppermute | solution.py:10
  377.2 29.2 %collective-permute-start.1 = (f32[4,320,128]{2,1,0:T(8,128)}, f32[4,320,128]{2,1,0:T(8,128)S(1)}, u32[]{:S(2)}, u32[]{:S(2)}) collective-permute-start(f32[4,320,128]{2,1,0:T(8,128)} %get-tuple-element.486), channel_id=1, source_target_pairs={{16,0},{32,16},{48,32},{64,48},{80,64},{96,80},{112,96},{128,112},... | collective-permute-start | bytes 1966088 | tf_op jit(solution)/shard_map/while/body/eval_jaxpr/ppermute | solution.py:10
  407.3 19.5 %collective-permute-start.1 = (f32[4,320,128]{2,1,0:T(8,128)}, f32[4,320,128]{2,1,0:T(8,128)S(1)}, u32[]{:S(2)}, u32[]{:S(2)}) collective-permute-start(f32[4,320,128]{2,1,0:T(8,128)} %get-tuple-element.486), channel_id=1, source_target_pairs={{16,0},{32,16},{48,32},{64,48},{80,64},{96,80},{112,96},{128,112},... | collective-permute-start | bytes 1966088 | tf_op jit(solution)/shard_map/while/body/eval_jaxpr/ppermute | solution.py:10
  427.6 27.8 %collective-permute-start.1 = (f32[4,320,128]{2,1,0:T(8,128)}, f32[4,320,128]{2,1,0:T(8,128)S(1)}, u32[]{:S(2)}, u32[]{:S(2)}) collective-permute-start(f32[4,320,128]{2,1,0:T(8,128)} %get-tuple-element.486), channel_id=1, source_target_pairs={{16,0},{32,16},{48,32},{64,48},{80,64},{96,80},{112,96},{128,112},... | collective-permute-start | bytes 1966088 | tf_op jit(solution)/shard_map/while/body/eval_jaxpr/ppermute | solution.py:10
  456.4 20.3 %collective-permute-start.1 = (f32[4,320,128]{2,1,0:T(8,128)}, f32[4,320,128]{2,1,0:T(8,128)S(1)}, u32[]{:S(2)}, u32[]{:S(2)}) collective-permute-start(f32[4,320,128]{2,1,0:T(8,128)} %get-tuple-element.486), channel_id=1, source_target_pairs={{16,0},{32,16},{48,32},{64,48},{80,64},{96,80},{112,96},{128,112},... | collective-permute-start | bytes 1966088 | tf_op jit(solution)/shard_map/while/body/eval_jaxpr/ppermute | solution.py:10
  477.6 19.3 %collective-permute-start.1 = (f32[4,320,128]{2,1,0:T(8,128)}, f32[4,320,128]{2,1,0:T(8,128)S(1)}, u32[]{:S(2)}, u32[]{:S(2)}) collective-permute-start(f32[4,320,128]{2,1,0:T(8,128)} %get-tuple-element.486), channel_id=1, source_target_pairs={{16,0},{32,16},{48,32},{64,48},{80,64},{96,80},{112,96},{128,112},... | collective-permute-start | bytes 1966088 | tf_op jit(solution)/shard_map/while/body/eval_jaxpr/ppermute | solution.py:10
  497.7 18.3 %collective-permute-start.1 = (f32[4,320,128]{2,1,0:T(8,128)}, f32[4,320,128]{2,1,0:T(8,128)S(1)}, u32[]{:S(2)}, u32[]{:S(2)}) collective-permute-start(f32[4,320,128]{2,1,0:T(8,128)} %get-tuple-element.486), channel_id=1, source_target_pairs={{16,0},{32,16},{48,32},{64,48},{80,64},{96,80},{112,96},{128,112},... | collective-permute-start | bytes 1966088 | tf_op jit(solution)/shard_map/while/body/eval_jaxpr/ppermute | solution.py:10
  516.9 35.5 %collective-permute-start.1 = (f32[4,320,128]{2,1,0:T(8,128)}, f32[4,320,128]{2,1,0:T(8,128)S(1)}, u32[]{:S(2)}, u32[]{:S(2)}) collective-permute-start(f32[4,320,128]{2,1,0:T(8,128)} %get-tuple-element.486), channel_id=1, source_target_pairs={{16,0},{32,16},{48,32},{64,48},{80,64},{96,80},{112,96},{128,112},... | collective-permute-start | bytes 1966088 | tf_op jit(solution)/shard_map/while/body/eval_jaxpr/ppermute | solution.py:10
  553.3 17.7 %collective-permute-start.1 = (f32[4,320,128]{2,1,0:T(8,128)}, f32[4,320,128]{2,1,0:T(8,128)S(1)}, u32[]{:S(2)}, u32[]{:S(2)}) collective-permute-start(f32[4,320,128]{2,1,0:T(8,128)} %get-tuple-element.486), channel_id=1, source_target_pairs={{16,0},{32,16},{48,32},{64,48},{80,64},{96,80},{112,96},{128,112},... | collective-permute-start | bytes 1966088 | tf_op jit(solution)/shard_map/while/body/eval_jaxpr/ppermute | solution.py:10
  571.9 16.7 %collective-permute-start.1 = (f32[4,320,128]{2,1,0:T(8,128)}, f32[4,320,128]{2,1,0:T(8,128)S(1)}, u32[]{:S(2)}, u32[]{:S(2)}) collective-permute-start(f32[4,320,128]{2,1,0:T(8,128)} %get-tuple-element.486), channel_id=1, source_target_pairs={{16,0},{32,16},{48,32},{64,48},{80,64},{96,80},{112,96},{128,112},... | collective-permute-start | bytes 1966088 | tf_op jit(solution)/shard_map/while/body/eval_jaxpr/ppermute | solution.py:10
  653.8 95.3 %collective-permute-start.1 = (f32[4,320,128]{2,1,0:T(8,128)}, f32[4,320,128]{2,1,0:T(8,128)S(1)}, u32[]{:S(2)}, u32[]{:S(2)}) collective-permute-start(f32[4,320,128]{2,1,0:T(8,128)} %get-tuple-element.486), channel_id=1, source_target_pairs={{16,0},{32,16},{48,32},{64,48},{80,64},{96,80},{112,96},{128,112},... | collective-permute-start | bytes 1966088 | tf_op jit(solution)/shard_map/while/body/eval_jaxpr/ppermute | solution.py:10
  (24 other events, 205.5 us)
where the time goes:
time: 807 us; the launch traced here: 803 us
  waiting for transfers between devices  534 us (66%)
  starting transfers between devices  175 us (22%)
  local copies, waits for them, and re-layouts  60.2 us (7%)
  matrix products  19 us (2%)
  other arithmetic  14.1 us (2%)
    ppermute x32, waiting for transfers between devices, passed_along(): lax.ppermute(value, axis, [(source, source + steps) for source in range(l...  527 us
    ppermute x32, starting transfers between devices, passed_along(): lax.ppermute(value, axis, [(source, source + steps) for source in range(l...  164 us
    another operation x34, local copies, waits for them, and re-layouts  28.3 us
    gather x7, local copies, waits for them, and re-layouts, to_sweep(): return jnp.take(flattened, slot_order, axis=0).reshape(values.shape)  21.9 us
  transfers between devices with their start and end apart: 36, of which 36 were waited for; matrix products, arithmetic and copies ran while one was open for 1% of the time, Pallas kernels for 0%

commit v1 on v0

v1 whole, which is shorter than its diff:
```python
import jax
import jax.numpy as jnp
from jax import lax
from jax.experimental import pallas as pl
from jax.experimental.pallas import tpu as pltpu
from jax.sharding import PartitionSpec as P

BF = jnp.bfloat16
F32 = jnp.float32
GROUP = 4
VMEM_LIMIT = 48 << 20


def mm(a, b):
    return jnp.dot(a, b, preferred_element_type=F32)


def packed_rows(n):
    return 2 * n + n // 2


def pack(ref, base, mat):
    n = mat.shape[0]
    half = n // 2
    ref[base : base + n, :] = mat[:, 0:128]
    ref[base + n : base + 2 * n, :] = mat[:, 128:256]
    ref[base + 2 * n : base + 2 * n + half, 0:64] = mat[0:half, 256:320]
    ref[base + 2 * n : base + 2 * n + half, 64:128] = mat[half:n, 256:320]


def unpack(ref, base, n):
    half = n // 2
    tail = ref[base + 2 * n : base + 2 * n + half, :]
    last = jnp.concatenate([tail[:, 0:64], tail[:, 64:128]], axis=0)
    return jnp.concatenate(
        [ref[base : base + n, :], ref[base + n : base + 2 * n, :], last], axis=1
    )


def local_maps_kernel(
    slots, d0, d1, l0, l1, u0, u1, r0, r1, maps, e0_out, a_out, h0_out, h1_out, y0_out, c_out
):
    n = d0.shape[0]
    rows = packed_rows(n)
    inv0, inv1 = d0[...], d1[...]
    e0 = mm(inv0, l0[...]).astype(BF)
    e1 = mm(inv1, l1[...]).astype(BF)
    h0 = mm(inv0, u0[...]).astype(BF)
    h1 = mm(inv1, u1[...]).astype(BF)
    y0 = mm(inv0, r0[...])
    y1 = mm(inv1, r1[...])
    a = mm(e1, e0).astype(BF)
    b = mm(h0, h1).astype(BF)
    c = y1 - mm(e1, y0.astype(BF))
    cb = c.astype(BF)
    g = -(e0.astype(F32) + mm(h0, a))
    h = y0 - mm(h0, cb)
    pack(maps, 0, a)
    pack(maps, rows, b)
    pack(maps, 2 * rows, g.astype(BF))
    maps[3 * rows : 3 * rows + n, :] = cb
    maps[3 * rows + n : 3 * rows + 2 * n, :] = h.astype(BF)
    e0_out[...] = e0
    a_out[...] = a
    h0_out[...] = h0
    h1_out[...] = h1
    y0_out[...] = y0
    c_out[...] = c


def local_maps(slots, diag_inv, lower, upper, source):
    n = diag_inv.shape[-1]
    cols = source.shape[-1]
    rows = 3 * packed_rows(n) + 2 * n

    def block(slab, width):
        return pl.BlockSpec((None, n, width), lambda p, sl: (sl[slab * GROUP + p], 0, 0))

    def out(width, height=n):
        return pl.BlockSpec((None, height, width), lambda p, sl: (p, 0, 0))

    shape = jax.ShapeDtypeStruct
    return pl.pallas_call(
        local_maps_kernel,
        grid_spec=pltpu.PrefetchScalarGridSpec(
            num_scalar_prefetch=1,
            grid=(GROUP,),
            in_specs=[
                block(0, n), block(1, n), block(0, n), block(1, n),
                block(0, n), block(1, n), block(0, cols), block(1, cols),
            ],
            out_specs=[out(cols, rows), out(n), out(n), out(n), out(n), out(cols), out(cols)],
        ),
        out_shape=[
            shape((GROUP, rows, cols), BF),
            shape((GROUP, n, n), BF),
            shape((GROUP, n, n), BF),
            shape((GROUP, n, n), BF),
            shape((GROUP, n, n), BF),
            shape((GROUP, n, cols), F32),
            shape((GROUP, n, cols), F32),
        ],
        compiler_params=pltpu.CompilerParams(vmem_limit_bytes=VMEM_LIMIT),
        name="local_maps",
    )(slots, diag_inv, diag_inv, lower, lower, upper, upper, source, source)


def joined(left, right):
    a_l, b_l, g_l, c_l, h_l = left
    a_r, b_r, g_r, c_r, h_r = right
    a = mm(a_r, a_l).astype(BF)
    b = mm(b_l, b_r).astype(BF)
    cb = c_l.astype(BF)
    c = mm(a_r, cb) + c_r
    g = (mm(b_l, mm(g_r, a_l).astype(BF)) + g_l.astype(F32)).astype(BF)
    h = mm(b_l, (mm(g_r, cb) + h_r).astype(BF)) + h_l
    return a, b, g, c, h


def segment(maps, j, n):
    rows = packed_rows(n)
    one = maps.at[j]
    return (
        unpack(one, 0, n),
        unpack(one, rows, n),
        unpack(one, 2 * rows, n),
        one[3 * rows : 3 * rows + n, :].astype(F32),
        one[3 * rows + n : 3 * rows + 2 * n, :].astype(F32),
    )


def group_map_kernel(group, maps, a_out, b_out, g_out, c_out, h_out, send):
    n = a_out.shape[0]
    a, b, g, c, h = joined(
        joined(segment(maps, 0, n), segment(maps, 1, n)),
        joined(segment(maps, 2, n), segment(maps, 3, n)),
    )
    a_out[...] = a
    b_out[...] = b
    g_out[...] = g
    c_out[...] = c
    h_out[...] = h
    send[0:n, :] = jnp.where(group[0] == 0, c, h).astype(BF)
    pack(send, n, g)


def forward_one_kernel(a, c, incoming, send):
    n = a.shape[0]
    send[...] = (mm(a[...], incoming[0:n, :]) + c[...]).astype(BF)


def turn_kernel(a, b, g, c, h, far, incoming, send, front_out, back_in):
    n = a.shape[0]
    front = incoming[...]
    ahead = (mm(a[...], front) + c[...]).astype(BF)
    back = (mm(unpack(far, n, n), ahead) + far[0:n, :].astype(F32)).astype(BF)
    send[...] = (mm(b[...], back) + mm(g[...], front) + h[...]).astype(BF)
    front_out[...] = ahead
    back_in[...] = back


def backward_one_kernel(group, b, g, h, far, incoming, ahead, send):
    n = b.shape[0]
    back = mm(b[...], incoming[...]) + mm(g[...], far[0:n, :]) + h[...]
    send[...] = jnp.where(group[0] == 1, back.astype(BF), ahead[...])


def interfaces_kernel(group, maps, far, hop2, hop3, back2, hop4, out):
    n = hop2.shape[0]
    rows = packed_rows(n)
    which = group[0]
    zero = jnp.zeros_like(hop2[...])
    front = jnp.where(
        which == 0, zero,
        jnp.where(which == 1, far[0:n, :], jnp.where(which == 2, hop2[...], hop4[...])),
    )
    back = jnp.where(
        which == 0, hop4[...],
        jnp.where(which == 1, hop3[...], jnp.where(which == 2, back2[...], zero)),
    )
    fronts = [front]
    for j in range(GROUP - 1):
        shift = maps[j, 3 * rows : 3 * rows + n, :].astype(F32)
        front = (mm(unpack(maps.at[j], 0, n), front) + shift).astype(BF)
        fronts.append(front)
    for j in reversed(range(GROUP)):
        out[j, 0:n, :] = fronts[j]
        out[j, n : 2 * n, :] = back
        if j:
            shift = maps[j, 3 * rows + n : 3 * rows + 2 * n, :].astype(F32)
            back = (
                mm(unpack(maps.at[j], rows, n), back)
                + (mm(unpack(maps.at[j], 2 * rows, n), fronts[j]) + shift)
            ).astype(BF)


def whole_call(kernel, outs, scalars, *operands, name):
    specs = [pl.BlockSpec(memory_space=pltpu.SMEM)] * len(scalars)
    specs += [pl.BlockSpec(memory_space=pltpu.VMEM)] * len(operands)
    return pl.pallas_call(
        kernel,
        in_specs=specs,
        out_specs=[pl.BlockSpec(memory_space=pltpu.VMEM)] * len(outs),
        out_shape=[jax.ShapeDtypeStruct(s, d) for s, d in outs],
        compiler_params=pltpu.CompilerParams(vmem_limit_bytes=VMEM_LIMIT),
        name=name,
    )(*scalars, *operands)


def finish_kernel(ends, e0, a, h0, h1, y0, c, p0, p1, first, last):
    n = e0.shape[0]
    pencil = pl.program_id(0)
    front = ends[0:n, :]
    back = ends[n : 2 * n, :]
    b1 = (c[...] + mm(a[...], front) - mm(h1[...], back)).astype(BF)
    b0 = (y0[...] - mm(e0[...], front) - mm(h0[...], b1)).astype(BF)
    p0[...] = b0
    p1[...] = b1

    @pl.when(pencil == 0)
    def _():
        first[0] = b0
        first[1] = b1

    @pl.when(pencil == GROUP - 1)
    def _():
        last[0] = b0
        last[1] = b1


def finish(ends, e0, a, h0, h1, y0, c):
    n, cols = y0.shape[1:]

    def per(height, width):
        return pl.BlockSpec((None, height, width), lambda p: (p, 0, 0))

    kept = pl.BlockSpec((2, n, cols), lambda p: (0, 0, 0))
    shape = jax.ShapeDtypeStruct
    return pl.pallas_call(
        finish_kernel,
        grid=(GROUP,),
        in_specs=[
            per(2 * n, cols), per(n, n), per(n, n), per(n, n), per(n, n),
            per(n, cols), per(n, cols),
        ],
        out_specs=[per(n, cols), per(n, cols), kept, kept],
        out_shape=[
            shape((GROUP, n, cols), BF), shape((GROUP, n, cols), BF),
            shape((2, n, cols), BF), shape((2, n, cols), BF),
        ],
        compiler_params=pltpu.CompilerParams(vmem_limit_bytes=VMEM_LIMIT),
        name="finish",
    )(ends, e0, a, h0, h1, y0, c)


def jacobian_kernel(
    slots, place, diag, lower, upper, minus, plus, p0, p1, ends, below, low, high, precond, jac, grid_vals
):
    n = diag.shape[0]
    element = pl.program_id(0)
    slab = element // GROUP
    pencil = element % GROUP

    @pl.when(element == 0)
    def _():
        zero = jnp.zeros((n, p0.shape[2]), BF)
        for p in range(GROUP):
            grid_vals[0, p + 1] = jnp.where(place[0] == 0, zero, below[p])
            grid_vals[1, p + 1] = p0[p]
            grid_vals[2, p + 1] = p1[p]
            grid_vals[3, p + 1] = ends[p, n : 2 * n, :]
        for s in range(2):
            grid_vals[s + 1, 0] = jnp.where(place[1] == 0, zero, low[s])
            grid_vals[s + 1, GROUP + 1] = jnp.where(place[1] == place[2] - 1, zero, high[s])

    own = grid_vals[slab + 1, pencil + 1]
    total = mm(diag[...], own)
    total = total + mm(lower[...], grid_vals[slab, pencil + 1])
    total = total + mm(upper[...], grid_vals[slab + 2, pencil + 1])
    total = total + mm(minus[...], grid_vals[slab + 1, pencil])
    total = total + mm(plus[...], grid_vals[slab + 1, pencil + 2])
    precond[...] = own
    jac[...] = total.astype(BF)


def jacobian(slots, place, blocks, p0, p1, ends, below, low, high):
    n, cols = p0.shape[1:]
    block = pl.BlockSpec((None, n, n), lambda e, sl, pc: (sl[e], 0, 0))
    out = pl.BlockSpec((None, n, cols), lambda e, sl, pc: (sl[e], 0, 0))

    def whole(array):
        return pl.BlockSpec(array.shape, lambda e, sl, pc: (0, 0, 0))

    vectors = (p0, p1, ends, below, low, high)
    shape = jax.ShapeDtypeStruct((2 * GROUP, n, cols), BF)
    return pl.pallas_call(
        jacobian_kernel,
        grid_spec=pltpu.PrefetchScalarGridSpec(
            num_scalar_prefetch=2,
            grid=(2 * GROUP,),
            in_specs=[block] * 5 + [whole(v) for v in vectors],
            out_specs=[out, out],
            scratch_shapes=[pltpu.VMEM((4, GROUP + 2, n, cols), BF)],
        ),
        out_shape=[shape, shape],
        compiler_params=pltpu.CompilerParams(vmem_limit_bytes=VMEM_LIMIT),
        name="jacobian",
    )(slots, place, *blocks, *vectors)


def local(right_side, diag_inv, diag_blk, lower_blk, upper_blk, cross_minus, cross_plus, elem_slot):
    n, cols = right_side.shape[2:]

    def flat(values):
        return values.reshape((-1,) + values.shape[2:])

    slots = elem_slot.reshape(-1)
    count = lax.axis_size("sweep")
    across = lax.axis_size("cross")
    sweep_at = lax.axis_index("sweep")
    group = (sweep_at // GROUP).astype(jnp.int32).reshape(1)
    place = jnp.stack([sweep_at, lax.axis_index("cross"), jnp.int32(across)]).astype(jnp.int32)
    groups = [list(range(g, g + GROUP)) for g in range(0, count, GROUP)]

    def exchange(values):
        return lax.all_to_all(values, "sweep", 0, 0, axis_index_groups=groups)

    def swap(values, order):
        pairs = [(g * GROUP + k, order[g] * GROUP + k) for g in range(GROUP) for k in range(GROUP)]
        return lax.ppermute(values, "sweep", pairs)

    outer, inner = (1, 0, 3, 2), (3, 2, 1, 0)

    maps, e0, a_loc, h0, h1, y0, c_loc = local_maps(
        slots, flat(diag_inv), flat(lower_blk), flat(upper_blk), flat(right_side)
    )
    maps = exchange(maps)
    mat, vec, vec32 = ((n, n), BF), ((n, cols), BF), ((n, cols), F32)
    a, b, g, c, h, send = whole_call(
        group_map_kernel,
        [mat, mat, mat, vec32, vec32, ((n + packed_rows(n), cols), BF)],
        [group], maps, name="group_map",
    )
    far = swap(send, outer)
    (send,) = whole_call(forward_one_kernel, [vec], [], a, c, far, name="forward_one")
    hop2 = swap(send, inner)
    send, ahead, back2 = whole_call(
        turn_kernel, [vec, vec, vec], [], a, b, g, c, h, far, hop2, name="turn"
    )
    hop3 = swap(send, inner)
    (send,) = whole_call(
        backward_one_kernel, [vec], [group], b, g, h, far, hop3, ahead, name="backward_one"
    )
    hop4 = swap(send, outer)
    (ends,) = whole_call(
        interfaces_kernel, [((GROUP, 2 * n, cols), BF)], [group],
        maps, far, hop2, hop3, back2, hop4, name="interfaces",
    )
    ends = exchange(ends)
    p0, p1, first, last = finish(ends, e0, a_loc, h0, h1, y0, c_loc)
    below = lax.ppermute(p1, "sweep", [(i, (i + 1) % count) for i in range(count)])
    low = lax.ppermute(last, "cross", [(i, (i + 1) % across) for i in range(across)])
    high = lax.ppermute(first, "cross", [((i + 1) % across, i) for i in range(across)])
    blocks = [flat(x) for x in (diag_blk, lower_blk, upper_blk, cross_minus, cross_plus)]
    precond, jac = jacobian(slots, place, blocks, p0, p1, ends, below, low, high)
    return precond.reshape(right_side.shape), jac.reshape(right_side.shape)


def solution(mesh):
    blocks = P("sweep", "cross", None, None)
    in_specs = (blocks,) * 7 + (P("sweep", "cross"),)
    return jax.shard_map(
        local, mesh=mesh, in_specs=in_specs, out_specs=(blocks, blocks), check_vma=False
    )
```

time: 807 us -> 143 us (0.18)
  waiting for transfers between devices: 534 us -> 67.7 us
  starting transfers between devices: 175 us -> 23.2 us
  local copies, waits for them, and re-layouts: 60.2 us -> 8.94 us
  Pallas kernels: 0 us -> 28.3 us
  matrix products: 19 us -> 0 us
  other arithmetic: 14.1 us -> 0.08 us
  blocking collectives: 0 us -> 12.8 us
    ppermute x36 -> x7, waiting for transfers between devices: 534 us -> 30.5 us  [the longest x4 22.8 us: swap(): return lax.ppermute(values, 'sweep', pairs)]
    ppermute x36 -> x7, starting transfers between devices: 175 us -> 18.3 us  [the longest x4 13.5 us: swap(): return lax.ppermute(values, 'sweep', pairs)]
    all_to_all x0 -> x1, waiting for transfers between devices: none -> 37.2 us  [exchange(): return lax.all_to_all(values, 'sweep', 0, 0, axis_index_groups=groups)]
    pallas_call x0 -> x8, Pallas kernels: none -> 28.3 us  [the longest x1 9.14 us: local_maps(): pl.pallas_call(local_maps_kernel, grid_spec=pltpu.PrefetchScalarGridSpec(...]
    another operation x34 -> x0, local copies, waits for them, and re-layouts: 28.3 us -> none
    gather x7 -> x0, local copies, waits for them, and re-layouts: 21.9 us -> none  [to_sweep(): return jnp.take(flattened, slot_order, axis=0).reshape(values.shape)]
    dot_general x13 -> x0, matrix products: 19 us -> none  [the longest x8 13.2 us: apply_blocks(): jnp.einsum('pij,pjr->pir', blocks.astype(jnp.float32), vectors, precision...]
    all_to_all x0 -> x1, blocking collectives: none -> 12.8 us  [exchange(): return lax.all_to_all(values, 'sweep', 0, 0, axis_index_groups=groups)]
  transfers between devices with their start and end apart: 36 -> 8, of which waited for: 36 -> 7; matrix products, arithmetic and copies ran while one was open for 1% -> 0% of each run, Pallas kernels for 0% -> 0%
where the time goes in v1:
time: 143 us; the launch traced here: 142 us
  waiting for transfers between devices  67.7 us (47%)
  Pallas kernels  28.3 us (20%)
  starting transfers between devices  23.2 us (16%)
  blocking collectives  12.8 us (9%)
  local copies, waits for them, and re-layouts  8.94 us (6%)
    all_to_all x1, waiting for transfers between devices, exchange(): return lax.all_to_all(values, 'sweep', 0, 0, axis_index_groups=groups)  37.2 us
    ppermute x4, waiting for transfers between devices, swap(): return lax.ppermute(values, 'sweep', pairs)  22.8 us
    ppermute x4, starting transfers between devices, swap(): return lax.ppermute(values, 'sweep', pairs)  13.5 us
    all_to_all x1, blocking collectives, exchange(): return lax.all_to_all(values, 'sweep', 0, 0, axis_index_groups=groups)  12.8 us
    pallas_call x1, Pallas kernels, local_maps(): pl.pallas_call(local_maps_kernel, grid_spec=pltpu.PrefetchScalarGridSpec(...  9.14 us
    pallas_call x1, Pallas kernels, jacobian(): pl.pallas_call(jacobian_kernel, grid_spec=pltpu.PrefetchScalarGridSpec(nu...  9.03 us
    unnamed x28, local copies, waits for them, and re-layouts  8.18 us
    pallas_call x5, Pallas kernels, whole_call(): pl.pallas_call(kernel, in_specs=specs, out_specs=[pl.BlockSpec(memory_spa...  5.78 us
  transfers between devices with their start and end apart: 8, of which 7 were waited for; matrix products, arithmetic and copies ran while one was open for 0% of the time, Pallas kernels for 0%

profile of v1, /device:TPU:8, one launch (start us, length us, event | category | flops | bytes accessed | tf_op | source)
XLA Modules:
  0.0 141.7 jit_solution(12209841324824070086)
XLA Ops:
  1.4 1.1 copy-done.1
  2.5 9.1 %local_maps.1 = (bf16[4,3040,128]{2,1,0:T(8,128)(2,1)}, bf16[4,320,320]{2,1,0:T(8,128)(2,1)S(1)}, bf16[4,320,320]{2,1,0:T(8,128)(2,1)S(1)}, bf16[4,320,320]{2,1,...) custom-call(s32[8]{0:T(128)S(1)} %reshape.39.slots, ...), custom_call_target="tpu_custom_call" | custom-call | tf_op jit(solution)/shard_map/local_maps/pallas_call | solution.py:83
  12.6 1.0 copy-done.5
  13.5 1.0 copy-done.7
  14.5 1.0 copy-done.9
  17.1 4.9 %all-to-all-start = ((bf16[4,3040,128]{2,1,0:T(8,128)(2,1)}), bf16[4,3040,128]{2,1,0:T(8,128)(2,1)S(1)}, u32[]{:S(2)}, u32[]{:S(2)}) async-start(bf16[4,3040,128]{2,1,0:T(8,128)(2,1)} %get-tuple-element.24), calls=%async_computation | async-start | bytes 6225920 | tf_op jit(solution)/shard_map/all_to_all | solution.py:326
  22.1 37.2 %all-to-all-done.maps = bf16[4,3040,128]{2,1,0:T(8,128)(2,1)S(1)} async-done(((bf16[4,3040,128]{2,1,0:T(8,128)(2,1)}), bf16[4,3040,128]{2,1,0:T(8,128)(2,1)S(1)}, u32[]{:S(2)}, u32[]{:S(2)}) %all-to-all-start) | async-done | bytes 3112992 | tf_op jit(solution)/shard_map/all_to_all | solution.py:326
  59.3 3.3 %group_map.1 = (bf16[320,320]{1,0:T(8,128)(2,1)S(1)}, bf16[320,320]{1,0:T(8,128)(2,1)S(1)}, bf16[320,320]{1,0:T(8,128)(2,1)S(1)}, f32[320,128]{1,0:T(8,128)S(1)}...) custom-call(s32[1]{0:T(128)} %bitcast.7.group, bf16[4,3040,128]{2,1,0:T(8,128)(2,1)S(1)} %all-to-all-done.maps), custom_call_target="tpu_custom_call" | custom-call | tf_op jit(solution)/shard_map/group_map/pallas_call | solution.py:200
  62.6 3.4 %collective-permute-start = (bf16[1120,128]{1,0:T(8,128)(2,1)S(1)}, bf16[1120,128]{1,0:T(8,128)(2,1)S(1)}, u32[]{:S(2)}, u32[]{:S(2)}) collective-permute-start(bf16[1120,128]{1,0:T(8,128)(2,1)S(1)} %get-tuple-element.25), channel_id=1, source_target_pairs={{0,64},{16,80},{32,96},{48,112},{64,0},{80,16},{96,32},{112,48},{1... | collective-permute-start | bytes 860168 | tf_op jit(solution)/shard_map/ppermute | solution.py:330
  66.0 12.2 %collective-permute-done.incoming.far = bf16[1120,128]{1,0:T(8,128)(2,1)S(1)} collective-permute-done((bf16[1120,128]{1,0:T(8,128)(2,1)S(1)}, bf16[1120,128]{1,0:T(8,128)(2,1)S(1)}, u32[]{:S(2)}, u32[]{:S(2)}) %collective-permute-start) | collective-permute-done | bytes 286752 | tf_op jit(solution)/shard_map/ppermute | solution.py:330
  78.4 2.9 %collective-permute-start.1 = (bf16[320,128]{1,0:T(8,128)(2,1)S(1)}, bf16[320,128]{1,0:T(8,128)(2,1)S(1)}, u32[]{:S(2)}, u32[]{:S(2)}) collective-permute-start(bf16[320,128]{1,0:T(8,128)(2,1)S(1)} %forward_one.1), channel_id=1, source_target_pairs={{0,192},{16,208},{32,224},{48,240},{64,128},{80,144},{96,160},{112... | collective-permute-start | bytes 245768 | tf_op jit(solution)/shard_map/ppermute | solution.py:330
  81.3 3.8 %collective-permute-done.1.incoming.hop2 = bf16[320,128]{1,0:T(8,128)(2,1)S(1)} collective-permute-done((bf16[320,128]{1,0:T(8,128)(2,1)S(1)}, bf16[320,128]{1,0:T(8,128)(2,1)S(1)}, u32[]{:S(2)}, u32[]{:S(2)}) %collective-permute-start.1) | collective-permute-done | bytes 81952 | tf_op jit(solution)/shard_map/ppermute | solution.py:330
  85.8 2.8 %collective-permute-start.2 = (bf16[320,128]{1,0:T(8,128)(2,1)S(1)}, bf16[320,128]{1,0:T(8,128)(2,1)S(1)}, u32[]{:S(2)}, u32[]{:S(2)}) collective-permute-start(bf16[320,128]{1,0:T(8,128)(2,1)S(1)} %get-tuple-element.31), channel_id=1, source_target_pairs={{0,192},{16,208},{32,224},{48,240},{64,128},{80,144},{96,160},{112... | collective-permute-start | bytes 245768 | tf_op jit(solution)/shard_map/ppermute | solution.py:330
  88.6 3.8 %collective-permute-done.2.incoming.hop3 = bf16[320,128]{1,0:T(8,128)(2,1)S(1)} collective-permute-done((bf16[320,128]{1,0:T(8,128)(2,1)S(1)}, bf16[320,128]{1,0:T(8,128)(2,1)S(1)}, u32[]{:S(2)}, u32[]{:S(2)}) %collective-permute-start.2) | collective-permute-done | bytes 81952 | tf_op jit(solution)/shard_map/ppermute | solution.py:330
  92.7 4.4 %collective-permute-start.3 = (bf16[320,128]{1,0:T(8,128)(2,1)S(1)}, bf16[320,128]{1,0:T(8,128)(2,1)S(1)}, u32[]{:S(2)}, u32[]{:S(2)}) collective-permute-start(bf16[320,128]{1,0:T(8,128)(2,1)S(1)} %backward_one.1), channel_id=1, source_target_pairs={{0,64},{16,80},{32,96},{48,112},{64,0},{80,16},{96,32},{112,48},{1... | collective-permute-start | bytes 245768 | tf_op jit(solution)/shard_map/ppermute | solution.py:330
  97.1 2.9 %collective-permute-done.3.hop4 = bf16[320,128]{1,0:T(8,128)(2,1)S(1)} collective-permute-done((bf16[320,128]{1,0:T(8,128)(2,1)S(1)}, bf16[320,128]{1,0:T(8,128)(2,1)S(1)}, u32[]{:S(2)}, u32[]{:S(2)}) %collective-permute-start.3) | collective-permute-done | bytes 81952 | tf_op jit(solution)/shard_map/ppermute | solution.py:330
  100.1 1.3 interfaces.1
  101.4 12.8 %all_to_all.10.ends = bf16[4,640,128]{2,1,0:T(8,128)(2,1)S(1)} all-to-all(bf16[4,640,128]{2,1,0:T(8,128)(2,1)S(1)} %interfaces.1), channel_id=1, replica_groups={{0,16,32,48},{64,80,96,112},{128,144,160,176},{192,208,224,240},{1,17,3..., dimensions={0} | all-to-all | bytes 1310720 | tf_op jit(solution)/shard_map/all_to_all | solution.py:326
  114.2 4.3 %finish.1 = (bf16[4,320,128]{2,1,0:T(8,128)(2,1)S(1)}, bf16[4,320,128]{2,1,0:T(8,128)(2,1)S(1)}, bf16[2,320,128]{2,1,0:T(8,128)(2,1)}, bf16[2,320,128]{2,1,0:T(8,128)(2,1)}) custom-call(bf16[4,640,128]{2,1,0:T(8,128)(2,1)S(1)} %all_to_all.10.ends, bf16[4,320,320]{2,1,0:T(8,128)(2,1)S(1)} %copy-done.4, bf16[4,320,320]{2,1,0:T(8,128)(2,1)S(1)} %copy-done.6, ...), custom_call_target="tpu_custom_call" | custom-call | tf_op jit(solution)/shard_map/finish/pallas_call | solution.py:239
  119.5 3.9 %collective-permute-start.6 = (bf16[2,320,128]{2,1,0:T(8,128)(2,1)}, bf16[2,320,128]{2,1,0:T(8,128)(2,1)}, u32[]{:S(2)}, u32[]{:S(2)}) collective-permute-start(bf16[2,320,128]{2,1,0:T(8,128)(2,1)} %get-tuple-element.43), channel_id=1, source_target_pairs={{1,0},{2,1},{3,2},{4,3},{5,4},{6,5},{7,6},{8,7},{9,8},{10,9},{11,1... | collective-permute-start | bytes 491528 | tf_op jit(solution)/shard_map/ppermute | solution.py:363
  123.4 3.2 %collective-permute-done.5.low = bf16[2,320,128]{2,1,0:T(8,128)(2,1)S(1)} collective-permute-done((bf16[2,320,128]{2,1,0:T(8,128)(2,1)}, bf16[2,320,128]{2,1,0:T(8,128)(2,1)S(1)}, u32[]{:S(2)}, u32[]{:S(2)}) %collective-permute-start.5) | collective-permute-done | bytes 163872 | tf_op jit(solution)/shard_map/ppermute | solution.py:362
  126.6 4.5 %collective-permute-done.4.below = bf16[4,320,128]{2,1,0:T(8,128)(2,1)} collective-permute-done((bf16[4,320,128]{2,1,0:T(8,128)(2,1)S(1)}, bf16[4,320,128]{2,1,0:T(8,128)(2,1)}, u32[]{:S(2)}, u32[]{:S(2)}) %collective-permute-start.4) | collective-permute-done | bytes 327712 | tf_op jit(solution)/shard_map/ppermute | solution.py:361
  131.1 1.5 %copy-done.2 = bf16[2,4,320,320]{3,2,1,0:T(8,128)(2,1)S(1)} copy-done((bf16[2,4,320,320]{3,2,1,0:T(8,128)(2,1)S(1)}, bf16[2,4,320,320]{3,2,1,0:T(8,128)(2,1)}, u32[]{:S(2)}) %copy-start.2) | copy-done | bytes 1638424
  132.7 9.0 %jacobian.1 = (bf16[8,320,128]{2,1,0:T(8,128)(2,1)}, bf16[8,320,128]{2,1,0:T(8,128)(2,1)}) custom-call(s32[8]{0:T(128)S(1)} %reshape.39.slots, s32[3]{0:T(128)S(1)} %pad_add_fusion.place, bf16[8,320,320]{2,1,0:T(8,128)(2,1)S(1)} %bitcast.17, bf16[8,320,320]{2,1,0:T(8,128)(2,1)S(1)} %bitcast.14, bf16[8,320,320]{2,1,0:T(8,128)(2,1)} %bitcast.20, ...), custom_call_target="tpu_custom_call" | custom-call | tf_op jit(solution)/shard_map/jacobian/pallas_call | solution.py:296
  (31 shorter events, 5.5 us)
Async XLA Ops:
  1.4 1.1 copy-start.1
  11.6 0.9 copy-start.3
  12.6 1.0 copy-start.5
  13.5 1.0 copy-start.7
  14.5 1.0 copy-start.9
  15.5 0.8 copy-start.10
  16.3 0.8 copy-start.12
  17.1 42.1 %all-to-all-start = ((bf16[4,3040,128]{2,1,0:T(8,128)(2,1)}), bf16[4,3040,128]{2,1,0:T(8,128)(2,1)S(1)}, u32[]{:S(2)}, u32[]{:S(2)}) async-start(bf16[4,3040,128]{2,1,0:T(8,128)(2,1)} %get-tuple-element.24), calls=%async_computation | async-start | bytes 6225920 | tf_op jit(solution)/shard_map/all_to_all | solution.py:326
  62.6 15.6 %collective-permute-start = (bf16[1120,128]{1,0:T(8,128)(2,1)S(1)}, bf16[1120,128]{1,0:T(8,128)(2,1)S(1)}, u32[]{:S(2)}, u32[]{:S(2)}) collective-permute-start(bf16[1120,128]{1,0:T(8,128)(2,1)S(1)} %get-tuple-element.25), channel_id=1, source_target_pairs={{0,64},{16,80},{32,96},{48,112},{64,0},{80,16},{96,32},{112,48},{1... | collective-permute-start | bytes 860168 | tf_op jit(solution)/shard_map/ppermute | solution.py:330
  78.4 6.7 %collective-permute-start.1 = (bf16[320,128]{1,0:T(8,128)(2,1)S(1)}, bf16[320,128]{1,0:T(8,128)(2,1)S(1)}, u32[]{:S(2)}, u32[]{:S(2)}) collective-permute-start(bf16[320,128]{1,0:T(8,128)(2,1)S(1)} %forward_one.1), channel_id=1, source_target_pairs={{0,192},{16,208},{32,224},{48,240},{64,128},{80,144},{96,160},{112... | collective-permute-start | bytes 245768 | tf_op jit(solution)/shard_map/ppermute | solution.py:330
  85.8 6.7 %collective-permute-start.2 = (bf16[320,128]{1,0:T(8,128)(2,1)S(1)}, bf16[320,128]{1,0:T(8,128)(2,1)S(1)}, u32[]{:S(2)}, u32[]{:S(2)}) collective-permute-start(bf16[320,128]{1,0:T(8,128)(2,1)S(1)} %get-tuple-element.31), channel_id=1, source_target_pairs={{0,192},{16,208},{32,224},{48,240},{64,128},{80,144},{96,160},{112... | collective-permute-start | bytes 245768 | tf_op jit(solution)/shard_map/ppermute | solution.py:330
  92.7 7.4 %collective-permute-start.3 = (bf16[320,128]{1,0:T(8,128)(2,1)S(1)}, bf16[320,128]{1,0:T(8,128)(2,1)S(1)}, u32[]{:S(2)}, u32[]{:S(2)}) collective-permute-start(bf16[320,128]{1,0:T(8,128)(2,1)S(1)} %backward_one.1), channel_id=1, source_target_pairs={{0,64},{16,80},{32,96},{48,112},{64,0},{80,16},{96,32},{112,48},{1... | collective-permute-start | bytes 245768 | tf_op jit(solution)/shard_map/ppermute | solution.py:330
  100.1 14.1 %copy-start.4 = (bf16[4,320,320]{2,1,0:T(8,128)(2,1)S(1)}, bf16[4,320,320]{2,1,0:T(8,128)(2,1)}, u32[]{:S(2)}) copy-start(bf16[4,320,320]{2,1,0:T(8,128)(2,1)} %copy-done.3) | copy-start | bytes 2457604
  100.1 14.1 %copy-start.6 = (bf16[4,320,320]{2,1,0:T(8,128)(2,1)S(1)}, bf16[4,320,320]{2,1,0:T(8,128)(2,1)}, u32[]{:S(2)}) copy-start(bf16[4,320,320]{2,1,0:T(8,128)(2,1)} %copy-done.5) | copy-start | bytes 2457604
  100.1 14.1 %copy-start.8 = (bf16[4,320,320]{2,1,0:T(8,128)(2,1)S(1)}, bf16[4,320,320]{2,1,0:T(8,128)(2,1)}, u32[]{:S(2)}) copy-start(bf16[4,320,320]{2,1,0:T(8,128)(2,1)} %copy-done.7) | copy-start | bytes 2457604
  100.1 14.1 %copy-start.11 = (f32[4,320,128]{2,1,0:T(8,128)S(1)}, f32[4,320,128]{2,1,0:T(8,128)}, u32[]{:S(2)}) copy-start(f32[4,320,128]{2,1,0:T(8,128)} %copy-done.10) | copy-start | bytes 1966084
  100.1 14.1 %copy-start.13 = (f32[4,320,128]{2,1,0:T(8,128)S(1)}, f32[4,320,128]{2,1,0:T(8,128)}, u32[]{:S(2)}) copy-start(f32[4,320,128]{2,1,0:T(8,128)} %copy-done.12) | copy-start | bytes 1966084
  114.2 16.9 %copy-start = (bf16[2,4,320,320]{3,2,1,0:T(8,128)(2,1)S(1)}, bf16[2,4,320,320]{3,2,1,0:T(8,128)(2,1)}, u32[]{:S(2)}) copy-start(bf16[2,4,320,320]{3,2,1,0:T(8,128)(2,1)} %param.11) | copy-start | bytes 4915204
  118.6 12.5 %collective-permute-start.4 = (bf16[4,320,128]{2,1,0:T(8,128)(2,1)S(1)}, bf16[4,320,128]{2,1,0:T(8,128)(2,1)}, u32[]{:S(2)}, u32[]{:S(2)}) collective-permute-start(bf16[4,320,128]{2,1,0:T(8,128)(2,1)S(1)} %get-tuple-element.41.p1), channel_id=1, source_target_pairs={{0,16},{16,32},{32,48},{48,64},{64,80},{80,96},{96,112},{112,128},... | collective-permute-start | bytes 983048 | tf_op jit(solution)/shard_map/ppermute | solution.py:361
  119.5 7.2 %collective-permute-start.5 = (bf16[2,320,128]{2,1,0:T(8,128)(2,1)}, bf16[2,320,128]{2,1,0:T(8,128)(2,1)S(1)}, u32[]{:S(2)}, u32[]{:S(2)}) collective-permute-start(bf16[2,320,128]{2,1,0:T(8,128)(2,1)} %get-tuple-element.42), channel_id=1, source_target_pairs={{0,1},{1,2},{2,3},{3,4},{4,5},{5,6},{6,7},{7,8},{8,9},{9,10},{10,1... | collective-permute-start | bytes 491528 | tf_op jit(solution)/shard_map/ppermute | solution.py:362
  119.5 7.2 %collective-permute-start.6 = (bf16[2,320,128]{2,1,0:T(8,128)(2,1)}, bf16[2,320,128]{2,1,0:T(8,128)(2,1)}, u32[]{:S(2)}, u32[]{:S(2)}) collective-permute-start(bf16[2,320,128]{2,1,0:T(8,128)(2,1)} %get-tuple-element.43), channel_id=1, source_target_pairs={{1,0},{2,1},{3,2},{4,3},{5,4},{6,5},{7,6},{8,7},{9,8},{10,9},{11,1... | collective-permute-start | bytes 491528 | tf_op jit(solution)/shard_map/ppermute | solution.py:363
  131.1 1.5 %copy-start.2 = (bf16[2,4,320,320]{3,2,1,0:T(8,128)(2,1)S(1)}, bf16[2,4,320,320]{3,2,1,0:T(8,128)(2,1)}, u32[]{:S(2)}) copy-start(bf16[2,4,320,320]{3,2,1,0:T(8,128)(2,1)} %param.10) | copy-start | bytes 4915204

commit v2 on v1

v2 whole, which is shorter than its diff:
```python
import jax
import jax.numpy as jnp
from jax import lax
from jax.experimental import pallas as pl
from jax.experimental.pallas import tpu as pltpu
from jax.sharding import PartitionSpec as P

BF = jnp.bfloat16
F32 = jnp.float32
GROUP = 4
VMEM_LIMIT = 48 << 20


def mm(a, b):
    return jnp.dot(a, b, preferred_element_type=F32)


def mm_fine(a, x):
    width = x.shape[1]
    top = x.astype(BF)
    rest = (x - top.astype(F32)).astype(BF)
    both = mm(a, jnp.concatenate([top, rest], axis=1))
    return both[:, :width] + both[:, width:]


def packed_rows(n):
    return 2 * n + n // 2


def pack(ref, base, mat):
    n = mat.shape[0]
    half = n // 2
    ref[base : base + n, :] = mat[:, 0:128]
    ref[base + n : base + 2 * n, :] = mat[:, 128:256]
    ref[base + 2 * n : base + 2 * n + half, 0:64] = mat[0:half, 256:320]
    ref[base + 2 * n : base + 2 * n + half, 64:128] = mat[half:n, 256:320]


def unpack(ref, base, n):
    half = n // 2
    tail = ref[base + 2 * n : base + 2 * n + half, :]
    last = jnp.concatenate([tail[:, 0:64], tail[:, 64:128]], axis=0)
    return jnp.concatenate(
        [ref[base : base + n, :], ref[base + n : base + 2 * n, :], last], axis=1
    )


def front_maps_kernel(slots, d0, d1, l0, l1, r0, r1, maps, c_out):
    n = d0.shape[0]
    rows = packed_rows(n)
    e0 = mm(d0[...], l0[...]).astype(BF)
    e1 = mm(d1[...], l1[...]).astype(BF)
    y0 = mm(d0[...], r0[...])
    y1 = mm(d1[...], r1[...])
    c = y1 - mm_fine(e1, y0)
    pack(maps, 0, mm(e1, e0).astype(BF))
    maps[rows : rows + n, :] = c.astype(BF)
    c_out[...] = c


def back_maps_kernel(slots, d0, d1, l0, u0, u1, r0, front, c, maps):
    n = d0.shape[0]
    rows = packed_rows(n)
    e0 = mm(d0[...], l0[...])
    h0 = mm(d0[...], u0[...]).astype(BF)
    h1 = mm(d1[...], u1[...]).astype(BF)
    y0 = mm(d0[...], r0[...])
    pack(maps, 0, mm(h0, h1).astype(BF))
    g = -(e0 + mm(h0, unpack(front, 0, n)))
    pack(maps, rows, g.astype(BF))
    maps[2 * rows : 2 * rows + n, :] = (y0 - mm_fine(h0, c[...])).astype(BF)


def stored(slab, height, width):
    return pl.BlockSpec((None, height, width), lambda p, sl: (sl[slab, p], 0, 0))


def in_order(height, width):
    return pl.BlockSpec((None, height, width), lambda p, sl: (p, 0, 0))


def pencil_call(kernel, in_specs, out_specs, out_shape, slots, *operands, name):
    return pl.pallas_call(
        kernel,
        grid_spec=pltpu.PrefetchScalarGridSpec(
            num_scalar_prefetch=1, grid=(GROUP,), in_specs=in_specs, out_specs=out_specs
        ),
        out_shape=out_shape,
        compiler_params=pltpu.CompilerParams(vmem_limit_bytes=VMEM_LIMIT),
        name=name,
    )(slots, *operands)


def front_maps(slots, diag_inv, lower, source):
    n, cols = source.shape[1:]
    rows = packed_rows(n) + n
    shape = jax.ShapeDtypeStruct
    return pencil_call(
        front_maps_kernel,
        [stored(s, n, n) for s in (0, 1, 0, 1)] + [stored(s, n, cols) for s in (0, 1)],
        [in_order(rows, cols), in_order(n, cols)],
        [shape((GROUP, rows, cols), BF), shape((GROUP, n, cols), F32)],
        slots, diag_inv, diag_inv, lower, lower, source, source, name="front_maps",
    )


def back_maps(slots, diag_inv, lower, upper, source, front, c):
    n, cols = source.shape[1:]
    rows = 2 * packed_rows(n) + n
    return pencil_call(
        back_maps_kernel,
        [stored(s, n, n) for s in (0, 1, 0, 0, 1)]
        + [stored(0, n, cols), in_order(front.shape[1], cols), in_order(n, cols)],
        in_order(rows, cols),
        jax.ShapeDtypeStruct((GROUP, rows, cols), BF),
        slots, diag_inv, diag_inv, lower, upper, upper, source, front, c, name="back_maps",
    )


def forward_through(maps, front, n):
    rows = packed_rows(n)
    fronts = []
    for j in range(GROUP):
        fronts.append(front)
        shift = maps[j, rows : rows + n, :].astype(F32)
        front = mm_fine(unpack(maps.at[j], 0, n), front) + shift
    return fronts, front


def backward_through(maps, shifts, back, n):
    backs = [None] * GROUP
    for j in reversed(range(GROUP)):
        backs[j] = back
        back = mm_fine(unpack(maps.at[j], 0, n), back) + shifts[j]
    return backs, back


def forward_first_kernel(maps, send):
    n = send.shape[0]
    rows = packed_rows(n)
    front = maps[0, rows : rows + n, :].astype(F32)
    for j in range(1, GROUP):
        shift = maps[j, rows : rows + n, :].astype(F32)
        front = mm_fine(unpack(maps.at[j], 0, n), front) + shift
    send[...] = front.astype(BF)


def forward_kernel(maps, incoming, send):
    n = send.shape[0]
    _, front = forward_through(maps, incoming[...].astype(F32), n)
    send[...] = front.astype(BF)


def turn_kernel(group, front_maps, back_maps, hop1, hop2, hop3, send, fronts_out, shifts_out):
    n = send.shape[0]
    rows = packed_rows(n)
    which = group[0]
    zero = jnp.zeros_like(hop1[...])
    front = jnp.where(
        which == 0, zero,
        jnp.where(which == 1, hop1[...], jnp.where(which == 2, hop2[...], hop3[...])),
    )
    fronts, _ = forward_through(front_maps, front.astype(F32), n)
    shifts = []
    for j in range(GROUP):
        shift = back_maps[j, 2 * rows : 2 * rows + n, :].astype(F32)
        shifts.append(mm_fine(unpack(back_maps.at[j], rows, n), fronts[j]) + shift)
        shifts_out[j] = shifts[j]
        fronts_out[j] = fronts[j].astype(BF)
    back = shifts[GROUP - 1]
    for j in reversed(range(GROUP - 1)):
        back = mm_fine(unpack(back_maps.at[j], 0, n), back) + shifts[j]
    send[...] = back.astype(BF)


def backward_kernel(maps, shifts, incoming, send):
    n = send.shape[0]
    _, back = backward_through(maps, shifts, incoming[...].astype(F32), n)
    send[...] = back.astype(BF)


def interfaces_kernel(group, maps, shifts, fronts, hop4, hop5, hop6, out):
    n = hop4.shape[0]
    which = group[0]
    zero = jnp.zeros_like(hop4[...])
    back = jnp.where(
        which == 0, hop6[...],
        jnp.where(which == 1, hop5[...], jnp.where(which == 2, hop4[...], zero)),
    )
    backs, _ = backward_through(maps, shifts, back.astype(F32), n)
    for j in range(GROUP):
        out[j, 0:n, :] = fronts[j]
        out[j, n : 2 * n, :] = backs[j].astype(BF)


def whole_call(kernel, outs, scalars, *operands, name):
    specs = [pl.BlockSpec(memory_space=pltpu.SMEM)] * len(scalars)
    specs += [pl.BlockSpec(memory_space=pltpu.VMEM)] * len(operands)
    return pl.pallas_call(
        kernel,
        in_specs=specs,
        out_specs=[pl.BlockSpec(memory_space=pltpu.VMEM)] * len(outs),
        out_shape=[jax.ShapeDtypeStruct(s, d) for s, d in outs],
        compiler_params=pltpu.CompilerParams(vmem_limit_bytes=VMEM_LIMIT),
        name=name,
    )(*scalars, *operands)


def finish_kernel(slots, ends, d0, d1, l0, l1, u0, u1, r0, r1, p0, p1, first, last):
    n = d0.shape[0]
    pencil = pl.program_id(0)
    front = ends[0:n, :]
    back = ends[n : 2 * n, :]
    f0 = mm_fine(d0[...], r0[...].astype(F32) - mm(l0[...], front))
    f1 = mm_fine(d1[...], r1[...].astype(F32) - mm_fine(l1[...], f0))
    x1 = f1 - mm_fine(d1[...], mm(u1[...], back))
    x0 = f0 - mm_fine(d0[...], mm_fine(u0[...], x1))
    b0 = x0.astype(BF)
    b1 = x1.astype(BF)
    p0[...] = b0
    p1[...] = b1

    @pl.when(pencil == 0)
    def _():
        first[0] = b0
        first[1] = b1

    @pl.when(pencil == GROUP - 1)
    def _():
        last[0] = b0
        last[1] = b1


def finish(slots, ends, diag_inv, lower, upper, source):
    n, cols = source.shape[1:]
    kept = pl.BlockSpec((2, n, cols), lambda p, sl: (0, 0, 0))
    shape = jax.ShapeDtypeStruct
    return pencil_call(
        finish_kernel,
        [in_order(2 * n, cols)]
        + [stored(s, n, n) for s in (0, 1, 0, 1, 0, 1)]
        + [stored(s, n, cols) for s in (0, 1)],
        [in_order(n, cols), in_order(n, cols), kept, kept],
        [
            shape((GROUP, n, cols), BF), shape((GROUP, n, cols), BF),
            shape((2, n, cols), BF), shape((2, n, cols), BF),
        ],
        slots, ends, diag_inv, diag_inv, lower, lower, upper, upper, source, source,
        name="finish",
    )


def inner_jacobian_kernel(
    slots, diag, lower, upper, minus, plus, p0, p1, ends, precond, partial, vals
):
    n = diag.shape[0]
    element = pl.program_id(0)
    slab = element // GROUP
    pencil = element % GROUP

    @pl.when(element == 0)
    def _():
        zero = jnp.zeros((n, p0.shape[2]), BF)
        for p in range(GROUP):
            vals[0, p + 1] = zero
            vals[1, p + 1] = p0[p]
            vals[2, p + 1] = p1[p]
            vals[3, p + 1] = ends[p, n : 2 * n, :]
        for s in range(2):
            vals[s + 1, 0] = zero
            vals[s + 1, GROUP + 1] = zero

    own = vals[slab + 1, pencil + 1]
    total = mm(diag[...], own)
    total = total + mm(lower[...], vals[slab, pencil + 1])
    total = total + mm(upper[...], vals[slab + 2, pencil + 1])
    total = total + mm(minus[...], vals[slab + 1, pencil])
    total = total + mm(plus[...], vals[slab + 1, pencil + 2])
    precond[...] = own
    partial[...] = total


def inner_jacobian(slots, blocks, p0, p1, ends):
    n, cols = p0.shape[1:]
    block = pl.BlockSpec((None, n, n), lambda e, sl: (sl[e // GROUP, e % GROUP], 0, 0))
    out = pl.BlockSpec((None, n, cols), lambda e, sl: (sl[e // GROUP, e % GROUP], 0, 0))
    seq = pl.BlockSpec((None, n, cols), lambda e, sl: (e, 0, 0))

    def whole(array):
        return pl.BlockSpec(array.shape, lambda e, sl: (0, 0, 0))

    vectors = (p0, p1, ends)
    shape = (2 * GROUP, n, cols)
    return pl.pallas_call(
        inner_jacobian_kernel,
        grid_spec=pltpu.PrefetchScalarGridSpec(
            num_scalar_prefetch=1,
            grid=(2 * GROUP,),
            in_specs=[block] * 5 + [whole(v) for v in vectors],
            out_specs=[out, seq],
            scratch_shapes=[pltpu.VMEM((4, GROUP + 2, n, cols), BF)],
        ),
        out_shape=[jax.ShapeDtypeStruct(shape, BF), jax.ShapeDtypeStruct(shape, F32)],
        compiler_params=pltpu.CompilerParams(vmem_limit_bytes=VMEM_LIMIT),
        name="inner_jacobian",
    )(slots, *blocks, *vectors)


def edge_jacobian_kernel(slots, place, *refs):
    lowers, minuses, pluses = refs[0:4], refs[4:6], refs[6:8]
    partial, below, low, high, jac = refs[8:]
    left = jnp.where(place[1] == 0, 0.0, 1.0).astype(F32)
    right = jnp.where(place[1] == place[2] - 1, 0.0, 1.0).astype(F32)
    start = jnp.where(place[0] == 0, 0.0, 1.0).astype(F32)
    for s in range(2):
        for p in range(GROUP):
            total = partial[s * GROUP + p]
            if s == 0:
                total = total + start * mm(lowers[p][...], below[p])
            if p == 0:
                total = total + left * mm(minuses[s][...], low[s])
            if p == GROUP - 1:
                total = total + right * mm(pluses[s][...], high[s])
            jac[slots[s, p]] = total.astype(BF)


def edge_jacobian(slots, place, lower, minus, plus, partial, below, low, high):
    n, cols = below.shape[1:]

    def block(s, p):
        return pl.BlockSpec((None, n, n), lambda i, sl, pc: (sl[s, p], 0, 0))

    def whole(shape):
        return pl.BlockSpec(shape, lambda i, sl, pc: (0, 0, 0))

    vectors = (partial, below, low, high)
    return pl.pallas_call(
        edge_jacobian_kernel,
        grid_spec=pltpu.PrefetchScalarGridSpec(
            num_scalar_prefetch=2,
            grid=(1,),
            in_specs=[block(0, p) for p in range(GROUP)]
            + [block(s, 0) for s in range(2)]
            + [block(s, GROUP - 1) for s in range(2)]
            + [whole(v.shape) for v in vectors],
            out_specs=whole((2 * GROUP, n, cols)),
        ),
        out_shape=jax.ShapeDtypeStruct((2 * GROUP, n, cols), BF),
        compiler_params=pltpu.CompilerParams(vmem_limit_bytes=VMEM_LIMIT),
        name="edge_jacobian",
    )(slots, place, *([lower] * GROUP), minus, minus, plus, plus, *vectors)


def local(right_side, diag_inv, diag_blk, lower_blk, upper_blk, cross_minus, cross_plus, elem_slot):
    n, cols = right_side.shape[2:]
    source, inverse, diagonal, lower, upper, minus, plus = (
        values.reshape((-1,) + values.shape[2:])
        for values in (
            right_side, diag_inv, diag_blk, lower_blk, upper_blk, cross_minus, cross_plus
        )
    )
    count = lax.axis_size("sweep")
    across = lax.axis_size("cross")
    sweep_at = lax.axis_index("sweep")
    group = (sweep_at // GROUP).astype(jnp.int32).reshape(1)
    place = jnp.stack([sweep_at, lax.axis_index("cross"), jnp.int32(across)]).astype(jnp.int32)
    groups = [list(range(g, g + GROUP)) for g in range(0, count, GROUP)]

    def exchange(values):
        return lax.all_to_all(values, "sweep", 0, 0, axis_index_groups=groups)

    def swap(values, order):
        pairs = [(g * GROUP + k, order[g] * GROUP + k) for g in range(GROUP) for k in range(GROUP)]
        return lax.ppermute(values, "sweep", pairs)

    outer, inner = (1, 0, 3, 2), (3, 2, 1, 0)
    vec = ((n, cols), BF)
    vecs, vecs32 = ((GROUP, n, cols), BF), ((GROUP, n, cols), F32)

    front, c = front_maps(elem_slot, inverse, lower, source)
    fronts = exchange(front)
    back = back_maps(elem_slot, inverse, lower, upper, source, front, c)
    backs = exchange(back)
    (send,) = whole_call(forward_first_kernel, [vec], [], fronts, name="forward_first")
    hop1 = swap(send, outer)
    (send,) = whole_call(forward_kernel, [vec], [], fronts, hop1, name="forward_second")
    hop2 = swap(send, inner)
    (send,) = whole_call(forward_kernel, [vec], [], fronts, hop2, name="forward_third")
    hop3 = swap(send, outer)
    send, entering, shifts = whole_call(
        turn_kernel, [vec, vecs, vecs32], [group], fronts, backs, hop1, hop2, hop3, name="turn"
    )
    hop4 = swap(send, outer)
    (send,) = whole_call(backward_kernel, [vec], [], backs, shifts, hop4, name="backward_third")
    hop5 = swap(send, inner)
    (send,) = whole_call(backward_kernel, [vec], [], backs, shifts, hop5, name="backward_second")
    hop6 = swap(send, outer)
    (ends,) = whole_call(
        interfaces_kernel, [((GROUP, 2 * n, cols), BF)], [group],
        backs, shifts, entering, hop4, hop5, hop6, name="interfaces",
    )
    ends = exchange(ends)
    p0, p1, first, last = finish(elem_slot, ends, inverse, lower, upper, source)
    low = lax.ppermute(last, "cross", [(i, (i + 1) % across) for i in range(across)])
    high = lax.ppermute(first, "cross", [((i + 1) % across, i) for i in range(across)])
    below = lax.ppermute(p1, "sweep", [(i, (i + 1) % count) for i in range(count)])
    precond, partial = inner_jacobian(elem_slot, (diagonal, lower, upper, minus, plus), p0, p1, ends)
    jac = edge_jacobian(elem_slot, place, lower, minus, plus, partial, below, low, high)
    return precond.reshape(right_side.shape), jac.reshape(right_side.shape)


def solution(mesh):
    blocks = P("sweep", "cross", None, None)
    in_specs = (blocks,) * 7 + (P("sweep", "cross"),)
    return jax.shard_map(
        local, mesh=mesh, in_specs=in_specs, out_specs=(blocks, blocks), check_vma=False
    )
```

time: 143 us -> 144 us (level)
  waiting for transfers between devices: 67.7 us -> 46.1 us
  Pallas kernels: 28.3 us -> 44 us
  starting transfers between devices: 23.2 us -> 29.3 us
  blocking collectives: 12.8 us -> 15.6 us
  local copies, waits for them, and re-layouts: 8.94 us -> 6.53 us
    all_to_all x1 -> x2, waiting for transfers between devices: 37.2 us -> 6.7 us  [exchange(): return lax.all_to_all(values, 'sweep', 0, 0, axis_index_groups=groups)]
    ppermute x4 -> x6, waiting for transfers between devices: 22.8 us -> 39.4 us  [swap(): return lax.ppermute(values, 'sweep', pairs)]
    pallas_call x3 -> x5, Pallas kernels: 22.5 us -> 35.9 us  [the longest x3 23.2 us: pencil_call(): pl.pallas_call(kernel, grid_spec=pltpu.PrefetchScalarGridSpec(num_scalar_...]
    ppermute x1, waiting for transfers between devices: 4.46 us -> 0.01 us  [local(): lax.ppermute(p1, 'sweep', [(i, (i + 1) % count) for i in range(count)])]
    all_to_all x1 -> x2, starting transfers between devices: 4.91 us -> 8.64 us  [exchange(): return lax.all_to_all(values, 'sweep', 0, 0, axis_index_groups=groups)]
    ppermute x1, waiting for transfers between devices: 3.23 us -> 0.01 us  [local(): lax.ppermute(last, 'cross', [(i, (i + 1) % across) for i in range(across)])]
    all_to_all x1, blocking collectives: 12.8 us -> 15.6 us  [exchange(): return lax.all_to_all(values, 'sweep', 0, 0, axis_index_groups=groups)]
    pallas_call x5 -> x7, Pallas kernels: 5.78 us -> 8.18 us  [whole_call(): pl.pallas_call(kernel, in_specs=specs, out_specs=[pl.BlockSpec(memory_spa...]
  transfers between devices with their start and end apart: 8 -> 11, of which waited for: 7 -> 7; matrix products, arithmetic and copies ran while one was open for 0% -> 0% of each run, Pallas kernels for 0% -> 14%
where the time goes in v2:
time: 144 us; the launch traced here: 142 us
  waiting for transfers between devices  46.1 us (32%)
  Pallas kernels  44 us (31%)
  starting transfers between devices  29.3 us (20%)
  blocking collectives  15.6 us (11%)
  local copies, waits for them, and re-layouts  6.53 us (5%)
    ppermute x6, waiting for transfers between devices, swap(): return lax.ppermute(values, 'sweep', pairs)  39.4 us
    pallas_call x3, Pallas kernels, pencil_call(): pl.pallas_call(kernel, grid_spec=pltpu.PrefetchScalarGridSpec(num_scalar_...  23.2 us
    ppermute x6, starting transfers between devices, swap(): return lax.ppermute(values, 'sweep', pairs)  15.9 us
    all_to_all x1, blocking collectives, exchange(): return lax.all_to_all(values, 'sweep', 0, 0, axis_index_groups=groups)  15.6 us
    pallas_call x1, Pallas kernels, inner_jacobian(): pl.pallas_call(inner_jacobian_kernel, grid_spec=pltpu.PrefetchScalarGridS...  9.32 us
    all_to_all x2, starting transfers between devices, exchange(): return lax.all_to_all(values, 'sweep', 0, 0, axis_index_groups=groups)  8.64 us
    pallas_call x7, Pallas kernels, whole_call(): pl.pallas_call(kernel, in_specs=specs, out_specs=[pl.BlockSpec(memory_spa...  8.18 us
    all_to_all x2, waiting for transfers between devices, exchange(): return lax.all_to_all(values, 'sweep', 0, 0, axis_index_groups=groups)  6.7 us
  transfers between devices with their start and end apart: 11, of which 7 were waited for; matrix products, arithmetic and copies ran while one was open for 0% of the time, Pallas kernels for 14%

profile of v2, /device:TPU:8, one launch (start us, length us, event | category | flops | bytes accessed | tf_op | source)
XLA Modules:
  0.0 142.4 jit_solution(12992326217010856245)
XLA Ops:
  0.6 1.5 %copy-done.1 = bf16[2,4,320,320]{3,2,1,0:T(8,128)(2,1)S(1)} copy-done((bf16[2,4,320,320]{3,2,1,0:T(8,128)(2,1)S(1)}, bf16[2,4,320,320]{3,2,1,0:T(8,128)(2,1)}, u32[]{:S(2)}) %copy-start.1) | copy-done | bytes 1638424
  3.9 6.4 %front_maps.1 = (bf16[4,1120,128]{2,1,0:T(8,128)(2,1)}, f32[4,320,128]{2,1,0:T(8,128)S(1)}) custom-call(s32[2,4]{1,0:T(2,128)S(1)} %copy-done.11, bf16[8,320,320]{2,1,0:T(8,128)(2,1)S(1)} %bitcast.24, bf16[8,320,320]{2,1,0:T(8,128)(2,1)S(1)} %bitcast.25, bf16[8,320,320]{2,1,0:T(8,128)(2,1)} %bitcast.12, bf16[8,320,320]{2,1,0:T(8,128)(2,1)} %bitcast.13, ...), custom_call_target="tpu_custom_call" | custom-call | tf_op jit(solution)/shard_map/front_maps/pallas_call | solution.py:83
  11.2 5.0 %all-to-all-start.1 = ((bf16[4,1120,128]{2,1,0:T(8,128)(2,1)}), bf16[4,1120,128]{2,1,0:T(8,128)(2,1)S(1)}, u32[]{:S(2)}, u32[]{:S(2)}) async-start(bf16[4,1120,128]{2,1,0:T(8,128)(2,1)} %get-tuple-element.13.front), calls=%async_computation.1 | async-start | bytes 2293760 | tf_op jit(solution)/shard_map/all_to_all | solution.py:370
  17.4 7.1 %back_maps.1 = bf16[4,1920,128]{2,1,0:T(8,128)(2,1)S(1)} custom-call(s32[2,4]{1,0:T(2,128)S(1)} %copy-done.12, bf16[8,320,320]{2,1,0:T(8,128)(2,1)} %bitcast.22, bf16[8,320,320]{2,1,0:T(8,128)(2,1)} %bitcast.23, bf16[8,320,320]{2,1,0:T(8,128)(2,1)} %bitcast.14, bf16[8,320,320]{2,1,0:T(8,128)(2,1)} %bitcast.37, bf16[8,320,320]{2,1,0:T(8,128)(2,1)} %bitcast.38, ...), custom_call_target="tpu_custom_call" | custom-call | tf_op jit(solution)/shard_map/back_maps/pallas_call | solution.py:83
  24.5 1.3 copy-done.7
  25.7 6.7 %all-to-all-done.1.maps.front_maps = bf16[4,1120,128]{2,1,0:T(8,128)(2,1)S(1)} async-done(((bf16[4,1120,128]{2,1,0:T(8,128)(2,1)}), bf16[4,1120,128]{2,1,0:T(8,128)(2,1)S(1)}, u32[]{:S(2)}, u32[]{:S(2)}) %all-to-all-start.1) | async-done | bytes 1146912 | tf_op jit(solution)/shard_map/all_to_all | solution.py:370
  32.4 3.6 %all-to-all-start = ((bf16[4,1920,128]{2,1,0:T(8,128)(2,1)}), bf16[4,1920,128]{2,1,0:T(8,128)(2,1)S(1)}, u32[]{:S(2)}, u32[]{:S(2)}) async-start(bf16[4,1920,128]{2,1,0:T(8,128)(2,1)} %copy-done.7), calls=%async_computation | async-start | bytes 3932160 | tf_op jit(solution)/shard_map/all_to_all | solution.py:370
  36.8 3.4 %collective-permute-start = (bf16[320,128]{1,0:T(8,128)(2,1)S(1)}, bf16[320,128]{1,0:T(8,128)(2,1)S(1)}, u32[]{:S(2)}, u32[]{:S(2)}) collective-permute-start(bf16[320,128]{1,0:T(8,128)(2,1)S(1)} %forward_first.1), channel_id=1, source_target_pairs={{0,64},{16,80},{32,96},{48,112},{64,0},{80,16},{96,32},{112,48},{1... | collective-permute-start | bytes 245768 | tf_op jit(solution)/shard_map/ppermute | solution.py:374
  40.2 18.4 %collective-permute-done.incoming.hop1 = bf16[320,128]{1,0:T(8,128)(2,1)S(1)} collective-permute-done((bf16[320,128]{1,0:T(8,128)(2,1)S(1)}, bf16[320,128]{1,0:T(8,128)(2,1)S(1)}, u32[]{:S(2)}, u32[]{:S(2)}) %collective-permute-start) | collective-permute-done | bytes 81952 | tf_op jit(solution)/shard_map/ppermute | solution.py:374
  58.5 1.1 forward_second.1
  59.7 7.4 %collective-permute-start.1 = (bf16[320,128]{1,0:T(8,128)(2,1)S(1)}, bf16[320,128]{1,0:T(8,128)(2,1)S(1)}, u32[]{:S(2)}, u32[]{:S(2)}) collective-permute-start(bf16[320,128]{1,0:T(8,128)(2,1)S(1)} %forward_second.1), channel_id=1, source_target_pairs={{0,192},{16,208},{32,224},{48,240},{64,128},{80,144},{96,160},{112... | collective-permute-start | bytes 245768 | tf_op jit(solution)/shard_map/ppermute | solution.py:374
  67.1 2.8 %collective-permute-done.1.incoming.hop2 = bf16[320,128]{1,0:T(8,128)(2,1)S(1)} collective-permute-done((bf16[320,128]{1,0:T(8,128)(2,1)S(1)}, bf16[320,128]{1,0:T(8,128)(2,1)S(1)}, u32[]{:S(2)}, u32[]{:S(2)}) %collective-permute-start.1) | collective-permute-done | bytes 81952 | tf_op jit(solution)/shard_map/ppermute | solution.py:374
  71.2 5.3 %collective-permute-done.2.hop3 = bf16[320,128]{1,0:T(8,128)(2,1)S(1)} collective-permute-done((bf16[320,128]{1,0:T(8,128)(2,1)S(1)}, bf16[320,128]{1,0:T(8,128)(2,1)S(1)}, u32[]{:S(2)}, u32[]{:S(2)}) %collective-permute-start.2) | collective-permute-done | bytes 81952 | tf_op jit(solution)/shard_map/ppermute | solution.py:374
  76.5 2.0 %turn.1 = (bf16[320,128]{1,0:T(8,128)(2,1)S(1)}, bf16[4,320,128]{2,1,0:T(8,128)(2,1)S(1)}, f32[4,320,128]{2,1,0:T(8,128)S(1)}) custom-call(s32[1]{0:T(128)} %bitcast.5.group, bf16[4,1120,128]{2,1,0:T(8,128)(2,1)S(1)} %all-to-all-done.1.maps.front_maps, bf16[4,1920,128]{2,1,0:T(8,128)(2,1)S(1)} %all-to-all-done.back_maps.maps, ...), custom_call_target="tpu_custom_call" | custom-call | tf_op jit(solution)/shard_map/turn/pallas_call | solution.py:199
  78.6 5.3 %collective-permute-done.3.incoming.hop4 = bf16[320,128]{1,0:T(8,128)(2,1)S(1)} collective-permute-done((bf16[320,128]{1,0:T(8,128)(2,1)S(1)}, bf16[320,128]{1,0:T(8,128)(2,1)S(1)}, u32[]{:S(2)}, u32[]{:S(2)}) %collective-permute-start.3) | collective-permute-done | bytes 81952 | tf_op jit(solution)/shard_map/ppermute | solution.py:374
  83.9 1.1 backward_third.1
  85.1 4.6 %collective-permute-start.4 = (bf16[320,128]{1,0:T(8,128)(2,1)S(1)}, bf16[320,128]{1,0:T(8,128)(2,1)S(1)}, u32[]{:S(2)}, u32[]{:S(2)}) collective-permute-start(bf16[320,128]{1,0:T(8,128)(2,1)S(1)} %backward_third.1), channel_id=1, source_target_pairs={{0,192},{16,208},{32,224},{48,240},{64,128},{80,144},{96,160},{112... | collective-permute-start | bytes 245768 | tf_op jit(solution)/shard_map/ppermute | solution.py:374
  89.7 2.4 %collective-permute-done.4.incoming.hop5 = bf16[320,128]{1,0:T(8,128)(2,1)S(1)} collective-permute-done((bf16[320,128]{1,0:T(8,128)(2,1)S(1)}, bf16[320,128]{1,0:T(8,128)(2,1)S(1)}, u32[]{:S(2)}, u32[]{:S(2)}) %collective-permute-start.4) | collective-permute-done | bytes 81952 | tf_op jit(solution)/shard_map/ppermute | solution.py:374
  93.6 5.1 %collective-permute-done.5.hop6 = bf16[320,128]{1,0:T(8,128)(2,1)S(1)} collective-permute-done((bf16[320,128]{1,0:T(8,128)(2,1)S(1)}, bf16[320,128]{1,0:T(8,128)(2,1)S(1)}, u32[]{:S(2)}, u32[]{:S(2)}) %collective-permute-start.5) | collective-permute-done | bytes 81952 | tf_op jit(solution)/shard_map/ppermute | solution.py:374
  99.6 15.6 %all_to_all.15.ends = bf16[4,640,128]{2,1,0:T(8,128)(2,1)S(1)} all-to-all(bf16[4,640,128]{2,1,0:T(8,128)(2,1)S(1)} %interfaces.1), channel_id=1, replica_groups={{0,16,32,48},{64,80,96,112},{128,144,160,176},{192,208,224,240},{1,17,3..., dimensions={0} | all-to-all | bytes 1310720 | tf_op jit(solution)/shard_map/all_to_all | solution.py:370
  115.1 9.7 %finish.1 = (bf16[4,320,128]{2,1,0:T(8,128)(2,1)S(1)}, bf16[4,320,128]{2,1,0:T(8,128)(2,1)S(1)}, bf16[2,320,128]{2,1,0:T(8,128)(2,1)}, bf16[2,320,128]{2,1,0:T(8,128)(2,1)}) custom-call(s32[2,4]{1,0:T(2,128)S(1)} %copy-done.12, bf16[4,640,128]{2,1,0:T(8,128)(2,1)S(1)} %all_to_all.15.ends, bf16[8,320,320]{2,1,0:T(8,128)(2,1)S(1)} %bitcast.26, ...), custom_call_target="tpu_custom_call" | custom-call | tf_op jit(solution)/shard_map/finish/pallas_call | solution.py:83
  125.8 3.9 %collective-permute-start.8 = (bf16[2,320,128]{2,1,0:T(8,128)(2,1)}, bf16[2,320,128]{2,1,0:T(8,128)(2,1)}, u32[]{:S(2)}, u32[]{:S(2)}) collective-permute-start(bf16[2,320,128]{2,1,0:T(8,128)(2,1)} %get-tuple-element.23), channel_id=1, source_target_pairs={{1,0},{2,1},{3,2},{4,3},{5,4},{6,5},{7,6},{8,7},{9,8},{10,9},{11,1... | collective-permute-start | bytes 491528 | tf_op jit(solution)/shard_map/ppermute | solution.py:405
  129.7 9.3 %inner_jacobian.1 = (bf16[8,320,128]{2,1,0:T(8,128)(2,1)}, f32[8,320,128]{2,1,0:T(8,128)S(1)}) custom-call(s32[2,4]{1,0:T(2,128)S(1)} %copy-done.12, bf16[8,320,320]{2,1,0:T(8,128)(2,1)S(1)} %bitcast.36, bf16[8,320,320]{2,1,0:T(8,128)(2,1)} %bitcast.17, bf16[8,320,320]{2,1,0:T(8,128)(2,1)} %bitcast.41, bf16[8,320,320]{2,1,0:T(8,128)(2,1)} %bitcast.28, ...), custom_call_target="tpu_custom_call" | custom-call | tf_op jit(solution)/shard_map/inner_jacobian/pallas_call | solution.py:294
  139.1 3.3 %edge_jacobian.1 = bf16[8,320,128]{2,1,0:T(8,128)(2,1)} custom-call(s32[2,4]{1,0:T(2,128)S(1)} %copy-done.12, s32[3]{0:T(128)S(1)} %pad_add_fusion.place, bf16[8,320,320]{2,1,0:T(8,128)(2,1)S(1)} %bitcast.18, bf16[8,320,320]{2,1,0:T(8,128)(2,1)S(1)} %bitcast.19, bf16[8,320,320]{2,1,0:T(8,128)(2,1)S(1)} %bitcast.20, bf16[8,320,320]{2,1,0:T(8,128)(2,1)S(1)} %bitcast.21, ...), custom_call_target="tpu_custom_call" | custom-call | tf_op jit(solution)/shard_map/edge_jacobian/pallas_call | solution.py:337
  (38 shorter events, 9.1 us)
Async XLA Ops:
  0.6 1.5 %copy-start.1 = (bf16[2,4,320,320]{3,2,1,0:T(8,128)(2,1)S(1)}, bf16[2,4,320,320]{3,2,1,0:T(8,128)(2,1)}, u32[]{:S(2)}) copy-start(bf16[2,4,320,320]{3,2,1,0:T(8,128)(2,1)} %param.9) | copy-start | bytes 4915204
  2.2 1.1 copy-start.4
  3.3 0.7 copy-start.11
  10.4 0.8 copy-start.9
  11.2 5.1 %copy-start.5 = (bf16[2,4,320,128]{3,2,1,0:T(8,128)(2,1)S(1)}, bf16[2,4,320,128]{3,2,1,0:T(8,128)(2,1)}, u32[]{:S(2)}) copy-start(bf16[2,4,320,128]{3,2,1,0:T(8,128)(2,1)} %param.8) | copy-start | bytes 1966084
  11.2 5.1 %copy-start.12 = (s32[2,4]{1,0:T(2,128)S(1)}, s32[2,4]{1,0:T(2,128)}, u32[]{:S(2)}) copy-start(s32[2,4]{1,0:T(2,128)} %slots.9) | copy-start | bytes 100
  11.2 21.2 %all-to-all-start.1 = ((bf16[4,1120,128]{2,1,0:T(8,128)(2,1)}), bf16[4,1120,128]{2,1,0:T(8,128)(2,1)S(1)}, u32[]{:S(2)}, u32[]{:S(2)}) async-start(bf16[4,1120,128]{2,1,0:T(8,128)(2,1)} %get-tuple-element.13.front), calls=%async_computation.1 | async-start | bytes 2293760 | tf_op jit(solution)/shard_map/all_to_all | solution.py:370
  16.3 1.1 copy-start.10
  24.4 1.3 copy-start.7
  32.4 44.0 %all-to-all-start = ((bf16[4,1920,128]{2,1,0:T(8,128)(2,1)}), bf16[4,1920,128]{2,1,0:T(8,128)(2,1)S(1)}, u32[]{:S(2)}, u32[]{:S(2)}) async-start(bf16[4,1920,128]{2,1,0:T(8,128)(2,1)} %copy-done.7), calls=%async_computation | async-start | bytes 3932160 | tf_op jit(solution)/shard_map/all_to_all | solution.py:370
  36.8 21.7 %collective-permute-start = (bf16[320,128]{1,0:T(8,128)(2,1)S(1)}, bf16[320,128]{1,0:T(8,128)(2,1)S(1)}, u32[]{:S(2)}, u32[]{:S(2)}) collective-permute-start(bf16[320,128]{1,0:T(8,128)(2,1)S(1)} %forward_first.1), channel_id=1, source_target_pairs={{0,64},{16,80},{32,96},{48,112},{64,0},{80,16},{96,32},{112,48},{1... | collective-permute-start | bytes 245768 | tf_op jit(solution)/shard_map/ppermute | solution.py:374
  59.7 10.2 %collective-permute-start.1 = (bf16[320,128]{1,0:T(8,128)(2,1)S(1)}, bf16[320,128]{1,0:T(8,128)(2,1)S(1)}, u32[]{:S(2)}, u32[]{:S(2)}) collective-permute-start(bf16[320,128]{1,0:T(8,128)(2,1)S(1)} %forward_second.1), channel_id=1, source_target_pairs={{0,192},{16,208},{32,224},{48,240},{64,128},{80,144},{96,160},{112... | collective-permute-start | bytes 245768 | tf_op jit(solution)/shard_map/ppermute | solution.py:374
  71.0 5.4 %collective-permute-start.2 = (bf16[320,128]{1,0:T(8,128)(2,1)S(1)}, bf16[320,128]{1,0:T(8,128)(2,1)S(1)}, u32[]{:S(2)}, u32[]{:S(2)}) collective-permute-start(bf16[320,128]{1,0:T(8,128)(2,1)S(1)} %forward_third.1), channel_id=1, source_target_pairs={{0,64},{16,80},{32,96},{48,112},{64,0},{80,16},{96,32},{112,48},{1... | collective-permute-start | bytes 245768 | tf_op jit(solution)/shard_map/ppermute | solution.py:374
  78.5 5.4 %collective-permute-start.3 = (bf16[320,128]{1,0:T(8,128)(2,1)S(1)}, bf16[320,128]{1,0:T(8,128)(2,1)S(1)}, u32[]{:S(2)}, u32[]{:S(2)}) collective-permute-start(bf16[320,128]{1,0:T(8,128)(2,1)S(1)} %get-tuple-element.17), channel_id=1, source_target_pairs={{0,64},{16,80},{32,96},{48,112},{64,0},{80,16},{96,32},{112,48},{1... | collective-permute-start | bytes 245768 | tf_op jit(solution)/shard_map/ppermute | solution.py:374
  85.1 7.1 %collective-permute-start.4 = (bf16[320,128]{1,0:T(8,128)(2,1)S(1)}, bf16[320,128]{1,0:T(8,128)(2,1)S(1)}, u32[]{:S(2)}, u32[]{:S(2)}) collective-permute-start(bf16[320,128]{1,0:T(8,128)(2,1)S(1)} %backward_third.1), channel_id=1, source_target_pairs={{0,192},{16,208},{32,224},{48,240},{64,128},{80,144},{96,160},{112... | collective-permute-start | bytes 245768 | tf_op jit(solution)/shard_map/ppermute | solution.py:374
  93.3 5.4 %collective-permute-start.5 = (bf16[320,128]{1,0:T(8,128)(2,1)S(1)}, bf16[320,128]{1,0:T(8,128)(2,1)S(1)}, u32[]{:S(2)}, u32[]{:S(2)}) collective-permute-start(bf16[320,128]{1,0:T(8,128)(2,1)S(1)} %backward_second.1), channel_id=1, source_target_pairs={{0,64},{16,80},{32,96},{48,112},{64,0},{80,16},{96,32},{112,48},{1... | collective-permute-start | bytes 245768 | tf_op jit(solution)/shard_map/ppermute | solution.py:374
  98.7 16.4 %copy-start.2 = (bf16[2,4,320,320]{3,2,1,0:T(8,128)(2,1)S(1)}, bf16[2,4,320,320]{3,2,1,0:T(8,128)(2,1)}, u32[]{:S(2)}) copy-start(bf16[2,4,320,320]{3,2,1,0:T(8,128)(2,1)} %param.9) | copy-start | bytes 4915204
  98.7 16.4 %copy-start.6 = (bf16[2,4,320,128]{3,2,1,0:T(8,128)(2,1)S(1)}, bf16[2,4,320,128]{3,2,1,0:T(8,128)(2,1)}, u32[]{:S(2)}) copy-start(bf16[2,4,320,128]{3,2,1,0:T(8,128)(2,1)} %param.8) | copy-start | bytes 1966084
  115.1 14.6 %copy-start.8 = (bf16[2,4,320,320]{3,2,1,0:T(8,128)(2,1)S(1)}, bf16[2,4,320,320]{3,2,1,0:T(8,128)(2,1)}, u32[]{:S(2)}) copy-start(bf16[2,4,320,320]{3,2,1,0:T(8,128)(2,1)} %param.10) | copy-start | bytes 4915204
  124.9 14.2 %collective-permute-start.6 = (bf16[4,320,128]{2,1,0:T(8,128)(2,1)S(1)}, bf16[4,320,128]{2,1,0:T(8,128)(2,1)}, u32[]{:S(2)}, u32[]{:S(2)}) collective-permute-start(bf16[4,320,128]{2,1,0:T(8,128)(2,1)S(1)} %get-tuple-element.19.p1), channel_id=1, source_target_pairs={{0,16},{16,32},{32,48},{48,64},{64,80},{80,96},{96,112},{112,128},... | collective-permute-start | bytes 983048 | tf_op jit(solution)/shard_map/ppermute | solution.py:406
  125.8 13.3 %collective-permute-start.7 = (bf16[2,320,128]{2,1,0:T(8,128)(2,1)}, bf16[2,320,128]{2,1,0:T(8,128)(2,1)S(1)}, u32[]{:S(2)}, u32[]{:S(2)}) collective-permute-start(bf16[2,320,128]{2,1,0:T(8,128)(2,1)} %get-tuple-element.22), channel_id=1, source_target_pairs={{0,1},{1,2},{2,3},{3,4},{4,5},{5,6},{6,7},{7,8},{8,9},{9,10},{10,1... | collective-permute-start | bytes 491528 | tf_op jit(solution)/shard_map/ppermute | solution.py:404
  125.8 13.3 %collective-permute-start.8 = (bf16[2,320,128]{2,1,0:T(8,128)(2,1)}, bf16[2,320,128]{2,1,0:T(8,128)(2,1)}, u32[]{:S(2)}, u32[]{:S(2)}) collective-permute-start(bf16[2,320,128]{2,1,0:T(8,128)(2,1)} %get-tuple-element.23), channel_id=1, source_target_pairs={{1,0},{2,1},{3,2},{4,3},{5,4},{6,5},{7,6},{8,7},{9,8},{10,9},{11,1... | collective-permute-start | bytes 491528 | tf_op jit(solution)/shard_map/ppermute | solution.py:405
  129.7 9.3 %copy-start = (bf16[2,4,320,320]{3,2,1,0:T(8,128)(2,1)S(1)}, bf16[2,4,320,320]{3,2,1,0:T(8,128)(2,1)}, u32[]{:S(2)}) copy-start(bf16[2,4,320,320]{3,2,1,0:T(8,128)(2,1)} %param.11) | copy-start | bytes 4915204
  129.7 9.4 %copy-start.3 = (bf16[2,4,320,320]{3,2,1,0:T(8,128)(2,1)S(1)}, bf16[2,4,320,320]{3,2,1,0:T(8,128)(2,1)}, u32[]{:S(2)}) copy-start(bf16[2,4,320,320]{3,2,1,0:T(8,128)(2,1)} %param.13) | copy-start | bytes 4915204

commit v3 on v1

v3 whole, which is shorter than its diff:
```python
import jax
import jax.numpy as jnp
from jax import lax
from jax.experimental import pallas as pl
from jax.experimental.pallas import tpu as pltpu
from jax.sharding import PartitionSpec as P

BF = jnp.bfloat16
F32 = jnp.float32
GROUP = 4
VMEM_LIMIT = 48 << 20


def mm(a, b):
    return jnp.dot(a, b, preferred_element_type=F32)


def mm_fine(a, x):
    width = x.shape[1]
    top = x.astype(BF)
    rest = (x - top.astype(F32)).astype(BF)
    both = mm(a, jnp.concatenate([top, rest], axis=1))
    return both[:, :width] + both[:, width:]


def packed_rows(n):
    return 2 * n + n // 2


def pack(ref, base, mat):
    n = mat.shape[0]
    half = n // 2
    ref[base : base + n, :] = mat[:, 0:128]
    ref[base + n : base + 2 * n, :] = mat[:, 128:256]
    ref[base + 2 * n : base + 2 * n + half, 0:64] = mat[0:half, 256:320]
    ref[base + 2 * n : base + 2 * n + half, 64:128] = mat[half:n, 256:320]


def unpack(ref, base, n):
    half = n // 2
    tail = ref[base + 2 * n : base + 2 * n + half, :]
    last = jnp.concatenate([tail[:, 0:64], tail[:, 64:128]], axis=0)
    return jnp.concatenate(
        [ref[base : base + n, :], ref[base + n : base + 2 * n, :], last], axis=1
    )


def map_rows(n):
    return 3 * packed_rows(n) + 2 * n


def local_map_kernel(slots, place, d0, d1, l0, l1, u0, u1, r0, r1, out):
    n = d0.shape[0]
    rows = packed_rows(n)
    inv0, inv1 = d0[...], d1[...]
    e0 = mm(inv0, l0[...])
    e1 = mm(inv1, l1[...]).astype(BF)
    h0 = mm(inv0, u0[...]).astype(BF)
    h1 = mm(inv1, u1[...]).astype(BF)
    y0 = mm(inv0, r0[...])
    y1 = mm(inv1, r1[...])
    a = mm(e1, e0.astype(BF)).astype(BF)
    c = y1 - mm_fine(e1, y0)
    b = mm(h0, h1).astype(BF)
    g = -(e0 + mm(h0, a))
    h = y0 - mm_fine(h0, c)
    pack(out, 0, a)
    pack(out, rows, b)
    pack(out, 2 * rows, g.astype(BF))
    out[3 * rows : 3 * rows + n, :] = c.astype(BF)
    out[3 * rows + n : 3 * rows + 2 * n, :] = h.astype(BF)


def stored(slab, pencil, height, width):
    return pl.BlockSpec(
        (None, height, width), lambda i, sl, at: (sl[slab, pencil(at)], 0, 0)
    )


def constant(shape):
    return pl.BlockSpec(shape, lambda i, sl, at: (0,) * len(shape))


def element_call(kernel, in_specs, out_shape, slots, place, *operands, name):
    return pl.pallas_call(
        kernel,
        grid_spec=pltpu.PrefetchScalarGridSpec(
            num_scalar_prefetch=2,
            grid=(1,),
            in_specs=in_specs,
            out_specs=[constant(o.shape) for o in out_shape],
        ),
        out_shape=out_shape,
        compiler_params=pltpu.CompilerParams(vmem_limit_bytes=VMEM_LIMIT),
        name=name,
    )(slots, place, *operands)


def local_map(slots, place, diag_inv, lower, upper, source, distance):
    n, cols = source.shape[1:]

    def pencil(at):
        return lax.bitwise_xor(at[3], jnp.int32(distance))

    (out,) = element_call(
        local_map_kernel,
        [stored(s, pencil, n, n) for s in (0, 1, 0, 1, 0, 1)]
        + [stored(s, pencil, n, cols) for s in (0, 1)],
        [jax.ShapeDtypeStruct((map_rows(n), cols), BF)],
        slots, place, diag_inv, diag_inv, lower, lower, upper, upper, source, source,
        name="local_map",
    )
    return out


def gather_maps(place, pieces, maps, sems):
    copies = []
    for distance, piece in enumerate(pieces):
        owner = lax.bitwise_xor(place[3], jnp.int32(distance))
        copy = pltpu.make_async_copy(piece, maps.at[owner], sems.at[distance])
        copy.start()
        copies.append(copy)
    for copy in copies:
        copy.wait()


def group_front_kernel(place, own, near, next_one, across, send, maps, sems):
    n = send.shape[0]
    rows = packed_rows(n)
    copies = []
    for distance, piece in enumerate((own, near, next_one, across)):
        owner = lax.bitwise_xor(place[3], jnp.int32(distance))
        for part, (start, size, to) in enumerate(((0, rows, 0), (3 * rows, n, rows))):
            copies.append(
                pltpu.make_async_copy(
                    piece.at[pl.ds(start, size)],
                    maps.at[owner, pl.ds(to, size)],
                    sems.at[distance, part],
                )
            )
            copies[-1].start()
    for copy in copies:
        copy.wait()
    front = maps[0, rows : rows + n, :].astype(F32)
    for j in range(1, GROUP):
        shift = maps[j, rows : rows + n, :].astype(F32)
        front = mm_fine(unpack(maps.at[j], 0, n), front) + shift
    send[...] = front.astype(BF)


def group_front(place, pieces, n, cols):
    return pl.pallas_call(
        group_front_kernel,
        in_specs=[pl.BlockSpec(memory_space=pltpu.SMEM)]
        + [pl.BlockSpec(memory_space=pl.ANY)] * GROUP,
        out_specs=pl.BlockSpec(memory_space=pltpu.VMEM),
        out_shape=jax.ShapeDtypeStruct((n, cols), BF),
        scratch_shapes=[
            pltpu.VMEM((GROUP, packed_rows(n) + n, cols), BF),
            pltpu.SemaphoreType.DMA((GROUP, 2)),
        ],
        compiler_params=pltpu.CompilerParams(vmem_limit_bytes=VMEM_LIMIT),
        name="group_front",
    )(place, *pieces)


def joined(left, right):
    a_l, b_l, g_l, c_l, h_l = left
    a_r, b_r, g_r, c_r, h_r = right
    a = mm(a_r, a_l).astype(BF)
    b = mm(b_l, b_r).astype(BF)
    g = (mm(b_l, mm(g_r, a_l).astype(BF)) + g_l.astype(F32)).astype(BF)
    c = mm_fine(a_r, c_l) + c_r
    h = mm_fine(b_l, mm_fine(g_r, c_l) + h_r) + h_l
    return a, b, g, c, h


def segment(maps, j, n):
    rows = packed_rows(n)
    one = maps.at[j]
    return (
        unpack(one, 0, n),
        unpack(one, rows, n),
        unpack(one, 2 * rows, n),
        one[3 * rows : 3 * rows + n, :].astype(F32),
        one[3 * rows + n : 3 * rows + 2 * n, :].astype(F32),
    )


def group_map_kernel(
    place, after, own, near, next_one, across, a_out, b_out, g_out, c_out, h_out, send_far, maps, sems
):
    n = a_out.shape[0]
    gather_maps(place, (own, near, next_one, across), maps, sems)
    a, b, g, c, h = joined(
        joined(segment(maps, 0, n), segment(maps, 1, n)),
        joined(segment(maps, 2, n), segment(maps, 3, n)),
    )
    a_out[...] = a
    b_out[...] = b
    g_out[...] = g
    c_out[...] = c
    h_out[...] = h
    send_far[0:n, :] = h.astype(BF)
    pack(send_far, n, g)


def group_map(place, after, pieces, n, cols):
    shapes = [
        ((n, n), BF), ((n, n), BF), ((n, n), BF), ((n, cols), F32), ((n, cols), F32),
        ((n + packed_rows(n), cols), BF),
    ]
    return pl.pallas_call(
        group_map_kernel,
        in_specs=[pl.BlockSpec(memory_space=pltpu.SMEM)]
        + [pl.BlockSpec(memory_space=pl.ANY)] * (GROUP + 1),
        out_specs=[pl.BlockSpec(memory_space=pltpu.VMEM)] * len(shapes),
        out_shape=[jax.ShapeDtypeStruct(s, d) for s, d in shapes],
        scratch_shapes=[
            pltpu.VMEM((GROUP, map_rows(n), cols), BF), pltpu.SemaphoreType.DMA((GROUP,))
        ],
        compiler_params=pltpu.CompilerParams(vmem_limit_bytes=VMEM_LIMIT),
        name="group_map",
    )(place, after, *pieces)


def forward_one_kernel(a, c, incoming, send):
    send[...] = (mm(a[...], incoming[...]) + c[...]).astype(BF)


def turn_kernel(a, b, g, c, h, far, incoming, send, front_out, back_in):
    n = a.shape[0]
    front = incoming[...]
    ahead = mm(a[...], front) + c[...]
    back = mm_fine(unpack(far, n, n), ahead) + far[0:n, :].astype(F32)
    send[...] = (mm_fine(b[...], back) + (mm(g[...], front) + h[...])).astype(BF)
    front_out[...] = ahead.astype(BF)
    back_in[...] = back.astype(BF)


def backward_one_kernel(place, b, g, h, hop1, incoming, ahead, send):
    back = mm(b[...], incoming[...]) + (mm(g[...], hop1[...]) + h[...])
    send[...] = jnp.where(place[4] == 1, back.astype(BF), ahead[...])


def interfaces_kernel(
    place, own, near, next_one, across, hop1, hop2, hop3, back2, hop4, out, maps, sems
):
    n = hop2.shape[0]
    rows = packed_rows(n)
    which = place[4]
    gather_maps(place, (own, near, next_one, across), maps, sems)
    zero = jnp.zeros_like(hop2[...])
    front = jnp.where(
        which == 0, zero,
        jnp.where(which == 1, hop1[...], jnp.where(which == 2, hop2[...], hop4[...])),
    ).astype(F32)
    back = jnp.where(
        which == 0, hop4[...],
        jnp.where(which == 1, hop3[...], jnp.where(which == 2, back2[...], zero)),
    ).astype(F32)
    fronts = [front]
    for j in range(GROUP - 1):
        shift = maps[j, 3 * rows : 3 * rows + n, :].astype(F32)
        front = mm_fine(unpack(maps.at[j], 0, n), front) + shift
        fronts.append(front)
    for j in reversed(range(GROUP)):
        out[j, 0:n, :] = fronts[j].astype(BF)
        out[j, n : 2 * n, :] = back.astype(BF)
        if j:
            shift = maps[j, 3 * rows + n : 3 * rows + 2 * n, :].astype(F32)
            inner = mm_fine(unpack(maps.at[j], 2 * rows, n), fronts[j]) + shift
            back = mm_fine(unpack(maps.at[j], rows, n), back) + inner


def interfaces(place, pieces, n, cols, *hops):
    return pl.pallas_call(
        interfaces_kernel,
        in_specs=[pl.BlockSpec(memory_space=pltpu.SMEM)]
        + [pl.BlockSpec(memory_space=pl.ANY)] * GROUP
        + [pl.BlockSpec(memory_space=pltpu.VMEM)] * len(hops),
        out_specs=pl.BlockSpec(memory_space=pltpu.VMEM),
        out_shape=jax.ShapeDtypeStruct((GROUP, 2 * n, cols), BF),
        scratch_shapes=[
            pltpu.VMEM((GROUP, map_rows(n), cols), BF), pltpu.SemaphoreType.DMA((GROUP,))
        ],
        compiler_params=pltpu.CompilerParams(vmem_limit_bytes=VMEM_LIMIT),
        name="interfaces",
    )(place, *pieces, *hops)


def whole_call(kernel, outs, scalars, *operands, name):
    specs = [pl.BlockSpec(memory_space=pltpu.SMEM)] * len(scalars)
    specs += [pl.BlockSpec(memory_space=pltpu.VMEM)] * len(operands)
    return pl.pallas_call(
        kernel,
        in_specs=specs,
        out_specs=[pl.BlockSpec(memory_space=pltpu.VMEM)] * len(outs),
        out_shape=[jax.ShapeDtypeStruct(s, d) for s, d in outs],
        compiler_params=pltpu.CompilerParams(vmem_limit_bytes=VMEM_LIMIT),
        name=name,
    )(*scalars, *operands)


def solve_pencils(ends, columns):
    n = ends[0].shape[0] // 2
    fronts = [e[0:n, :] for e in ends]
    backs = [e[n : 2 * n, :] for e in ends]
    both = range(len(ends))
    d0, d1, l0, l1, u0, u1, r0, r1 = zip(*columns)
    v = [mm(u1[i][...], backs[i]) for i in both]
    q = [r0[i][...].astype(F32) - mm(l0[i][...], fronts[i]) for i in both]
    f0 = [mm_fine(d0[i][...], q[i]) for i in both]
    v = [mm_fine(d1[i][...], v[i]) for i in both]
    q = [r1[i][...].astype(F32) - mm_fine(l1[i][...], f0[i]) for i in both]
    x1 = [mm_fine(d1[i][...], q[i]) - v[i] for i in both]
    q = [mm_fine(u0[i][...], x1[i]) for i in both]
    x0 = [f0[i] - mm_fine(d0[i][...], q[i]) for i in both]
    return [(x0[i].astype(BF), x1[i].astype(BF)) for i in both]


def outer_pencils_kernel(slots, place, ends, *refs):
    first, last = refs[16:]
    solved = solve_pencils([ends[0], ends[GROUP - 1]], [refs[0:8], refs[8:16]])
    for (x0, x1), out in zip(solved, (first, last)):
        out[0] = x0
        out[1] = x1


def inner_pencils_kernel(slots, place, ends, *refs):
    first, last, second, third, tops = refs[16:]
    solved = solve_pencils([ends[1], ends[2]], [refs[0:8], refs[8:16]])
    for (x0, x1), out, pencil in zip(solved, (second, third), (1, 2)):
        out[0] = x0
        out[1] = x1
        tops[pencil] = x1
    tops[0] = first[1]
    tops[GROUP - 1] = last[1]


def pencils(kernel, chosen, outs, slots, place, ends, diag_inv, lower, upper, source, *more, name):
    n, cols = source.shape[1:]
    specs, operands = [constant(ends.shape)], [ends]
    for p in chosen:
        for array in (diag_inv, lower, upper, source):
            for s in range(2):
                specs.append(stored(s, lambda at, p=p: p, n, array.shape[-1]))
                operands.append(array)
    specs += [constant(m.shape) for m in more]
    return element_call(
        kernel, specs, [jax.ShapeDtypeStruct(o, BF) for o in outs],
        slots, place, *operands, *more, name=name,
    )


def inner_jacobian_kernel(slots, *refs):
    blocks, (first, second, third, last, ends) = refs[0:10], refs[10:15]
    precond, partial, vals = refs[15:]
    n = first.shape[1]
    pencil = pl.program_id(0)

    @pl.when(pencil == 0)
    def _():
        zero = jnp.zeros(first.shape[1:], BF)
        for p, values in enumerate((first, second, third, last)):
            vals[0, p + 1] = zero
            vals[1, p + 1] = values[0]
            vals[2, p + 1] = values[1]
            vals[3, p + 1] = ends[p, n : 2 * n, :]
        for s in range(2):
            vals[s + 1, 0] = zero
            vals[s + 1, GROUP + 1] = zero

    both = range(2)
    near = [
        [
            vals[s + 1, pencil + 1], vals[s, pencil + 1], vals[s + 2, pencil + 1],
            vals[s + 1, pencil], vals[s + 1, pencil + 2],
        ]
        for s in both
    ]
    totals = [mm(blocks[5 * s][...], near[s][0]) for s in both]
    for t in range(1, 5):
        totals = [totals[s] + mm(blocks[5 * s + t][...], near[s][t]) for s in both]
    for s in both:
        precond[slots[s, pencil]] = near[s][0]
        partial[s] = totals[s]


def inner_jacobian(slots, blocks, vectors):
    n, cols = vectors[0].shape[1:]

    def whole(shape):
        return pl.BlockSpec(shape, lambda p, sl: (0, 0, 0))

    specs = [
        pl.BlockSpec((None, n, n), lambda p, sl, s=s: (sl[s, p], 0, 0))
        for s in range(2)
        for _ in blocks
    ]
    stored_shape = (2 * GROUP, n, cols)
    return pl.pallas_call(
        inner_jacobian_kernel,
        grid_spec=pltpu.PrefetchScalarGridSpec(
            num_scalar_prefetch=1,
            grid=(GROUP,),
            in_specs=specs + [whole(v.shape) for v in vectors],
            out_specs=[
                whole(stored_shape),
                pl.BlockSpec((None, 2, n, cols), lambda p, sl: (p, 0, 0, 0)),
            ],
            scratch_shapes=[pltpu.VMEM((4, GROUP + 2, n, cols), BF)],
        ),
        out_shape=[
            jax.ShapeDtypeStruct(stored_shape, BF),
            jax.ShapeDtypeStruct((GROUP, 2, n, cols), F32),
        ],
        compiler_params=pltpu.CompilerParams(vmem_limit_bytes=VMEM_LIMIT),
        name="inner_jacobian",
    )(slots, *blocks, *blocks, *vectors)


def edge_jacobian_kernel(slots, place, *refs):
    lowers, minuses, pluses = refs[0:4], refs[4:6], refs[6:8]
    partial, below, low, high, jac = refs[8:]
    left = jnp.where(place[1] == 0, 0.0, 1.0).astype(F32)
    right = jnp.where(place[1] == place[2] - 1, 0.0, 1.0).astype(F32)
    start = jnp.where(place[0] == 0, 0.0, 1.0).astype(F32)
    for s in range(2):
        for p in range(GROUP):
            total = partial[p, s]
            if s == 0:
                total = total + start * mm(lowers[p][...], below[p])
            if p == 0:
                total = total + left * mm(minuses[s][...], low[s])
            if p == GROUP - 1:
                total = total + right * mm(pluses[s][...], high[s])
            jac[slots[s, p]] = total.astype(BF)


def edge_jacobian(slots, place, lower, minus, plus, partial, below, low, high):
    n, cols = below.shape[1:]

    def block(s, p):
        return pl.BlockSpec((None, n, n), lambda i, sl, pc: (sl[s, p], 0, 0))

    def whole(shape):
        return pl.BlockSpec(shape, lambda i, sl, pc: (0,) * len(shape))

    vectors = (partial, below, low, high)
    return pl.pallas_call(
        edge_jacobian_kernel,
        grid_spec=pltpu.PrefetchScalarGridSpec(
            num_scalar_prefetch=2,
            grid=(1,),
            in_specs=[block(0, p) for p in range(GROUP)]
            + [block(s, 0) for s in range(2)]
            + [block(s, GROUP - 1) for s in range(2)]
            + [whole(v.shape) for v in vectors],
            out_specs=whole((2 * GROUP, n, cols)),
        ),
        out_shape=jax.ShapeDtypeStruct((2 * GROUP, n, cols), BF),
        compiler_params=pltpu.CompilerParams(vmem_limit_bytes=VMEM_LIMIT),
        name="edge_jacobian",
    )(slots, place, *([lower] * GROUP), minus, minus, plus, plus, *vectors)


def local(right_side, diag_inv, diag_blk, lower_blk, upper_blk, cross_minus, cross_plus, elem_slot):
    n, cols = right_side.shape[2:]
    source, inverse, diagonal, lower, upper, minus, plus = (
        pltpu.with_memory_space_constraint(
            values.reshape((-1,) + values.shape[2:]), pltpu.HBM
        )
        for values in (
            right_side, diag_inv, diag_blk, lower_blk, upper_blk, cross_minus, cross_plus
        )
    )
    count = lax.axis_size("sweep")
    across = lax.axis_size("cross")
    sweep_at = lax.axis_index("sweep")
    place = jnp.stack(
        [
            sweep_at, lax.axis_index("cross"), jnp.int32(across),
            lax.rem(sweep_at, GROUP), lax.div(sweep_at, GROUP),
        ]
    ).astype(jnp.int32)
    groups = [list(range(g, g + GROUP)) for g in range(0, count, GROUP)]

    def swap(values, order):
        pairs = [(g * GROUP + k, order[g] * GROUP + k) for g in range(GROUP) for k in range(GROUP)]
        return lax.ppermute(values, "sweep", pairs)

    def to_peer(values, distance):
        return lax.ppermute(values, "sweep", [(i, i ^ distance) for i in range(count)])

    outer, inner = (1, 0, 3, 2), (3, 2, 1, 0)
    maps = [None] * GROUP
    for distance in (3, 1, 2, 0):
        piece = local_map(elem_slot, place, inverse, lower, upper, source, distance)
        maps[distance] = to_peer(piece, distance) if distance else piece

    send = group_front(place, maps, n, cols)
    hop1 = swap(send, outer)
    a, b, g, c, h, send_far = group_map(place, send, maps, n, cols)
    far = swap(send_far, outer)
    vec = ((n, cols), BF)
    (send,) = whole_call(forward_one_kernel, [vec], [], a, c, hop1, name="forward_one")
    hop2 = swap(send, inner)
    send, ahead, back2 = whole_call(
        turn_kernel, [vec, vec, vec], [], a, b, g, c, h, far, hop2, name="turn"
    )
    hop3 = swap(send, inner)
    (send,) = whole_call(
        backward_one_kernel, [vec], [place], b, g, h, hop1, hop3, ahead, name="backward_one"
    )
    hop4 = swap(send, outer)
    ends = interfaces(place, maps, n, cols, hop1, hop2, hop3, back2, hop4)
    ends = lax.all_to_all(ends, "sweep", 0, 0, axis_index_groups=groups)

    pair, four = (2, n, cols), (GROUP, n, cols)
    first, last = pencils(
        outer_pencils_kernel, (0, GROUP - 1), [pair, pair],
        elem_slot, place, ends, inverse, lower, upper, source, name="outer_pencils",
    )
    low = lax.ppermute(last, "cross", [(i, (i + 1) % across) for i in range(across)])
    high = lax.ppermute(first, "cross", [((i + 1) % across, i) for i in range(across)])
    second, third, tops = pencils(
        inner_pencils_kernel, (1, 2), [pair, pair, four],
        elem_slot, place, ends, inverse, lower, upper, source, first, last, name="inner_pencils",
    )
    below = lax.ppermute(tops, "sweep", [(i, (i + 1) % count) for i in range(count)])
    precond, partial = inner_jacobian(
        elem_slot, (diagonal, lower, upper, minus, plus), (first, second, third, last, ends)
    )
    jac = edge_jacobian(elem_slot, place, lower, minus, plus, partial, below, low, high)
    return precond.reshape(right_side.shape), jac.reshape(right_side.shape)


def solution(mesh):
    blocks = P("sweep", "cross", None, None)
    in_specs = (blocks,) * 7 + (P("sweep", "cross"),)
    return jax.shard_map(
        local, mesh=mesh, in_specs=in_specs, out_specs=(blocks, blocks), check_vma=False
    )
```

time: 143 us -> 140 us (0.979)
  Pallas kernels: 28.3 us -> 48.5 us
  waiting for transfers between devices: 67.7 us -> 55.4 us
  local copies, waits for them, and re-layouts: 8.94 us -> 0.76 us
  starting transfers between devices: 23.2 us -> 21.5 us
    all_to_all x1 -> x0, waiting for transfers between devices: 37.2 us -> none  [exchange(): return lax.all_to_all(values, 'sweep', 0, 0, axis_index_groups=groups)]
    ppermute x1 -> x4, waiting for transfers between devices: 4.46 us -> 29.8 us  [the longest x3 26.3 us: to_peer(): lax.ppermute(values, 'sweep', [(i, i ^ distance) for i in range(count)])]
    pallas_call x3 -> x11, Pallas kernels: 22.5 us -> 46.7 us  [the longest x6 23.4 us: element_call(): pl.pallas_call(kernel, grid_spec=pltpu.PrefetchScalarGridSpec(num_scalar_...]
    unnamed x28 -> x2, local copies, waits for them, and re-layouts: 8.18 us -> 0.68 us
    ppermute x1 -> x4, starting transfers between devices: 0.92 us -> 6.25 us  [the longest x3 5.25 us: to_peer(): lax.ppermute(values, 'sweep', [(i, i ^ distance) for i in range(count)])]
    all_to_all x1 -> x0, starting transfers between devices: 4.91 us -> none  [exchange(): return lax.all_to_all(values, 'sweep', 0, 0, axis_index_groups=groups)]
    pallas_call x5 -> x3, Pallas kernels: 5.78 us -> 1.85 us  [whole_call(): pl.pallas_call(kernel, in_specs=specs, out_specs=[pl.BlockSpec(memory_spa...]
    ppermute x1, starting transfers between devices: 3.85 us -> 0.01 us  [local(): lax.ppermute(first, 'cross', [((i + 1) % across, i) for i in range(across)])]
  transfers between devices with their start and end apart: 8 -> 11, of which waited for: 7 -> 8; matrix products, arithmetic and copies ran while one was open for 0% -> 0% of each run, Pallas kernels for 0% -> 13%
where the time goes in v3:
time: 140 us
  waiting for transfers between devices  55.4 us (40%)
  Pallas kernels  48.5 us (35%)
  starting transfers between devices  21.5 us (15%)
  blocking collectives  13.1 us (9%)
    ppermute x3, waiting for transfers between devices, to_peer(): lax.ppermute(values, 'sweep', [(i, i ^ distance) for i in range(count)])  26.3 us
    ppermute x5, waiting for transfers between devices, swap(): return lax.ppermute(values, 'sweep', pairs)  25.6 us
    pallas_call x6, Pallas kernels, element_call(): pl.pallas_call(kernel, grid_spec=pltpu.PrefetchScalarGridSpec(num_scalar_...  23.4 us
    ppermute x5, starting transfers between devices, swap(): return lax.ppermute(values, 'sweep', pairs)  14.7 us
    all_to_all x1, blocking collectives, local(): ends = lax.all_to_all(ends, 'sweep', 0, 0, axis_index_groups=groups)  13.1 us
    pallas_call x1, Pallas kernels, inner_jacobian(): pl.pallas_call(inner_jacobian_kernel, grid_spec=pltpu.PrefetchScalarGridS...  7.49 us
    pallas_call x1, Pallas kernels, group_map(): pl.pallas_call(group_map_kernel, in_specs=[pl.BlockSpec(memory_space=pltp...  5.54 us
    ppermute x3, starting transfers between devices, to_peer(): lax.ppermute(values, 'sweep', [(i, i ^ distance) for i in range(count)])  5.25 us
  transfers between devices with their start and end apart: 11, of which 8 were waited for; matrix products, arithmetic and copies ran while one was open for 0% of the time, Pallas kernels for 13%

profile of v3, /device:TPU:8, one launch (start us, length us, event | category | flops | bytes accessed | tf_op | source)
XLA Modules:
  0.0 140.0 jit_solution(502825200130812262)
XLA Ops:
  1.4 3.6 %local_map.5 = bf16[3040,128]{1,0:T(8,128)(2,1)S(1)} custom-call(s32[2,4]{1,0:T(2,128)S(1)} %copy-done, s32[5]{0:T(128)S(1)} %stack.19.place, bf16[8,320,320]{2,1,0:T(8,128)(2,1)} %bitcast.53, bf16[8,320,320]{2,1,0:T(8,128)(2,1)} %bitcast.54, bf16[8,320,320]{2,1,0:T(8,128)(2,1)} %bitcast.13, bf16[8,320,320]{2,1,0:T(8,128)(2,1)} %bitcast.14, ...), custom_call_target="tpu_custom_call" | custom-call | tf_op jit(solution)/shard_map/local_map/pallas_call | solution.py:85
  7.4 3.6 %local_map.6 = bf16[3040,128]{1,0:T(8,128)(2,1)S(1)} custom-call(s32[2,4]{1,0:T(2,128)S(1)} %copy-done, s32[5]{0:T(128)S(1)} %stack.19.place, bf16[8,320,320]{2,1,0:T(8,128)(2,1)} %bitcast.55, bf16[8,320,320]{2,1,0:T(8,128)(2,1)} %bitcast.56, bf16[8,320,320]{2,1,0:T(8,128)(2,1)} %bitcast.15, bf16[8,320,320]{2,1,0:T(8,128)(2,1)} %bitcast.16, ...), custom_call_target="tpu_custom_call" | custom-call | tf_op jit(solution)/shard_map/local_map/pallas_call | solution.py:85
  13.0 3.6 %local_map.7 = bf16[3040,128]{1,0:T(8,128)(2,1)S(1)} custom-call(s32[2,4]{1,0:T(2,128)S(1)} %copy-done, s32[5]{0:T(128)S(1)} %stack.19.place, bf16[8,320,320]{2,1,0:T(8,128)(2,1)} %bitcast.57, bf16[8,320,320]{2,1,0:T(8,128)(2,1)} %bitcast.58, bf16[8,320,320]{2,1,0:T(8,128)(2,1)} %bitcast.17, bf16[8,320,320]{2,1,0:T(8,128)(2,1)} %bitcast.18, ...), custom_call_target="tpu_custom_call" | custom-call | tf_op jit(solution)/shard_map/local_map/pallas_call | solution.py:85
  17.5 3.6 %local_map.4.own = bf16[3040,128]{1,0:T(8,128)(2,1)S(1)} custom-call(s32[2,4]{1,0:T(2,128)S(1)} %copy-done, s32[5]{0:T(128)S(1)} %stack.19.place, bf16[8,320,320]{2,1,0:T(8,128)(2,1)} %bitcast.59, bf16[8,320,320]{2,1,0:T(8,128)(2,1)} %bitcast.60, bf16[8,320,320]{2,1,0:T(8,128)(2,1)} %bitcast.19, bf16[8,320,320]{2,1,0:T(8,128)(2,1)} %bitcast.20, ...), custom_call_target="tpu_custom_call" | custom-call | tf_op jit(solution)/shard_map/local_map/pallas_call | solution.py:85
  21.2 4.6 %collective-permute-done.near = bf16[3040,128]{1,0:T(8,128)(2,1)S(1)} collective-permute-done((bf16[3040,128]{1,0:T(8,128)(2,1)S(1)}, bf16[3040,128]{1,0:T(8,128)(2,1)S(1)}, u32[]{:S(2)}, u32[]{:S(2)}) %collective-permute-start) | collective-permute-done | bytes 778272 | tf_op jit(solution)/shard_map/ppermute | solution.py:494
  25.7 5.7 %collective-permute-done.1.next_one = bf16[3040,128]{1,0:T(8,128)(2,1)S(1)} collective-permute-done((bf16[3040,128]{1,0:T(8,128)(2,1)S(1)}, bf16[3040,128]{1,0:T(8,128)(2,1)S(1)}, u32[]{:S(2)}, u32[]{:S(2)}) %collective-permute-start.1) | collective-permute-done | bytes 778272 | tf_op jit(solution)/shard_map/ppermute | solution.py:494
  31.4 16.1 %collective-permute-done.2.across = bf16[3040,128]{1,0:T(8,128)(2,1)S(1)} collective-permute-done((bf16[3040,128]{1,0:T(8,128)(2,1)S(1)}, bf16[3040,128]{1,0:T(8,128)(2,1)S(1)}, u32[]{:S(2)}, u32[]{:S(2)}) %collective-permute-start.2) | collective-permute-done | bytes 778272 | tf_op jit(solution)/shard_map/ppermute | solution.py:494
  47.5 2.9 %group_front.1.after = bf16[320,128]{1,0:T(8,128)(2,1)S(1)} custom-call(s32[5]{0:T(128)S(1)} %stack.19.place, bf16[3040,128]{1,0:T(8,128)(2,1)S(1)} %local_map.4.own, bf16[3040,128]{1,0:T(8,128)(2,1)S(1)} %collective-permute-done.near, bf16[3040,128]{1,0:T(8,128)(2,1)S(1)} %collective-permute-done.1.next_one, bf16[3040,128]{1,0:T(8,128)(2,1)S(1)} %collective-permute-done.2.across), custom_call_target="tpu_custom_call" | custom-call | tf_op jit(solution)/shard_map/group_front/pallas_call | solution.py:152
  50.4 5.5 %group_map.1 = (bf16[320,320]{1,0:T(8,128)(2,1)S(1)}, bf16[320,320]{1,0:T(8,128)(2,1)S(1)}, bf16[320,320]{1,0:T(8,128)(2,1)S(1)}, f32[320,128]{1,0:T(8,128)S(1)}...) custom-call(s32[5]{0:T(128)S(1)} %stack.19.place, bf16[320,128]{1,0:T(8,128)(2,1)S(1)} %group_front.1.after, ...), custom_call_target="tpu_custom_call" | custom-call | tf_op jit(solution)/shard_map/group_map/pallas_call | solution.py:213
  55.9 3.4 %collective-permute-start.5 = (bf16[1120,128]{1,0:T(8,128)(2,1)S(1)}, bf16[1120,128]{1,0:T(8,128)(2,1)S(1)}, u32[]{:S(2)}, u32[]{:S(2)}) collective-permute-start(bf16[1120,128]{1,0:T(8,128)(2,1)S(1)} %get-tuple-element.23), channel_id=1, source_target_pairs={{0,64},{16,80},{32,96},{48,112},{64,0},{80,16},{96,32},{112,48},{1... | collective-permute-start | bytes 860168 | tf_op jit(solution)/shard_map/ppermute | solution.py:491
  59.6 15.2 %collective-permute-done.3.incoming.hop1 = bf16[320,128]{1,0:T(8,128)(2,1)S(1)} collective-permute-done((bf16[320,128]{1,0:T(8,128)(2,1)S(1)}, bf16[320,128]{1,0:T(8,128)(2,1)S(1)}, u32[]{:S(2)}, u32[]{:S(2)}) %collective-permute-start.3) | collective-permute-done | bytes 81952 | tf_op jit(solution)/shard_map/ppermute | solution.py:491
  75.0 3.4 %collective-permute-start.4 = (bf16[320,128]{1,0:T(8,128)(2,1)S(1)}, bf16[320,128]{1,0:T(8,128)(2,1)S(1)}, u32[]{:S(2)}, u32[]{:S(2)}) collective-permute-start(bf16[320,128]{1,0:T(8,128)(2,1)S(1)} %forward_one.1), channel_id=1, source_target_pairs={{0,192},{16,208},{32,224},{48,240},{64,128},{80,144},{96,160},{112... | collective-permute-start | bytes 245768 | tf_op jit(solution)/shard_map/ppermute | solution.py:491
  78.5 3.3 %collective-permute-done.4.incoming.hop2 = bf16[320,128]{1,0:T(8,128)(2,1)S(1)} collective-permute-done((bf16[320,128]{1,0:T(8,128)(2,1)S(1)}, bf16[320,128]{1,0:T(8,128)(2,1)S(1)}, u32[]{:S(2)}, u32[]{:S(2)}) %collective-permute-start.4) | collective-permute-done | bytes 81952 | tf_op jit(solution)/shard_map/ppermute | solution.py:491
  82.6 3.3 %collective-permute-start.6 = (bf16[320,128]{1,0:T(8,128)(2,1)S(1)}, bf16[320,128]{1,0:T(8,128)(2,1)S(1)}, u32[]{:S(2)}, u32[]{:S(2)}) collective-permute-start(bf16[320,128]{1,0:T(8,128)(2,1)S(1)} %get-tuple-element.24), channel_id=1, source_target_pairs={{0,192},{16,208},{32,224},{48,240},{64,128},{80,144},{96,160},{112... | collective-permute-start | bytes 245768 | tf_op jit(solution)/shard_map/ppermute | solution.py:491
  85.9 3.4 %collective-permute-done.6.incoming.hop3 = bf16[320,128]{1,0:T(8,128)(2,1)S(1)} collective-permute-done((bf16[320,128]{1,0:T(8,128)(2,1)S(1)}, bf16[320,128]{1,0:T(8,128)(2,1)S(1)}, u32[]{:S(2)}, u32[]{:S(2)}) %collective-permute-start.6) | collective-permute-done | bytes 81952 | tf_op jit(solution)/shard_map/ppermute | solution.py:491
  90.2 4.3 %collective-permute-start.7 = (bf16[320,128]{1,0:T(8,128)(2,1)S(1)}, bf16[320,128]{1,0:T(8,128)(2,1)S(1)}, u32[]{:S(2)}, u32[]{:S(2)}) collective-permute-start(bf16[320,128]{1,0:T(8,128)(2,1)S(1)} %backward_one.1), channel_id=1, source_target_pairs={{0,64},{16,80},{32,96},{48,112},{64,0},{80,16},{96,32},{112,48},{1... | collective-permute-start | bytes 245768 | tf_op jit(solution)/shard_map/ppermute | solution.py:491
  94.5 3.6 %collective-permute-done.7.hop4 = bf16[320,128]{1,0:T(8,128)(2,1)S(1)} collective-permute-done((bf16[320,128]{1,0:T(8,128)(2,1)S(1)}, bf16[320,128]{1,0:T(8,128)(2,1)S(1)}, u32[]{:S(2)}, u32[]{:S(2)}) %collective-permute-start.7) | collective-permute-done | bytes 81952 | tf_op jit(solution)/shard_map/ppermute | solution.py:491
  98.1 3.7 %interfaces.1 = bf16[4,640,128]{2,1,0:T(8,128)(2,1)S(1)} custom-call(s32[5]{0:T(128)S(1)} %stack.19.place, bf16[3040,128]{1,0:T(8,128)(2,1)S(1)} %local_map.4.own, bf16[3040,128]{1,0:T(8,128)(2,1)S(1)} %collective-permute-done.near, bf16[3040,128]{1,0:T(8,128)(2,1)S(1)} %collective-permute-done.1.next_one, ...), custom_call_target="tpu_custom_call" | custom-call | tf_op jit(solution)/shard_map/interfaces/pallas_call | solution.py:277
  101.8 13.1 %all_to_all.5.ends.refs_14_ = bf16[4,640,128]{2,1,0:T(8,128)(2,1)S(1)} all-to-all(bf16[4,640,128]{2,1,0:T(8,128)(2,1)S(1)} %interfaces.1), channel_id=1, replica_groups={{0,16,32,48},{64,80,96,112},{128,144,160,176},{192,208,224,240},{1,17,3..., dimensions={0} | all-to-all | bytes 1310720 | tf_op jit(solution)/shard_map/all_to_all | solution.py:518
  114.9 4.4 %outer_pencils.1 = (bf16[2,320,128]{2,1,0:T(8,128)(2,1)S(1)}, bf16[2,320,128]{2,1,0:T(8,128)(2,1)S(1)}) custom-call(s32[2,4]{1,0:T(2,128)S(1)} %copy-done, s32[5]{0:T(128)S(1)} %stack.19.place, bf16[4,640,128]{2,1,0:T(8,128)(2,1)S(1)} %all_to_all.5.ends.refs_14_, bf16[8,320,320]{2,1,0:T(8,128)(2,1)} %bitcast.61, bf16[8,320,320]{2,1,0:T(8,128)(2,1)} %bitcast.62, ...), custom_call_target="tpu_custom_call" | custom-call | tf_op jit(solution)/shard_map/outer_pencils/pallas_call | solution.py:85
  119.4 4.5 %inner_pencils.1 = (bf16[2,320,128]{2,1,0:T(8,128)(2,1)S(1)}, bf16[2,320,128]{2,1,0:T(8,128)(2,1)S(1)}, bf16[4,320,128]{2,1,0:T(8,128)(2,1)S(1)}) custom-call(s32[2,4]{1,0:T(2,128)S(1)} %copy-done, s32[5]{0:T(128)S(1)} %stack.19.place, bf16[4,640,128]{2,1,0:T(8,128)(2,1)S(1)} %all_to_all.5.ends.refs_14_, bf16[8,320,320]{2,1,0:T(8,128)(2,1)} %bitcast.65, ...), custom_call_target="tpu_custom_call" | custom-call | tf_op jit(solution)/shard_map/inner_pencils/pallas_call | solution.py:85
  125.3 7.5 %inner_jacobian.1 = (bf16[8,320,128]{2,1,0:T(8,128)(2,1)}, f32[4,2,320,128]{3,2,1,0:T(8,128)S(1)}) custom-call(s32[2,4]{1,0:T(2,128)S(1)} %copy-done, bf16[8,320,320]{2,1,0:T(8,128)(2,1)} %bitcast.93, bf16[8,320,320]{2,1,0:T(8,128)(2,1)} %bitcast.29, bf16[8,320,320]{2,1,0:T(8,128)(2,1)} %bitcast.51, bf16[8,320,320]{2,1,0:T(8,128)(2,1)} %bitcast.85, ...), custom_call_target="tpu_custom_call" | custom-call | tf_op jit(solution)/shard_map/inner_jacobian/pallas_call | solution.py:402
  132.8 3.5 %collective-permute-done.8.refs_9_ = bf16[4,320,128]{2,1,0:T(8,128)(2,1)S(1)} collective-permute-done((bf16[4,320,128]{2,1,0:T(8,128)(2,1)S(1)}, bf16[4,320,128]{2,1,0:T(8,128)(2,1)S(1)}, u32[]{:S(2)}, u32[]{:S(2)}) %collective-permute-start.8) | collective-permute-done | bytes 327712 | tf_op jit(solution)/shard_map/ppermute | solution.py:531
  136.3 3.7 %edge_jacobian.1 = bf16[8,320,128]{2,1,0:T(8,128)(2,1)} custom-call(s32[2,4]{1,0:T(2,128)S(1)} %copy-done, s32[5]{0:T(128)S(1)} %stack.19.place, bf16[8,320,320]{2,1,0:T(8,128)(2,1)} %bitcast.31, bf16[8,320,320]{2,1,0:T(8,128)(2,1)} %bitcast.32, bf16[8,320,320]{2,1,0:T(8,128)(2,1)} %bitcast.33, bf16[8,320,320]{2,1,0:T(8,128)(2,1)} %bitcast.34, ...), custom_call_target="tpu_custom_call" | custom-call | tf_op jit(solution)/shard_map/edge_jacobian/pallas_call | solution.py:451
  (16 shorter events, 9.7 us)
Async XLA Ops:
  0.7 0.7 copy-start
  5.0 20.7 %collective-permute-start = (bf16[3040,128]{1,0:T(8,128)(2,1)S(1)}, bf16[3040,128]{1,0:T(8,128)(2,1)S(1)}, u32[]{:S(2)}, u32[]{:S(2)}) collective-permute-start(bf16[3040,128]{1,0:T(8,128)(2,1)S(1)} %local_map.5), channel_id=1, source_target_pairs={{0,16},{16,0},{32,48},{48,32},{64,80},{80,64},{96,112},{112,96},{1... | collective-permute-start | bytes 2334728 | tf_op jit(solution)/shard_map/ppermute | solution.py:494
  11.0 20.4 %collective-permute-start.1 = (bf16[3040,128]{1,0:T(8,128)(2,1)S(1)}, bf16[3040,128]{1,0:T(8,128)(2,1)S(1)}, u32[]{:S(2)}, u32[]{:S(2)}) collective-permute-start(bf16[3040,128]{1,0:T(8,128)(2,1)S(1)} %local_map.6), channel_id=1, source_target_pairs={{0,32},{16,48},{32,0},{48,16},{64,96},{80,112},{96,64},{112,80},{1... | collective-permute-start | bytes 2334728 | tf_op jit(solution)/shard_map/ppermute | solution.py:494
  16.7 30.8 %collective-permute-start.2 = (bf16[3040,128]{1,0:T(8,128)(2,1)S(1)}, bf16[3040,128]{1,0:T(8,128)(2,1)S(1)}, u32[]{:S(2)}, u32[]{:S(2)}) collective-permute-start(bf16[3040,128]{1,0:T(8,128)(2,1)S(1)} %local_map.7), channel_id=1, source_target_pairs={{0,48},{16,32},{32,16},{48,0},{64,112},{80,96},{96,80},{112,64},{1... | collective-permute-start | bytes 2334728 | tf_op jit(solution)/shard_map/ppermute | solution.py:494
  55.9 25.8 %collective-permute-start.5 = (bf16[1120,128]{1,0:T(8,128)(2,1)S(1)}, bf16[1120,128]{1,0:T(8,128)(2,1)S(1)}, u32[]{:S(2)}, u32[]{:S(2)}) collective-permute-start(bf16[1120,128]{1,0:T(8,128)(2,1)S(1)} %get-tuple-element.23), channel_id=1, source_target_pairs={{0,64},{16,80},{32,96},{48,112},{64,0},{80,16},{96,32},{112,48},{1... | collective-permute-start | bytes 860168 | tf_op jit(solution)/shard_map/ppermute | solution.py:491
  59.3 15.5 %collective-permute-start.3 = (bf16[320,128]{1,0:T(8,128)(2,1)S(1)}, bf16[320,128]{1,0:T(8,128)(2,1)S(1)}, u32[]{:S(2)}, u32[]{:S(2)}) collective-permute-start(bf16[320,128]{1,0:T(8,128)(2,1)S(1)} %group_front.1.after), channel_id=1, source_target_pairs={{0,64},{16,80},{32,96},{48,112},{64,0},{80,16},{96,32},{112,48},{1... | collective-permute-start | bytes 245768 | tf_op jit(solution)/shard_map/ppermute | solution.py:491
  75.0 6.7 %collective-permute-start.4 = (bf16[320,128]{1,0:T(8,128)(2,1)S(1)}, bf16[320,128]{1,0:T(8,128)(2,1)S(1)}, u32[]{:S(2)}, u32[]{:S(2)}) collective-permute-start(bf16[320,128]{1,0:T(8,128)(2,1)S(1)} %forward_one.1), channel_id=1, source_target_pairs={{0,192},{16,208},{32,224},{48,240},{64,128},{80,144},{96,160},{112... | collective-permute-start | bytes 245768 | tf_op jit(solution)/shard_map/ppermute | solution.py:491
  82.6 6.7 %collective-permute-start.6 = (bf16[320,128]{1,0:T(8,128)(2,1)S(1)}, bf16[320,128]{1,0:T(8,128)(2,1)S(1)}, u32[]{:S(2)}, u32[]{:S(2)}) collective-permute-start(bf16[320,128]{1,0:T(8,128)(2,1)S(1)} %get-tuple-element.24), channel_id=1, source_target_pairs={{0,192},{16,208},{32,224},{48,240},{64,128},{80,144},{96,160},{112... | collective-permute-start | bytes 245768 | tf_op jit(solution)/shard_map/ppermute | solution.py:491
  90.2 7.9 %collective-permute-start.7 = (bf16[320,128]{1,0:T(8,128)(2,1)S(1)}, bf16[320,128]{1,0:T(8,128)(2,1)S(1)}, u32[]{:S(2)}, u32[]{:S(2)}) collective-permute-start(bf16[320,128]{1,0:T(8,128)(2,1)S(1)} %backward_one.1), channel_id=1, source_target_pairs={{0,64},{16,80},{32,96},{48,112},{64,0},{80,16},{96,32},{112,48},{1... | collective-permute-start | bytes 245768 | tf_op jit(solution)/shard_map/ppermute | solution.py:491
  123.8 12.5 %collective-permute-start.8 = (bf16[4,320,128]{2,1,0:T(8,128)(2,1)S(1)}, bf16[4,320,128]{2,1,0:T(8,128)(2,1)S(1)}, u32[]{:S(2)}, u32[]{:S(2)}) collective-permute-start(bf16[4,320,128]{2,1,0:T(8,128)(2,1)S(1)} %get-tuple-element.33), channel_id=1, source_target_pairs={{0,16},{16,32},{32,48},{48,64},{64,80},{80,96},{96,112},{112,128},... | collective-permute-start | bytes 983048 | tf_op jit(solution)/shard_map/ppermute | solution.py:531
  124.8 8.0 %collective-permute-start.10 = (bf16[2,320,128]{2,1,0:T(8,128)(2,1)S(1)}, bf16[2,320,128]{2,1,0:T(8,128)(2,1)S(1)}, u32[]{:S(2)}, u32[]{:S(2)}) collective-permute-start(bf16[2,320,128]{2,1,0:T(8,128)(2,1)S(1)} %get-tuple-element.27.refs_16_.refs_10_), channel_id=1, source_target_pairs={{1,0},{2,1},{3,2},{4,3},{5,4},{6,5},{7,6},{8,7},{9,8},{10,9},{11,1... | collective-permute-start | bytes 491528 | tf_op jit(solution)/shard_map/ppermute | solution.py:526
  124.8 8.0 %collective-permute-start.9 = (bf16[2,320,128]{2,1,0:T(8,128)(2,1)S(1)}, bf16[2,320,128]{2,1,0:T(8,128)(2,1)S(1)}, u32[]{:S(2)}, u32[]{:S(2)}) collective-permute-start(bf16[2,320,128]{2,1,0:T(8,128)(2,1)S(1)} %get-tuple-element.28.refs_17_.refs_13_), channel_id=1, source_target_pairs={{0,1},{1,2},{2,3},{3,4},{4,5},{5,6},{6,7},{7,8},{8,9},{9,10},{10,1... | collective-permute-start | bytes 491528 | tf_op jit(solution)/shard_map/ppermute | solution.py:525

commit v4 on v3

v4 whole, which is shorter than its diff:
```python
import functools

import jax
import jax.numpy as jnp
from jax import lax
from jax.experimental import pallas as pl
from jax.experimental.pallas import tpu as pltpu
from jax.sharding import PartitionSpec as P

BF = jnp.bfloat16
F32 = jnp.float32
GROUP = 4
VMEM_LIMIT = 48 << 20
LONG = pl.CostEstimate(flops=10**10, transcendentals=0, bytes_accessed=1024)
SHORT = pl.CostEstimate(flops=1024, transcendentals=0, bytes_accessed=1024)


def mm(a, b):
    return jnp.dot(a, b, preferred_element_type=F32)


def mm_fine(a, x):
    width = x.shape[1]
    top = x.astype(BF)
    rest = (x - top.astype(F32)).astype(BF)
    both = mm(a, jnp.concatenate([top, rest], axis=1))
    return both[:, :width] + both[:, width:]


def packed_rows(n):
    return 2 * n + n // 2


def pack(ref, base, mat):
    n = mat.shape[0]
    half = n // 2
    ref[base : base + n, :] = mat[:, 0:128]
    ref[base + n : base + 2 * n, :] = mat[:, 128:256]
    ref[base + 2 * n : base + 2 * n + half, 0:64] = mat[0:half, 256:320]
    ref[base + 2 * n : base + 2 * n + half, 64:128] = mat[half:n, 256:320]


def unpack(ref, base, n):
    half = n // 2
    tail = ref[base + 2 * n : base + 2 * n + half, :]
    last = jnp.concatenate([tail[:, 0:64], tail[:, 64:128]], axis=0)
    return jnp.concatenate(
        [ref[base : base + n, :], ref[base + n : base + 2 * n, :], last], axis=1
    )


def map_rows(n):
    return 3 * packed_rows(n) + 2 * n


def local_map_kernel(slots, place, d0, d1, l0, l1, u0, u1, r0, r1, out):
    n = d0.shape[0]
    rows = packed_rows(n)
    inv0, inv1 = d0[...], d1[...]
    e0 = mm(inv0, l0[...])
    e1 = mm(inv1, l1[...]).astype(BF)
    h0 = mm(inv0, u0[...]).astype(BF)
    h1 = mm(inv1, u1[...]).astype(BF)
    y0 = mm(inv0, r0[...])
    y1 = mm(inv1, r1[...])
    a = mm(e1, e0.astype(BF)).astype(BF)
    c = y1 - mm_fine(e1, y0)
    b = mm(h0, h1).astype(BF)
    g = -(e0 + mm(h0, a))
    h = y0 - mm_fine(h0, c)
    pack(out, 0, a)
    pack(out, rows, b)
    pack(out, 2 * rows, g.astype(BF))
    out[3 * rows : 3 * rows + n, :] = c.astype(BF)
    out[3 * rows + n : 3 * rows + 2 * n, :] = h.astype(BF)


def stored(slab, pencil, height, width):
    return pl.BlockSpec(
        (None, height, width), lambda i, sl, at: (sl[slab, pencil(at)], 0, 0)
    )


def constant(shape):
    return pl.BlockSpec(shape, lambda i, sl, at: (0,) * len(shape))


def element_call(kernel, in_specs, out_shape, slots, place, *operands, name, cost=SHORT):
    return pl.pallas_call(
        kernel,
        grid_spec=pltpu.PrefetchScalarGridSpec(
            num_scalar_prefetch=2,
            grid=(1,),
            in_specs=in_specs,
            out_specs=[constant(o.shape) for o in out_shape],
        ),
        out_shape=out_shape,
        compiler_params=pltpu.CompilerParams(vmem_limit_bytes=VMEM_LIMIT),
        cost_estimate=cost,
        name=name,
    )(slots, place, *operands)


def local_map(slots, place, diag_inv, lower, upper, source, distance):
    n, cols = source.shape[1:]

    def pencil(at):
        return lax.bitwise_xor(at[3], jnp.int32(distance))

    (out,) = element_call(
        local_map_kernel,
        [stored(s, pencil, n, n) for s in (0, 1, 0, 1, 0, 1)]
        + [stored(s, pencil, n, cols) for s in (0, 1)],
        [jax.ShapeDtypeStruct((map_rows(n), cols), BF)],
        slots, place, diag_inv, diag_inv, lower, lower, upper, upper, source, source,
        name="local_map",
    )
    return out


def per_owner(place, pieces, body):
    for owned in range(GROUP):

        @pl.when(place[3] == owned)
        def _(owned=owned):
            body([pieces[owned ^ j] for j in range(GROUP)])


def group_front_kernel(place, across, near, next_one, own, send):
    n = send.shape[0]
    rows = packed_rows(n)

    def body(maps):
        front = maps[0][3 * rows : 3 * rows + n, :].astype(F32)
        for one in maps[1:]:
            shift = one[3 * rows : 3 * rows + n, :].astype(F32)
            front = mm_fine(unpack(one, 0, n), front) + shift
        send[...] = front.astype(BF)

    per_owner(place, (own, near, next_one, across), body)


def joined(left, right):
    a_l, b_l, g_l, c_l, h_l = left
    a_r, b_r, g_r, c_r, h_r = right
    a = mm(a_r, a_l).astype(BF)
    b = mm(b_l, b_r).astype(BF)
    g = (mm(b_l, mm(g_r, a_l).astype(BF)) + g_l.astype(F32)).astype(BF)
    c = mm_fine(a_r, c_l) + c_r
    h = mm_fine(b_l, mm_fine(g_r, c_l) + h_r) + h_l
    return a, b, g, c, h


def segment(one, n):
    rows = packed_rows(n)
    return (
        unpack(one, 0, n),
        unpack(one, rows, n),
        unpack(one, 2 * rows, n),
        one[3 * rows : 3 * rows + n, :].astype(F32),
        one[3 * rows + n : 3 * rows + 2 * n, :].astype(F32),
    )


def group_map_kernel(
    place, across, near, next_one, own, a_out, b_out, g_out, c_out, h_out, send_far
):
    n = a_out.shape[0]

    def body(maps):
        segments = [segment(one, n) for one in maps]
        a, b, g, c, h = joined(joined(*segments[:2]), joined(*segments[2:]))
        a_out[...] = a
        b_out[...] = b
        g_out[...] = g
        c_out[...] = c
        h_out[...] = h
        send_far[0:n, :] = h.astype(BF)
        pack(send_far, n, g)

    per_owner(place, (own, near, next_one, across), body)


def forward_one_kernel(incoming, a, c, send):
    send[...] = (mm(a[...], incoming[...]) + c[...]).astype(BF)


def turn_kernel(incoming, far, a, b, g, c, h, send, front_out, back_in):
    n = a.shape[0]
    front = incoming[...]
    ahead = mm(a[...], front) + c[...]
    back = mm_fine(unpack(far, n, n), ahead) + far[0:n, :].astype(F32)
    send[...] = (mm_fine(b[...], back) + (mm(g[...], front) + h[...])).astype(BF)
    front_out[...] = ahead.astype(BF)
    back_in[...] = back.astype(BF)


def backward_one_kernel(place, b, g, h, hop1, incoming, ahead, send):
    back = mm(b[...], incoming[...]) + (mm(g[...], hop1[...]) + h[...])
    send[...] = jnp.where(place[4] == 1, back.astype(BF), ahead[...])


def interfaces_kernel(place, across, near, next_one, own, hop1, hop2, hop3, back2, hop4, out):
    n = hop2.shape[0]
    rows = packed_rows(n)
    which = place[4]
    zero = jnp.zeros_like(hop2[...])
    first = jnp.where(
        which == 0, zero,
        jnp.where(which == 1, hop1[...], jnp.where(which == 2, hop2[...], hop4[...])),
    ).astype(F32)
    last = jnp.where(
        which == 0, hop4[...],
        jnp.where(which == 1, hop3[...], jnp.where(which == 2, back2[...], zero)),
    ).astype(F32)

    def body(maps):
        fronts, back = [first], last
        for one in maps[:-1]:
            shift = one[3 * rows : 3 * rows + n, :].astype(F32)
            fronts.append(mm_fine(unpack(one, 0, n), fronts[-1]) + shift)
        for j in reversed(range(GROUP)):
            out[j, 0:n, :] = fronts[j].astype(BF)
            out[j, n : 2 * n, :] = back.astype(BF)
            if j:
                shift = maps[j][3 * rows + n : 3 * rows + 2 * n, :].astype(F32)
                inner = mm_fine(unpack(maps[j], 2 * rows, n), fronts[j]) + shift
                back = mm_fine(unpack(maps[j], rows, n), back) + inner

    per_owner(place, (own, near, next_one, across), body)


def whole_call(kernel, outs, scalars, *operands, name, cost=SHORT):
    specs = [pl.BlockSpec(memory_space=pltpu.SMEM)] * len(scalars)
    specs += [pl.BlockSpec(memory_space=pltpu.VMEM)] * len(operands)
    return pl.pallas_call(
        kernel,
        in_specs=specs,
        out_specs=[pl.BlockSpec(memory_space=pltpu.VMEM)] * len(outs),
        out_shape=[jax.ShapeDtypeStruct(s, d) for s, d in outs],
        compiler_params=pltpu.CompilerParams(vmem_limit_bytes=VMEM_LIMIT),
        cost_estimate=cost,
        name=name,
    )(*scalars, *operands)


def solve_pencils(ends, columns):
    n = ends[0].shape[0] // 2
    fronts = [e[0:n, :] for e in ends]
    backs = [e[n : 2 * n, :] for e in ends]
    both = range(len(ends))
    d0, d1, l0, l1, u0, u1, r0, r1 = zip(*columns)
    v = [mm(u1[i][...], backs[i]) for i in both]
    q = [r0[i][...].astype(F32) - mm(l0[i][...], fronts[i]) for i in both]
    f0 = [mm_fine(d0[i][...], q[i]) for i in both]
    v = [mm_fine(d1[i][...], v[i]) for i in both]
    q = [r1[i][...].astype(F32) - mm_fine(l1[i][...], f0[i]) for i in both]
    x1 = [mm_fine(d1[i][...], q[i]) - v[i] for i in both]
    q = [mm_fine(u0[i][...], x1[i]) for i in both]
    x0 = [f0[i] - mm_fine(d0[i][...], q[i]) for i in both]
    return [(x0[i].astype(BF), x1[i].astype(BF)) for i in both]


def two_pencils_kernel(chosen, slots, place, ends, *refs):
    outs, tops = refs[16:18], refs[18]
    solved = solve_pencils([ends[p] for p in chosen], [refs[0:8], refs[8:16]])
    for i, ((x0, x1), out) in enumerate(zip(solved, outs)):
        out[0] = x0
        out[1] = x1
        tops[i] = x1


def two_pencils(chosen, slots, place, ends, diag_inv, lower, upper, source):
    n, cols = source.shape[1:]
    specs, operands = [constant(ends.shape)], [ends]
    for p in chosen:
        for array in (diag_inv, lower, upper, source):
            for s in range(2):
                specs.append(stored(s, lambda at, p=p: p, n, array.shape[-1]))
                operands.append(array)
    return element_call(
        functools.partial(two_pencils_kernel, chosen), specs,
        [jax.ShapeDtypeStruct((2, n, cols), BF)] * 3, slots, place, *operands, name="two_pencils",
        cost=LONG if 0 in chosen else SHORT,
    )


def inner_jacobian_kernel(slots, *refs):
    blocks, (first, second, third, last, ends) = refs[0:10], refs[10:15]
    precond, partial, lowers, sides, vals = refs[15:]
    n = first.shape[1]
    pencil = pl.program_id(0)

    @pl.when(pencil == 0)
    def _():
        zero = jnp.zeros(first.shape[1:], BF)
        for p, values in enumerate((first, second, third, last)):
            vals[0, p + 1] = zero
            vals[1, p + 1] = values[0]
            vals[2, p + 1] = values[1]
            vals[3, p + 1] = ends[p, n : 2 * n, :]
        for s in range(2):
            vals[s + 1, 0] = zero
            vals[s + 1, GROUP + 1] = zero

    both = range(2)
    near = [
        [
            vals[s + 1, pencil + 1], vals[s, pencil + 1], vals[s + 2, pencil + 1],
            vals[s + 1, pencil], vals[s + 1, pencil + 2],
        ]
        for s in both
    ]
    totals = [mm(blocks[5 * s][...], near[s][0]) for s in both]
    for t in range(1, 5):
        totals = [totals[s] + mm(blocks[5 * s + t][...], near[s][t]) for s in both]
    for s in both:
        precond[slots[s, pencil]] = near[s][0]
        partial[s] = totals[s]
    lowers[...] = blocks[1][...]

    @pl.when(pencil == 0)
    def _():
        for s in both:
            sides[s] = blocks[5 * s + 3][...]

    @pl.when(pencil == GROUP - 1)
    def _():
        for s in both:
            sides[s + 2] = blocks[5 * s + 4][...]


def inner_jacobian(slots, blocks, vectors):
    n, cols = vectors[0].shape[1:]

    def whole(shape):
        return pl.BlockSpec(shape, lambda p, sl: (0, 0, 0))

    specs = [
        pl.BlockSpec((None, n, n), lambda p, sl, s=s: (sl[s, p], 0, 0))
        for s in range(2)
        for _ in blocks
    ]
    stored_shape = (2 * GROUP, n, cols)
    return pl.pallas_call(
        inner_jacobian_kernel,
        grid_spec=pltpu.PrefetchScalarGridSpec(
            num_scalar_prefetch=1,
            grid=(GROUP,),
            in_specs=specs + [whole(v.shape) for v in vectors],
            out_specs=[
                whole(stored_shape),
                pl.BlockSpec((None, 2, n, cols), lambda p, sl: (p, 0, 0, 0)),
                pl.BlockSpec((None, n, n), lambda p, sl: (p, 0, 0)),
                whole((4, n, n)),
            ],
            scratch_shapes=[pltpu.VMEM((4, GROUP + 2, n, cols), BF)],
        ),
        out_shape=[
            jax.ShapeDtypeStruct(stored_shape, BF),
            jax.ShapeDtypeStruct((GROUP, 2, n, cols), F32),
            jax.ShapeDtypeStruct((GROUP, n, n), BF),
            jax.ShapeDtypeStruct((4, n, n), BF),
        ],
        compiler_params=pltpu.CompilerParams(vmem_limit_bytes=VMEM_LIMIT),
        cost_estimate=SHORT,
        name="inner_jacobian",
    )(slots, *blocks, *blocks, *vectors)


def edge_jacobian_kernel(slots, place, low, high, below_outer, below_inner, partial, lowers, sides, jac):
    below = (below_outer.at[0], below_inner.at[0], below_inner.at[1], below_outer.at[1])
    left = jnp.where(place[1] == 0, 0.0, 1.0).astype(F32)
    right = jnp.where(place[1] == place[2] - 1, 0.0, 1.0).astype(F32)
    start = jnp.where(place[0] == 0, 0.0, 1.0).astype(F32)
    for s in range(2):
        for p in range(GROUP):
            total = partial[p, s]
            if s == 0:
                total = total + start * mm(lowers[p], below[p][...])
            if p == 0:
                total = total + left * mm(sides[s], low[s])
            if p == GROUP - 1:
                total = total + right * mm(sides[s + 2], high[s])
            jac[slots[s, p]] = total.astype(BF)


def local(right_side, diag_inv, diag_blk, lower_blk, upper_blk, cross_minus, cross_plus, elem_slot):
    n, cols = right_side.shape[2:]
    source, inverse, diagonal, lower, upper, minus, plus = (
        pltpu.with_memory_space_constraint(
            values.reshape((-1,) + values.shape[2:]), pltpu.HBM
        )
        for values in (
            right_side, diag_inv, diag_blk, lower_blk, upper_blk, cross_minus, cross_plus
        )
    )
    count = lax.axis_size("sweep")
    across = lax.axis_size("cross")
    sweep_at = lax.axis_index("sweep")
    place = jnp.stack(
        [
            sweep_at, lax.axis_index("cross"), jnp.int32(across),
            lax.rem(sweep_at, GROUP), lax.div(sweep_at, GROUP),
        ]
    ).astype(jnp.int32)
    groups = [list(range(g, g + GROUP)) for g in range(0, count, GROUP)]

    def swap(values, order):
        pairs = [(g * GROUP + k, order[g] * GROUP + k) for g in range(GROUP) for k in range(GROUP)]
        return lax.ppermute(values, "sweep", pairs)

    def to_peer(values, distance):
        return lax.ppermute(values, "sweep", [(i, i ^ distance) for i in range(count)])

    low_pair, high_pair, outer, inner = (1, 0, 2, 3), (0, 1, 3, 2), (1, 0, 3, 2), (0, 2, 1, 3)
    vec = ((n, cols), BF)
    maps = [None] * GROUP
    for distance in (3, 1, 2, 0):
        piece = local_map(elem_slot, place, inverse, lower, upper, source, distance)
        maps[distance] = to_peer(piece, distance) if distance else piece
    pieces = (maps[3], maps[1], maps[2], maps[0])

    (send,) = whole_call(group_front_kernel, [vec], [place], *pieces, name="group_front")
    hop1 = swap(send, low_pair)
    a, b, g, c, h, send_far = whole_call(
        group_map_kernel,
        [
            ((n, n), BF), ((n, n), BF), ((n, n), BF), ((n, cols), F32), ((n, cols), F32),
            ((n + packed_rows(n), cols), BF),
        ],
        [place], *pieces, name="group_map",
    )
    far = swap(send_far, high_pair)
    (send,) = whole_call(forward_one_kernel, [vec], [], hop1, a, c, name="forward_one", cost=LONG)
    hop2 = swap(send, inner)
    send, ahead, back2 = whole_call(
        turn_kernel, [vec, vec, vec], [], hop2, far, a, b, g, c, h, name="turn"
    )
    hop3 = swap(send, inner)
    (send,) = whole_call(
        backward_one_kernel, [vec], [place], b, g, h, hop1, hop3, ahead, name="backward_one"
    )
    hop4 = swap(send, outer)
    (ends,) = whole_call(
        interfaces_kernel, [((GROUP, 2 * n, cols), BF)], [place],
        *pieces, hop1, hop2, hop3, back2, hop4, name="interfaces",
    )
    ends = lax.all_to_all(ends, "sweep", 0, 0, axis_index_groups=groups)

    def solved(*chosen):
        return two_pencils(chosen, elem_slot, place, ends, inverse, lower, upper, source)

    def up(values):
        return lax.ppermute(values, "sweep", [(i, (i + 1) % count) for i in range(count)])

    first, last, tops = solved(0, GROUP - 1)
    low = lax.ppermute(last, "cross", [(i, (i + 1) % across) for i in range(across)])
    high = lax.ppermute(first, "cross", [((i + 1) % across, i) for i in range(across)])
    below_outer = up(tops)
    second, third, tops = solved(1, 2)
    below_inner = up(tops)
    precond, partial, lowers, sides = inner_jacobian(
        elem_slot, (diagonal, lower, upper, minus, plus), (first, second, third, last, ends)
    )
    (jac,) = whole_call(
        edge_jacobian_kernel, [((2 * GROUP, n, cols), BF)], [elem_slot, place],
        low, high, below_outer, below_inner, partial, lowers, sides, name="edge_jacobian",
    )
    return precond.reshape(right_side.shape), jac.reshape(right_side.shape)


def solution(mesh):
    blocks = P("sweep", "cross", None, None)
    in_specs = (blocks,) * 7 + (P("sweep", "cross"),)
    return jax.shard_map(
        local, mesh=mesh, in_specs=in_specs, out_specs=(blocks, blocks), check_vma=False
    )
```

time: 140 us -> 128 us (0.914)
  waiting for transfers between devices: 55.4 us -> 24.6 us
  starting transfers between devices: 21.5 us -> 43.7 us
  Pallas kernels: 48.5 us -> 43 us
    ppermute x5, waiting for transfers between devices: 25.6 us -> 2.43 us  [swap(): return lax.ppermute(values, 'sweep', pairs)]
    ppermute x5, starting transfers between devices: 14.7 us -> 30.6 us  [swap(): return lax.ppermute(values, 'sweep', pairs)]
    pallas_call x4 -> x0, Pallas kernels: 15.8 us -> none  [the longest x1 5.54 us: group_map(): pl.pallas_call(group_map_kernel, in_specs=[pl.BlockSpec(memory_space=pltp...]
    pallas_call x3 -> x7, Pallas kernels: 1.85 us -> 11.8 us  [whole_call(): pl.pallas_call(kernel, in_specs=specs, out_specs=[pl.BlockSpec(memory_spa...]
    ppermute x3, waiting for transfers between devices: 26.3 us -> 22.1 us  [to_peer(): lax.ppermute(values, 'sweep', [(i, i ^ distance) for i in range(count)])]
    ppermute x1, starting transfers between devices: 0.01 us -> 3.85 us  [local(): lax.ppermute(first, 'cross', [((i + 1) % across, i) for i in range(across)])]
    ppermute x1 -> x2, waiting for transfers between devices: 3.51 us -> 0.01 us  [up(): lax.ppermute(values, 'sweep', [(i, (i + 1) % count) for i in range(count)])]
    ppermute x1 -> x2, starting transfers between devices: 0.99 us -> 4.03 us  [up(): lax.ppermute(values, 'sweep', [(i, (i + 1) % count) for i in range(count)])]
  transfers between devices with their start and end apart: 11 -> 12, of which waited for: 8 -> 3; matrix products, arithmetic and copies ran while one was open for 0% -> 0% of each run, Pallas kernels for 13% -> 22%
where the time goes in v4:
time: 128 us; the launch traced here: 127 us
  starting transfers between devices  43.7 us (34%)
  Pallas kernels  43 us (34%)
  waiting for transfers between devices  24.6 us (19%)
  blocking collectives  13.9 us (11%)
    ppermute x5, starting transfers between devices, swap(): return lax.ppermute(values, 'sweep', pairs)  30.6 us
    pallas_call x6, Pallas kernels, element_call(): pl.pallas_call(kernel, grid_spec=pltpu.PrefetchScalarGridSpec(num_scalar_...  23.3 us
    ppermute x3, waiting for transfers between devices, to_peer(): lax.ppermute(values, 'sweep', [(i, i ^ distance) for i in range(count)])  22.1 us
    all_to_all x1, blocking collectives, local(): ends = lax.all_to_all(ends, 'sweep', 0, 0, axis_index_groups=groups)  13.9 us
    pallas_call x7, Pallas kernels, whole_call(): pl.pallas_call(kernel, in_specs=specs, out_specs=[pl.BlockSpec(memory_spa...  11.8 us
    pallas_call x1, Pallas kernels, inner_jacobian(): pl.pallas_call(inner_jacobian_kernel, grid_spec=pltpu.PrefetchScalarGridS...  7.89 us
    ppermute x3, starting transfers between devices, to_peer(): lax.ppermute(values, 'sweep', [(i, i ^ distance) for i in range(count)])  5.26 us
    ppermute x2, starting transfers between devices, up(): lax.ppermute(values, 'sweep', [(i, (i + 1) % count) for i in range(count)])  4.03 us
  transfers between devices with their start and end apart: 12, of which 3 were waited for; matrix products, arithmetic and copies ran while one was open for 0% of the time, Pallas kernels for 22%

profile of v4, /device:TPU:8, one launch (start us, length us, event | category | flops | bytes accessed | tf_op | source)
XLA Modules:
  0.0 126.8 jit_solution(5126707813037650340)
XLA Ops:
  1.4 3.6 %local_map.4 = bf16[3040,128]{1,0:T(8,128)(2,1)S(1)} custom-call(s32[2,4]{1,0:T(2,128)S(1)} %copy-done, s32[5]{0:T(128)S(1)} %stack.19.place, bf16[8,320,320]{2,1,0:T(8,128)(2,1)} %bitcast.49, bf16[8,320,320]{2,1,0:T(8,128)(2,1)} %bitcast.50, bf16[8,320,320]{2,1,0:T(8,128)(2,1)} %bitcast.13, bf16[8,320,320]{2,1,0:T(8,128)(2,1)} %bitcast.14, ...), custom_call_target="tpu_custom_call" | custom-call | flops 1024 | bytes 1024 | tf_op jit(solution)/shard_map/local_map/pallas_call | solution.py:89
  5.0 3.7 %collective-permute-start = (bf16[3040,128]{1,0:T(8,128)(2,1)S(1)}, bf16[3040,128]{1,0:T(8,128)(2,1)S(1)}, u32[]{:S(2)}, u32[]{:S(2)}) collective-permute-start(bf16[3040,128]{1,0:T(8,128)(2,1)S(1)} %local_map.4), channel_id=1, source_target_pairs={{0,48},{16,32},{32,16},{48,0},{64,112},{80,96},{96,80},{112,64},{1... | collective-permute-start | bytes 2334728 | tf_op jit(solution)/shard_map/ppermute | solution.py:414
  8.8 3.6 %local_map.5 = bf16[3040,128]{1,0:T(8,128)(2,1)S(1)} custom-call(s32[2,4]{1,0:T(2,128)S(1)} %copy-done, s32[5]{0:T(128)S(1)} %stack.19.place, bf16[8,320,320]{2,1,0:T(8,128)(2,1)} %bitcast.51, bf16[8,320,320]{2,1,0:T(8,128)(2,1)} %bitcast.52, bf16[8,320,320]{2,1,0:T(8,128)(2,1)} %bitcast.15, bf16[8,320,320]{2,1,0:T(8,128)(2,1)} %bitcast.16, ...), custom_call_target="tpu_custom_call" | custom-call | flops 1024 | bytes 1024 | tf_op jit(solution)/shard_map/local_map/pallas_call | solution.py:89
  12.4 1.3 %collective-permute-start.1 = (bf16[3040,128]{1,0:T(8,128)(2,1)S(1)}, bf16[3040,128]{1,0:T(8,128)(2,1)S(1)}, u32[]{:S(2)}, u32[]{:S(2)}) collective-permute-start(bf16[3040,128]{1,0:T(8,128)(2,1)S(1)} %local_map.5), channel_id=1, source_target_pairs={{0,16},{16,0},{32,48},{48,32},{64,80},{80,64},{96,112},{112,96},{1... | collective-permute-start | bytes 2334728 | tf_op jit(solution)/shard_map/ppermute | solution.py:414
  13.7 3.6 %local_map.6 = bf16[3040,128]{1,0:T(8,128)(2,1)S(1)} custom-call(s32[2,4]{1,0:T(2,128)S(1)} %copy-done, s32[5]{0:T(128)S(1)} %stack.19.place, bf16[8,320,320]{2,1,0:T(8,128)(2,1)} %bitcast.53, bf16[8,320,320]{2,1,0:T(8,128)(2,1)} %bitcast.54, bf16[8,320,320]{2,1,0:T(8,128)(2,1)} %bitcast.17, bf16[8,320,320]{2,1,0:T(8,128)(2,1)} %bitcast.18, ...), custom_call_target="tpu_custom_call" | custom-call | flops 1024 | bytes 1024 | tf_op jit(solution)/shard_map/local_map/pallas_call | solution.py:89
  17.6 3.6 %local_map.7.own = bf16[3040,128]{1,0:T(8,128)(2,1)S(1)} custom-call(s32[2,4]{1,0:T(2,128)S(1)} %copy-done, s32[5]{0:T(128)S(1)} %stack.19.place, bf16[8,320,320]{2,1,0:T(8,128)(2,1)} %bitcast.55, bf16[8,320,320]{2,1,0:T(8,128)(2,1)} %bitcast.56, bf16[8,320,320]{2,1,0:T(8,128)(2,1)} %bitcast.19, bf16[8,320,320]{2,1,0:T(8,128)(2,1)} %bitcast.20, ...), custom_call_target="tpu_custom_call" | custom-call | flops 1024 | bytes 1024 | tf_op jit(solution)/shard_map/local_map/pallas_call | solution.py:89
  21.2 6.6 %collective-permute-done.across = bf16[3040,128]{1,0:T(8,128)(2,1)S(1)} collective-permute-done((bf16[3040,128]{1,0:T(8,128)(2,1)S(1)}, bf16[3040,128]{1,0:T(8,128)(2,1)S(1)}, u32[]{:S(2)}, u32[]{:S(2)}) %collective-permute-start) | collective-permute-done | bytes 778272 | tf_op jit(solution)/shard_map/ppermute | solution.py:414
  27.8 15.5 %collective-permute-done.1.near = bf16[3040,128]{1,0:T(8,128)(2,1)S(1)} collective-permute-done((bf16[3040,128]{1,0:T(8,128)(2,1)S(1)}, bf16[3040,128]{1,0:T(8,128)(2,1)S(1)}, u32[]{:S(2)}, u32[]{:S(2)}) %collective-permute-start.1) | collective-permute-done | bytes 778272 | tf_op jit(solution)/shard_map/ppermute | solution.py:414
  43.3 1.4 %group_front.1 = bf16[320,128]{1,0:T(8,128)(2,1)S(1)} custom-call(s32[5]{0:T(128)S(1)} %stack.19.place, bf16[3040,128]{1,0:T(8,128)(2,1)S(1)} %collective-permute-done.across, bf16[3040,128]{1,0:T(8,128)(2,1)S(1)} %collective-permute-done.1.near, bf16[3040,128]{1,0:T(8,128)(2,1)S(1)} %collective-permute-done.2.next_one, bf16[3040,128]{1,0:T(8,128)(2,1)S(1)} %local_map.7.own), custom_call_target="tpu_custom_call" | custom-call | flops 1024 | bytes 1024 | tf_op jit(solution)/shard_map/group_front/pallas_call | solution.py:236
  44.7 5.2 %collective-permute-start.3 = (bf16[320,128]{1,0:T(8,128)(2,1)S(1)}, bf16[320,128]{1,0:T(8,128)(2,1)S(1)}, u32[]{:S(2)}, u32[]{:S(2)}) collective-permute-start(bf16[320,128]{1,0:T(8,128)(2,1)S(1)} %group_front.1), channel_id=1, source_target_pairs={{0,64},{16,80},{32,96},{48,112},{64,0},{80,16},{96,32},{112,48},{1... | collective-permute-start | bytes 245768 | tf_op jit(solution)/shard_map/ppermute | solution.py:411
  49.9 4.2 %group_map.1 = (bf16[320,320]{1,0:T(8,128)(2,1)S(1)}, bf16[320,320]{1,0:T(8,128)(2,1)S(1)}, bf16[320,320]{1,0:T(8,128)(2,1)S(1)}, f32[320,128]{1,0:T(8,128)S(1)}...) custom-call(s32[5]{0:T(128)S(1)} %stack.19.place, bf16[3040,128]{1,0:T(8,128)(2,1)S(1)} %collective-permute-done.across, ...), custom_call_target="tpu_custom_call" | custom-call | flops 1024 | bytes 1024 | tf_op jit(solution)/shard_map/group_map/pallas_call | solution.py:236
  55.0 0.9 collective-permute-start.4
  57.5 0.8 backward_one.1
  58.3 23.2 %collective-permute-start.7 = (bf16[320,128]{1,0:T(8,128)(2,1)S(1)}, bf16[320,128]{1,0:T(8,128)(2,1)S(1)}, u32[]{:S(2)}, u32[]{:S(2)}) collective-permute-start(bf16[320,128]{1,0:T(8,128)(2,1)S(1)} %backward_one.1), channel_id=1, source_target_pairs={{0,64},{16,80},{32,96},{48,112},{64,0},{80,16},{96,32},{112,48},{1... | collective-permute-start | bytes 245768 | tf_op jit(solution)/shard_map/ppermute | solution.py:411
  81.5 2.4 %collective-permute-done.7.hop4 = bf16[320,128]{1,0:T(8,128)(2,1)S(1)} collective-permute-done((bf16[320,128]{1,0:T(8,128)(2,1)S(1)}, bf16[320,128]{1,0:T(8,128)(2,1)S(1)}, u32[]{:S(2)}, u32[]{:S(2)}) %collective-permute-start.7) | collective-permute-done | bytes 81952 | tf_op jit(solution)/shard_map/ppermute | solution.py:411
  83.9 2.3 %interfaces.1 = bf16[4,640,128]{2,1,0:T(8,128)(2,1)S(1)} custom-call(s32[5]{0:T(128)S(1)} %stack.19.place, bf16[3040,128]{1,0:T(8,128)(2,1)S(1)} %collective-permute-done.across, bf16[3040,128]{1,0:T(8,128)(2,1)S(1)} %collective-permute-done.1.near, bf16[3040,128]{1,0:T(8,128)(2,1)S(1)} %collective-permute-done.2.next_one, ...), custom_call_target="tpu_custom_call" | custom-call | flops 1024 | bytes 1024 | tf_op jit(solution)/shard_map/interfaces/pallas_call | solution.py:236
  86.2 13.9 %all_to_all.5.ends.refs_14_ = bf16[4,640,128]{2,1,0:T(8,128)(2,1)S(1)} all-to-all(bf16[4,640,128]{2,1,0:T(8,128)(2,1)S(1)} %interfaces.1), channel_id=1, replica_groups={{0,16,32,48},{64,80,96,112},{128,144,160,176},{192,208,224,240},{1,17,3..., dimensions={0} | all-to-all | bytes 1310720 | tf_op jit(solution)/shard_map/all_to_all | solution.py:449
  100.0 4.4 %two_pencils.3 = (bf16[2,320,128]{2,1,0:T(8,128)(2,1)S(1)}, bf16[2,320,128]{2,1,0:T(8,128)(2,1)S(1)}, bf16[2,320,128]{2,1,0:T(8,128)(2,1)S(1)}) custom-call(s32[2,4]{1,0:T(2,128)S(1)} %copy-done, s32[5]{0:T(128)S(1)} %stack.19.place, bf16[4,640,128]{2,1,0:T(8,128)(2,1)S(1)} %all_to_all.5.ends.refs_14_, bf16[8,320,320]{2,1,0:T(8,128)(2,1)} %bitcast.57, ...), custom_call_target="tpu_custom_call" | custom-call | flops 1024 | bytes 1024 | tf_op jit(solution)/shard_map/two_pencils/pallas_call | solution.py:89
  104.5 1.0 collective-permute-start.11
  105.5 4.4 %two_pencils.2 = (bf16[2,320,128]{2,1,0:T(8,128)(2,1)S(1)}, bf16[2,320,128]{2,1,0:T(8,128)(2,1)S(1)}, bf16[2,320,128]{2,1,0:T(8,128)(2,1)S(1)}) custom-call(s32[2,4]{1,0:T(2,128)S(1)} %copy-done, s32[5]{0:T(128)S(1)} %stack.19.place, bf16[4,640,128]{2,1,0:T(8,128)(2,1)S(1)} %all_to_all.5.ends.refs_14_, bf16[8,320,320]{2,1,0:T(8,128)(2,1)} %bitcast.61, ...), custom_call_target="tpu_custom_call" | custom-call | flops 10000000000 | bytes 1024 | tf_op jit(solution)/shard_map/two_pencils/pallas_call | solution.py:89
  109.9 3.0 %collective-permute-start.10 = (bf16[2,320,128]{2,1,0:T(8,128)(2,1)S(1)}, bf16[2,320,128]{2,1,0:T(8,128)(2,1)S(1)}, u32[]{:S(2)}, u32[]{:S(2)}) collective-permute-start(bf16[2,320,128]{2,1,0:T(8,128)(2,1)S(1)} %get-tuple-element.35), channel_id=1, source_target_pairs={{0,16},{16,32},{32,48},{48,64},{64,80},{80,96},{96,112},{112,128},... | collective-permute-start | bytes 491528 | tf_op jit(solution)/shard_map/ppermute | solution.py:455
  112.9 3.9 %collective-permute-start.9 = (bf16[2,320,128]{2,1,0:T(8,128)(2,1)S(1)}, bf16[2,320,128]{2,1,0:T(8,128)(2,1)S(1)}, u32[]{:S(2)}, u32[]{:S(2)}) collective-permute-start(bf16[2,320,128]{2,1,0:T(8,128)(2,1)S(1)} %get-tuple-element.30.refs_10_), channel_id=1, source_target_pairs={{1,0},{2,1},{3,2},{4,3},{5,4},{6,5},{7,6},{8,7},{9,8},{10,9},{11,1... | collective-permute-start | bytes 491528 | tf_op jit(solution)/shard_map/ppermute | solution.py:459
  116.8 7.9 %inner_jacobian.1 = (bf16[8,320,128]{2,1,0:T(8,128)(2,1)}, f32[4,2,320,128]{3,2,1,0:T(8,128)S(1)}, bf16[4,320,320]{2,1,0:T(8,128)(2,1)S(1)}, bf16[4,320,320]{2,1,0:T(8,128)(2,1)S(1)}) custom-call(s32[2,4]{1,0:T(2,128)S(1)} %copy-done, bf16[8,320,320]{2,1,0:T(8,128)(2,1)} %bitcast.81, bf16[8,320,320]{2,1,0:T(8,128)(2,1)} %bitcast.29, ...), custom_call_target="tpu_custom_call" | custom-call | flops 1024 | bytes 1024 | tf_op jit(solution)/shard_map/inner_jacobian/pallas_call | solution.py:345
  124.7 2.1 %edge_jacobian.1 = bf16[8,320,128]{2,1,0:T(8,128)(2,1)} custom-call(s32[2,4]{1,0:T(2,128)S(1)} %copy-done, s32[5]{0:T(128)S(1)} %stack.19.place, bf16[2,320,128]{2,1,0:T(8,128)(2,1)S(1)} %collective-permute-done.8.low, bf16[2,320,128]{2,1,0:T(8,128)(2,1)S(1)} %collective-permute-done.9.high, bf16[2,320,128]{2,1,0:T(8,128)(2,1)S(1)} %collective-permute-done.10.below_outer, ...), custom_call_target="tpu_custom_call" | custom-call | flops 1024 | bytes 1024 | tf_op jit(solution)/shard_map/edge_jacobian/pallas_call | solution.py:236
  (18 shorter events, 3.4 us)
Async XLA Ops:
  0.7 0.7 copy-start
  5.0 22.8 %collective-permute-start = (bf16[3040,128]{1,0:T(8,128)(2,1)S(1)}, bf16[3040,128]{1,0:T(8,128)(2,1)S(1)}, u32[]{:S(2)}, u32[]{:S(2)}) collective-permute-start(bf16[3040,128]{1,0:T(8,128)(2,1)S(1)} %local_map.4), channel_id=1, source_target_pairs={{0,48},{16,32},{32,16},{48,0},{64,112},{80,96},{96,80},{112,64},{1... | collective-permute-start | bytes 2334728 | tf_op jit(solution)/shard_map/ppermute | solution.py:414
  12.4 30.9 %collective-permute-start.1 = (bf16[3040,128]{1,0:T(8,128)(2,1)S(1)}, bf16[3040,128]{1,0:T(8,128)(2,1)S(1)}, u32[]{:S(2)}, u32[]{:S(2)}) collective-permute-start(bf16[3040,128]{1,0:T(8,128)(2,1)S(1)} %local_map.5), channel_id=1, source_target_pairs={{0,16},{16,0},{32,48},{48,32},{64,80},{80,64},{96,112},{112,96},{1... | collective-permute-start | bytes 2334728 | tf_op jit(solution)/shard_map/ppermute | solution.py:414
  17.3 26.0 %collective-permute-start.2 = (bf16[3040,128]{1,0:T(8,128)(2,1)S(1)}, bf16[3040,128]{1,0:T(8,128)(2,1)S(1)}, u32[]{:S(2)}, u32[]{:S(2)}) collective-permute-start(bf16[3040,128]{1,0:T(8,128)(2,1)S(1)} %local_map.6), channel_id=1, source_target_pairs={{0,32},{16,48},{32,0},{48,16},{64,96},{80,112},{96,64},{112,80},{1... | collective-permute-start | bytes 2334728 | tf_op jit(solution)/shard_map/ppermute | solution.py:414
  44.7 10.1 %collective-permute-start.3 = (bf16[320,128]{1,0:T(8,128)(2,1)S(1)}, bf16[320,128]{1,0:T(8,128)(2,1)S(1)}, u32[]{:S(2)}, u32[]{:S(2)}) collective-permute-start(bf16[320,128]{1,0:T(8,128)(2,1)S(1)} %group_front.1), channel_id=1, source_target_pairs={{0,64},{16,80},{32,96},{48,112},{64,0},{80,16},{96,32},{112,48},{1... | collective-permute-start | bytes 245768 | tf_op jit(solution)/shard_map/ppermute | solution.py:411
  54.1 1.8 %collective-permute-start.5 = (bf16[1120,128]{1,0:T(8,128)(2,1)S(1)}, bf16[1120,128]{1,0:T(8,128)(2,1)S(1)}, u32[]{:S(2)}, u32[]{:S(2)}) collective-permute-start(bf16[1120,128]{1,0:T(8,128)(2,1)S(1)} %get-tuple-element.23), channel_id=1, source_target_pairs={{0,0},{16,16},{32,32},{48,48},{64,64},{80,80},{96,96},{112,112},{1... | collective-permute-start | bytes 860168 | tf_op jit(solution)/shard_map/ppermute | solution.py:411
  55.0 0.9 collective-permute-start.4
  56.8 0.7 collective-permute-start.6
  58.3 25.6 %collective-permute-start.7 = (bf16[320,128]{1,0:T(8,128)(2,1)S(1)}, bf16[320,128]{1,0:T(8,128)(2,1)S(1)}, u32[]{:S(2)}, u32[]{:S(2)}) collective-permute-start(bf16[320,128]{1,0:T(8,128)(2,1)S(1)} %backward_one.1), channel_id=1, source_target_pairs={{0,64},{16,80},{32,96},{48,112},{64,0},{80,16},{96,32},{112,48},{1... | collective-permute-start | bytes 245768 | tf_op jit(solution)/shard_map/ppermute | solution.py:411
  104.5 20.2 %collective-permute-start.11 = (bf16[2,320,128]{2,1,0:T(8,128)(2,1)S(1)}, bf16[2,320,128]{2,1,0:T(8,128)(2,1)S(1)}, u32[]{:S(2)}, u32[]{:S(2)}) collective-permute-start(bf16[2,320,128]{2,1,0:T(8,128)(2,1)S(1)} %get-tuple-element.36), channel_id=1, source_target_pairs={{0,16},{16,32},{32,48},{48,64},{64,80},{80,96},{96,112},{112,128},... | collective-permute-start | bytes 491528 | tf_op jit(solution)/shard_map/ppermute | solution.py:455
  109.9 14.8 %collective-permute-start.10 = (bf16[2,320,128]{2,1,0:T(8,128)(2,1)S(1)}, bf16[2,320,128]{2,1,0:T(8,128)(2,1)S(1)}, u32[]{:S(2)}, u32[]{:S(2)}) collective-permute-start(bf16[2,320,128]{2,1,0:T(8,128)(2,1)S(1)} %get-tuple-element.35), channel_id=1, source_target_pairs={{0,16},{16,32},{32,48},{48,64},{64,80},{80,96},{96,112},{112,128},... | collective-permute-start | bytes 491528 | tf_op jit(solution)/shard_map/ppermute | solution.py:455
  112.9 11.8 %collective-permute-start.8 = (bf16[2,320,128]{2,1,0:T(8,128)(2,1)S(1)}, bf16[2,320,128]{2,1,0:T(8,128)(2,1)S(1)}, u32[]{:S(2)}, u32[]{:S(2)}) collective-permute-start(bf16[2,320,128]{2,1,0:T(8,128)(2,1)S(1)} %get-tuple-element.33.refs_13_), channel_id=1, source_target_pairs={{0,1},{1,2},{2,3},{3,4},{4,5},{5,6},{6,7},{7,8},{8,9},{9,10},{10,1... | collective-permute-start | bytes 491528 | tf_op jit(solution)/shard_map/ppermute | solution.py:458
  112.9 11.8 %collective-permute-start.9 = (bf16[2,320,128]{2,1,0:T(8,128)(2,1)S(1)}, bf16[2,320,128]{2,1,0:T(8,128)(2,1)S(1)}, u32[]{:S(2)}, u32[]{:S(2)}) collective-permute-start(bf16[2,320,128]{2,1,0:T(8,128)(2,1)S(1)} %get-tuple-element.30.refs_10_), channel_id=1, source_target_pairs={{1,0},{2,1},{3,2},{4,3},{5,4},{6,5},{7,6},{8,7},{9,8},{10,9},{11,1... | collective-permute-start | bytes 491528 | tf_op jit(solution)/shard_map/ppermute | solution.py:459

commit v5 on v4

--- a/solution.py
+++ b/solution.py
@@ -10,7 +10,7 @@
 BF = jnp.bfloat16
 F32 = jnp.float32
 GROUP = 4
-VMEM_LIMIT = 48 << 20
+VMEM_LIMIT = 28 << 20
 LONG = pl.CostEstimate(flops=10**10, transcendentals=0, bytes_accessed=1024)
 SHORT = pl.CostEstimate(flops=1024, transcendentals=0, bytes_accessed=1024)
 
@@ -118,6 +118,76 @@
     return out
 
 
+def halves(x):
+    top = x.astype(BF)
+    return top, (x - top.astype(F32)).astype(BF)
+
+
+def prepare_kernel(
+    slots, place, d0, d1, l0, l1, u0, u1, r0, r1, out, first_ops, second_ops, c_out, y_out
+):
+    n = d0.shape[0]
+    rows = packed_rows(n)
+    inv0, inv1 = d0[...], d1[...]
+    e0 = mm(inv0, l0[...])
+    e0_top, e0_rest = halves(e0)
+    e1_top, e1_rest = halves(mm(inv1, l1[...]))
+    h0_top, h0_rest = halves(mm(inv0, u0[...]))
+    h1_top, h1_rest = halves(mm(inv1, u1[...]))
+    y0 = mm(inv0, r0[...])
+    a = mm(e1_top, e0_top) + (mm(e1_top, e0_rest) + mm(e1_rest, e0_top))
+    c = mm(inv1, r1[...]) - (mm_fine(e1_top, y0) + mm(e1_rest, y0.astype(BF)))
+    a_top, a_rest = halves(a)
+    for t, part in enumerate((a_top, a_rest, -h1_top, -h1_rest)):
+        first_ops[:, t * n : (t + 1) * n] = part
+    for t, part in enumerate((-e0_top, -e0_rest, -h0_top, -h0_rest, -h0_top)):
+        second_ops[:, t * n : (t + 1) * n] = part
+    c_out[...] = c
+    y_out[...] = y0
+
+    @pl.when(pl.program_id(0) == place[3])
+    def _():
+        pack(out, 0, a_top)
+        pack(out, rows, mm(h0_top, h1_top).astype(BF))
+        pack(out, 2 * rows, (-(e0 + mm(h0_top, a_top))).astype(BF))
+        out[3 * rows : 3 * rows + n, :] = c.astype(BF)
+        out[3 * rows + n : 3 * rows + 2 * n, :] = (y0 - mm_fine(h0_top, c)).astype(BF)
+
+
+def prepare(slots, place, diag_inv, lower, upper, source):
+    n, cols = source.shape[1:]
+
+    def block(slab, width):
+        return pl.BlockSpec((None, n, width), lambda p, sl, at: (sl[slab, p], 0, 0))
+
+    def per(width):
+        return pl.BlockSpec((None, n, width), lambda p, sl, at: (p, 0, 0))
+
+    shape = jax.ShapeDtypeStruct
+    return pl.pallas_call(
+        prepare_kernel,
+        grid_spec=pltpu.PrefetchScalarGridSpec(
+            num_scalar_prefetch=2,
+            grid=(GROUP,),
+            in_specs=[block(s, n) for s in (0, 1, 0, 1, 0, 1)] + [block(s, cols) for s in (0, 1)],
+            out_specs=[
+                pl.BlockSpec((map_rows(n), cols), lambda p, sl, at: (0, 0)),
+                per(4 * n), per(5 * n), per(cols), per(cols),
+            ],
+        ),
+        out_shape=[
+            shape((map_rows(n), cols), BF),
+            shape((GROUP, n, 4 * n), BF),
+            shape((GROUP, n, 5 * n), BF),
+            shape((GROUP, n, cols), F32),
+            shape((GROUP, n, cols), F32),
+        ],
+        compiler_params=pltpu.CompilerParams(vmem_limit_bytes=VMEM_LIMIT),
+        cost_estimate=SHORT,
+        name="prepare",
+    )(slots, place, diag_inv, diag_inv, lower, lower, upper, upper, source, source)
+
+
 def per_owner(place, pieces, body):
     for owned in range(GROUP):
 
@@ -244,60 +314,43 @@
     )(*scalars, *operands)
 
 
-def solve_pencils(ends, columns):
-    n = ends[0].shape[0] // 2
-    fronts = [e[0:n, :] for e in ends]
-    backs = [e[n : 2 * n, :] for e in ends]
-    both = range(len(ends))
-    d0, d1, l0, l1, u0, u1, r0, r1 = zip(*columns)
-    v = [mm(u1[i][...], backs[i]) for i in both]
-    q = [r0[i][...].astype(F32) - mm(l0[i][...], fronts[i]) for i in both]
-    f0 = [mm_fine(d0[i][...], q[i]) for i in both]
-    v = [mm_fine(d1[i][...], v[i]) for i in both]
-    q = [r1[i][...].astype(F32) - mm_fine(l1[i][...], f0[i]) for i in both]
-    x1 = [mm_fine(d1[i][...], q[i]) - v[i] for i in both]
-    q = [mm_fine(u0[i][...], x1[i]) for i in both]
-    x0 = [f0[i] - mm_fine(d0[i][...], q[i]) for i in both]
-    return [(x0[i].astype(BF), x1[i].astype(BF)) for i in both]
-
-
-def two_pencils_kernel(chosen, slots, place, ends, *refs):
-    outs, tops = refs[16:18], refs[18]
-    solved = solve_pencils([ends[p] for p in chosen], [refs[0:8], refs[8:16]])
-    for i, ((x0, x1), out) in enumerate(zip(solved, outs)):
-        out[0] = x0
-        out[1] = x1
-        tops[i] = x1
-
-
-def two_pencils(chosen, slots, place, ends, diag_inv, lower, upper, source):
-    n, cols = source.shape[1:]
-    specs, operands = [constant(ends.shape)], [ends]
-    for p in chosen:
-        for array in (diag_inv, lower, upper, source):
-            for s in range(2):
-                specs.append(stored(s, lambda at, p=p: p, n, array.shape[-1]))
-                operands.append(array)
-    return element_call(
-        functools.partial(two_pencils_kernel, chosen), specs,
-        [jax.ShapeDtypeStruct((2, n, cols), BF)] * 3, slots, place, *operands, name="two_pencils",
-        cost=LONG if 0 in chosen else SHORT,
-    )
+def finish_kernel(place, ends, first_ops, second_ops, c, y0, within, beside, tops, solved):
+    n = c.shape[1]
+    every = range(GROUP)
+    fronts = [ends[p, 0:n, :] for p in every]
+    backs = [ends[p, n : 2 * n, :] for p in every]
+    x1 = [
+        c[p] + mm(first_ops[p], jnp.concatenate([fronts[p], fronts[p], backs[p], backs[p]], axis=0))
+        for p in every
+    ]
+    for p in every:
+        top, rest = halves(x1[p])
+        x0 = y0[p] + mm(
+            second_ops[p], jnp.concatenate([fronts[p], fronts[p], top, top, rest], axis=0)
+        )
+        solved[p, 0] = x0.astype(BF)
+        solved[p, 1] = top
+        tops[p] = top
+    even = lax.rem(place[1], 2) == 0
+    for s in range(2):
+        first, last = solved[0, s], solved[GROUP - 1, s]
+        within[s] = jnp.where(even, last, first)
+        beside[s] = jnp.where(even, first, last)
 
 
 def inner_jacobian_kernel(slots, *refs):
-    blocks, (first, second, third, last, ends) = refs[0:10], refs[10:15]
-    precond, partial, lowers, sides, vals = refs[15:]
-    n = first.shape[1]
+    blocks, (solved, ends) = refs[0:10], refs[10:12]
+    precond, partial, lowers, sides, vals = refs[12:]
+    n = solved.shape[2]
     pencil = pl.program_id(0)
 
     @pl.when(pencil == 0)
     def _():
-        zero = jnp.zeros(first.shape[1:], BF)
-        for p, values in enumerate((first, second, third, last)):
+        zero = jnp.zeros(solved.shape[2:], BF)
+        for p in range(GROUP):
             vals[0, p + 1] = zero
-            vals[1, p + 1] = values[0]
-            vals[2, p + 1] = values[1]
+            vals[1, p + 1] = solved[p, 0]
+            vals[2, p + 1] = solved[p, 1]
             vals[3, p + 1] = ends[p, n : 2 * n, :]
         for s in range(2):
             vals[s + 1, 0] = zero
@@ -331,10 +384,10 @@
 
 
 def inner_jacobian(slots, blocks, vectors):
-    n, cols = vectors[0].shape[1:]
+    n, cols = vectors[0].shape[2:]
 
     def whole(shape):
-        return pl.BlockSpec(shape, lambda p, sl: (0, 0, 0))
+        return pl.BlockSpec(shape, lambda p, sl: (0,) * len(shape))
 
     specs = [
         pl.BlockSpec((None, n, n), lambda p, sl, s=s: (sl[s, p], 0, 0))
@@ -368,8 +421,10 @@
     )(slots, *blocks, *blocks, *vectors)
 
 
-def edge_jacobian_kernel(slots, place, low, high, below_outer, below_inner, partial, lowers, sides, jac):
-    below = (below_outer.at[0], below_inner.at[0], below_inner.at[1], below_outer.at[1])
+def edge_jacobian_kernel(slots, place, beside, below, within, partial, lowers, sides, jac):
+    even = lax.rem(place[1], 2) == 0
+    low = [jnp.where(even, beside[s], within[s]) for s in range(2)]
+    high = [jnp.where(even, within[s], beside[s]) for s in range(2)]
     left = jnp.where(place[1] == 0, 0.0, 1.0).astype(F32)
     right = jnp.where(place[1] == place[2] - 1, 0.0, 1.0).astype(F32)
     start = jnp.where(place[0] == 0, 0.0, 1.0).astype(F32)
@@ -377,7 +432,7 @@
         for p in range(GROUP):
             total = partial[p, s]
             if s == 0:
-                total = total + start * mm(lowers[p], below[p][...])
+                total = total + start * mm(lowers[p], below[p])
             if p == 0:
                 total = total + left * mm(sides[s], low[s])
             if p == GROUP - 1:
@@ -416,9 +471,12 @@
     low_pair, high_pair, outer, inner = (1, 0, 2, 3), (0, 1, 3, 2), (1, 0, 3, 2), (0, 2, 1, 3)
     vec = ((n, cols), BF)
     maps = [None] * GROUP
-    for distance in (3, 1, 2, 0):
+    for distance in (3, 1, 2):
         piece = local_map(elem_slot, place, inverse, lower, upper, source, distance)
-        maps[distance] = to_peer(piece, distance) if distance else piece
+        maps[distance] = to_peer(piece, distance)
+    maps[0], first_ops, second_ops, c_own, y_own = prepare(
+        elem_slot, place, inverse, lower, upper, source
+    )
     pieces = (maps[3], maps[1], maps[2], maps[0])
 
     (send,) = whole_call(group_front_kernel, [vec], [place], *pieces, name="group_front")
@@ -448,24 +506,23 @@
     )
     ends = lax.all_to_all(ends, "sweep", 0, 0, axis_index_groups=groups)
 
-    def solved(*chosen):
-        return two_pencils(chosen, elem_slot, place, ends, inverse, lower, upper, source)
-
-    def up(values):
-        return lax.ppermute(values, "sweep", [(i, (i + 1) % count) for i in range(count)])
-
-    first, last, tops = solved(0, GROUP - 1)
-    low = lax.ppermute(last, "cross", [(i, (i + 1) % across) for i in range(across)])
-    high = lax.ppermute(first, "cross", [((i + 1) % across, i) for i in range(across)])
-    below_outer = up(tops)
-    second, third, tops = solved(1, 2)
-    below_inner = up(tops)
+    pair = ((2, n, cols), BF)
+    within, beside, tops, solved = whole_call(
+        finish_kernel, [pair, pair, ((GROUP, n, cols), BF), ((GROUP, 2, n, cols), BF)], [place],
+        ends, first_ops, second_ops, c_own, y_own, name="finish",
+    )
+    aside = [(across - 1, across - 1), (0, 0)]
+    for i in range(1, across - 1, 2):
+        aside += [(i, i + 1), (i + 1, i)]
+    beside = lax.ppermute(beside, "cross", aside)
+    below = lax.ppermute(tops, "sweep", [(i, (i + 1) % count) for i in range(count)])
+    within = lax.ppermute(within, "cross", [(i, i ^ 1) for i in range(across)])
     precond, partial, lowers, sides = inner_jacobian(
-        elem_slot, (diagonal, lower, upper, minus, plus), (first, second, third, last, ends)
+        elem_slot, (diagonal, lower, upper, minus, plus), (solved, ends)
     )
     (jac,) = whole_call(
         edge_jacobian_kernel, [((2 * GROUP, n, cols), BF)], [elem_slot, place],
-        low, high, below_outer, below_inner, partial, lowers, sides, name="edge_jacobian",
+        beside, below, within, partial, lowers, sides, name="edge_jacobian",
     )
     return precond.reshape(right_side.shape), jac.reshape(right_side.shape)
 

time: 128 us -> 120 us (0.938); the launches traced: 127 us -> 117 us
  waiting for transfers between devices: 24.6 us -> 19 us
  starting transfers between devices: 43.7 us -> 40.4 us
    pallas_call x6 -> x3, Pallas kernels: 23.3 us -> 10.9 us  [element_call(): pl.pallas_call(kernel, grid_spec=pltpu.PrefetchScalarGridSpec(num_scalar_...]
    pallas_call x0 -> x1, Pallas kernels: none -> 9.22 us  [prepare(): pl.pallas_call(prepare_kernel, grid_spec=pltpu.PrefetchScalarGridSpec(num...]
    ppermute x3, waiting for transfers between devices: 22.1 us -> 16.5 us  [to_peer(): lax.ppermute(values, 'sweep', [(i, i ^ distance) for i in range(count)])]
    ppermute x4 -> x3, starting transfers between devices: 7.89 us -> 4.57 us  [the longest x1 2.46 us: local(): beside = lax.ppermute(beside, 'cross', aside)]
    pallas_call x7 -> x8, Pallas kernels: 11.8 us -> 14.5 us  [whole_call(): pl.pallas_call(kernel, in_specs=specs, out_specs=[pl.BlockSpec(memory_spa...]
  transfers between devices with their start and end apart: 12 -> 11, of which waited for: 3 -> 3; matrix products, arithmetic and copies ran while one was open for 0% -> 0% of each run, Pallas kernels for 22% -> 25%
where the time goes in v5:
time: 120 us; the launch traced here: 117 us
  Pallas kernels  42.5 us (35%)
  starting transfers between devices  40.4 us (34%)
  waiting for transfers between devices  19 us (16%)
  blocking collectives  13.9 us (12%)
    ppermute x5, starting transfers between devices, swap(): return lax.ppermute(values, 'sweep', pairs)  30.6 us
    ppermute x3, waiting for transfers between devices, to_peer(): lax.ppermute(values, 'sweep', [(i, i ^ distance) for i in range(count)])  16.5 us
    pallas_call x8, Pallas kernels, whole_call(): pl.pallas_call(kernel, in_specs=specs, out_specs=[pl.BlockSpec(memory_spa...  14.5 us
    all_to_all x1, blocking collectives, local(): ends = lax.all_to_all(ends, 'sweep', 0, 0, axis_index_groups=groups)  13.9 us
    pallas_call x3, Pallas kernels, element_call(): pl.pallas_call(kernel, grid_spec=pltpu.PrefetchScalarGridSpec(num_scalar_...  10.9 us
    pallas_call x1, Pallas kernels, prepare(): pl.pallas_call(prepare_kernel, grid_spec=pltpu.PrefetchScalarGridSpec(num...  9.22 us
    pallas_call x1, Pallas kernels, inner_jacobian(): pl.pallas_call(inner_jacobian_kernel, grid_spec=pltpu.PrefetchScalarGridS...  7.88 us
    ppermute x3, starting transfers between devices, to_peer(): lax.ppermute(values, 'sweep', [(i, i ^ distance) for i in range(count)])  5.26 us
  transfers between devices with their start and end apart: 11, of which 3 were waited for; matrix products, arithmetic and copies ran while one was open for 0% of the time, Pallas kernels for 25%

profile of v5, /device:TPU:8, one launch (start us, length us, event | category | flops | bytes accessed | tf_op | source)
XLA Modules:
  0.0 117.4 jit_solution(9430903454403699509)
XLA Ops:
  1.4 3.6 %local_map.3 = bf16[3040,128]{1,0:T(8,128)(2,1)S(1)} custom-call(s32[2,4]{1,0:T(2,128)S(1)} %copy-done, s32[5]{0:T(128)S(1)} %stack.19.place, bf16[8,320,320]{2,1,0:T(8,128)(2,1)} %bitcast.33, bf16[8,320,320]{2,1,0:T(8,128)(2,1)} %bitcast.34, bf16[8,320,320]{2,1,0:T(8,128)(2,1)} %bitcast.13, bf16[8,320,320]{2,1,0:T(8,128)(2,1)} %bitcast.14, ...), custom_call_target="tpu_custom_call" | custom-call | flops 1024 | bytes 1024 | tf_op jit(solution)/shard_map/local_map/pallas_call | solution.py:89
  5.0 3.7 %collective-permute-start = (bf16[3040,128]{1,0:T(8,128)(2,1)S(1)}, bf16[3040,128]{1,0:T(8,128)(2,1)S(1)}, u32[]{:S(2)}, u32[]{:S(2)}) collective-permute-start(bf16[3040,128]{1,0:T(8,128)(2,1)S(1)} %local_map.3), channel_id=1, source_target_pairs={{0,48},{16,32},{32,16},{48,0},{64,112},{80,96},{96,80},{112,64},{1... | collective-permute-start | bytes 2334728 | tf_op jit(solution)/shard_map/ppermute | solution.py:469
  8.8 3.6 %local_map.4 = bf16[3040,128]{1,0:T(8,128)(2,1)S(1)} custom-call(s32[2,4]{1,0:T(2,128)S(1)} %copy-done, s32[5]{0:T(128)S(1)} %stack.19.place, bf16[8,320,320]{2,1,0:T(8,128)(2,1)} %bitcast.35, bf16[8,320,320]{2,1,0:T(8,128)(2,1)} %bitcast.36, bf16[8,320,320]{2,1,0:T(8,128)(2,1)} %bitcast.15, bf16[8,320,320]{2,1,0:T(8,128)(2,1)} %bitcast.16, ...), custom_call_target="tpu_custom_call" | custom-call | flops 1024 | bytes 1024 | tf_op jit(solution)/shard_map/local_map/pallas_call | solution.py:89
  12.4 1.3 %collective-permute-start.1 = (bf16[3040,128]{1,0:T(8,128)(2,1)S(1)}, bf16[3040,128]{1,0:T(8,128)(2,1)S(1)}, u32[]{:S(2)}, u32[]{:S(2)}) collective-permute-start(bf16[3040,128]{1,0:T(8,128)(2,1)S(1)} %local_map.4), channel_id=1, source_target_pairs={{0,16},{16,0},{32,48},{48,32},{64,80},{80,64},{96,112},{112,96},{1... | collective-permute-start | bytes 2334728 | tf_op jit(solution)/shard_map/ppermute | solution.py:469
  13.7 3.6 %local_map.5 = bf16[3040,128]{1,0:T(8,128)(2,1)S(1)} custom-call(s32[2,4]{1,0:T(2,128)S(1)} %copy-done, s32[5]{0:T(128)S(1)} %stack.19.place, bf16[8,320,320]{2,1,0:T(8,128)(2,1)} %bitcast.37, bf16[8,320,320]{2,1,0:T(8,128)(2,1)} %bitcast.38, bf16[8,320,320]{2,1,0:T(8,128)(2,1)} %bitcast.17, bf16[8,320,320]{2,1,0:T(8,128)(2,1)} %bitcast.18, ...), custom_call_target="tpu_custom_call" | custom-call | flops 1024 | bytes 1024 | tf_op jit(solution)/shard_map/local_map/pallas_call | solution.py:89
  17.6 9.2 %prepare.1 = (bf16[3040,128]{1,0:T(8,128)(2,1)S(1)}, bf16[4,320,1280]{2,1,0:T(8,128)(2,1)S(1)}, bf16[4,320,1600]{2,1,0:T(8,128)(2,1)S(1)}, f32[4,320,128]{2,1,0:T(8,128)S(1)}, f32[4,320,128]{2,1,0:T(8,128)S(1)}) custom-call(s32[2,4]{1,0:T(2,128)S(1)} %copy-done, s32[5]{0:T(128)S(1)} %stack.19.place, bf16[8,320,320]{2,1,0:T(8,128)(2,1)} %bitcast.39, ...), custom_call_target="tpu_custom_call" | custom-call | flops 1024 | bytes 1024 | tf_op jit(solution)/shard_map/prepare/pallas_call | solution.py:167
  26.8 1.0 collective-permute-done.across
  27.8 15.5 %collective-permute-done.1.near = bf16[3040,128]{1,0:T(8,128)(2,1)S(1)} collective-permute-done((bf16[3040,128]{1,0:T(8,128)(2,1)S(1)}, bf16[3040,128]{1,0:T(8,128)(2,1)S(1)}, u32[]{:S(2)}, u32[]{:S(2)}) %collective-permute-start.1) | collective-permute-done | bytes 778272 | tf_op jit(solution)/shard_map/ppermute | solution.py:469
  43.3 1.4 %group_front.1 = bf16[320,128]{1,0:T(8,128)(2,1)S(1)} custom-call(s32[5]{0:T(128)S(1)} %stack.19.place, bf16[3040,128]{1,0:T(8,128)(2,1)S(1)} %collective-permute-done.across, bf16[3040,128]{1,0:T(8,128)(2,1)S(1)} %collective-permute-done.1.near, bf16[3040,128]{1,0:T(8,128)(2,1)S(1)} %collective-permute-done.2.next_one, ...), custom_call_target="tpu_custom_call" | custom-call | flops 1024 | bytes 1024 | tf_op jit(solution)/shard_map/group_front/pallas_call | solution.py:306
  44.7 5.2 %collective-permute-start.3 = (bf16[320,128]{1,0:T(8,128)(2,1)S(1)}, bf16[320,128]{1,0:T(8,128)(2,1)S(1)}, u32[]{:S(2)}, u32[]{:S(2)}) collective-permute-start(bf16[320,128]{1,0:T(8,128)(2,1)S(1)} %group_front.1), channel_id=1, source_target_pairs={{0,64},{16,80},{32,96},{48,112},{64,0},{80,16},{96,32},{112,48},{1... | collective-permute-start | bytes 245768 | tf_op jit(solution)/shard_map/ppermute | solution.py:466
  49.9 4.2 %group_map.1 = (bf16[320,320]{1,0:T(8,128)(2,1)S(1)}, bf16[320,320]{1,0:T(8,128)(2,1)S(1)}, bf16[320,320]{1,0:T(8,128)(2,1)S(1)}, f32[320,128]{1,0:T(8,128)S(1)}...) custom-call(s32[5]{0:T(128)S(1)} %stack.19.place, bf16[3040,128]{1,0:T(8,128)(2,1)S(1)} %collective-permute-done.across, ...), custom_call_target="tpu_custom_call" | custom-call | flops 1024 | bytes 1024 | tf_op jit(solution)/shard_map/group_map/pallas_call | solution.py:306
  55.0 0.9 collective-permute-start.4
  55.9 0.8 turn.1
  57.5 0.8 backward_one.1
  58.3 23.2 %collective-permute-start.7 = (bf16[320,128]{1,0:T(8,128)(2,1)S(1)}, bf16[320,128]{1,0:T(8,128)(2,1)S(1)}, u32[]{:S(2)}, u32[]{:S(2)}) collective-permute-start(bf16[320,128]{1,0:T(8,128)(2,1)S(1)} %backward_one.1), channel_id=1, source_target_pairs={{0,64},{16,80},{32,96},{48,112},{64,0},{80,16},{96,32},{112,48},{1... | collective-permute-start | bytes 245768 | tf_op jit(solution)/shard_map/ppermute | solution.py:466
  81.5 2.4 %collective-permute-done.7.hop4 = bf16[320,128]{1,0:T(8,128)(2,1)S(1)} collective-permute-done((bf16[320,128]{1,0:T(8,128)(2,1)S(1)}, bf16[320,128]{1,0:T(8,128)(2,1)S(1)}, u32[]{:S(2)}, u32[]{:S(2)}) %collective-permute-start.7) | collective-permute-done | bytes 81952 | tf_op jit(solution)/shard_map/ppermute | solution.py:466
  83.9 2.3 %interfaces.1 = bf16[4,640,128]{2,1,0:T(8,128)(2,1)S(1)} custom-call(s32[5]{0:T(128)S(1)} %stack.19.place, bf16[3040,128]{1,0:T(8,128)(2,1)S(1)} %collective-permute-done.across, bf16[3040,128]{1,0:T(8,128)(2,1)S(1)} %collective-permute-done.1.near, bf16[3040,128]{1,0:T(8,128)(2,1)S(1)} %collective-permute-done.2.next_one, ...), custom_call_target="tpu_custom_call" | custom-call | flops 1024 | bytes 1024 | tf_op jit(solution)/shard_map/interfaces/pallas_call | solution.py:306
  86.2 13.9 %all_to_all.5.ends.refs_11_ = bf16[4,640,128]{2,1,0:T(8,128)(2,1)S(1)} all-to-all(bf16[4,640,128]{2,1,0:T(8,128)(2,1)S(1)} %interfaces.1), channel_id=1, replica_groups={{0,16,32,48},{64,80,96,112},{128,144,160,176},{192,208,224,240},{1,17,3..., dimensions={0} | all-to-all | bytes 1310720 | tf_op jit(solution)/shard_map/all_to_all | solution.py:507
  100.1 2.7 %finish.1 = (bf16[2,320,128]{2,1,0:T(8,128)(2,1)S(1)}, bf16[2,320,128]{2,1,0:T(8,128)(2,1)S(1)}, bf16[4,320,128]{2,1,0:T(8,128)(2,1)S(1)}, bf16[4,2,320,128]{3,2,1,0:T(8,128)(2,1)S(1)}) custom-call(s32[5]{0:T(128)S(1)} %stack.19.place, bf16[4,640,128]{2,1,0:T(8,128)(2,1)S(1)} %all_to_all.5.ends.refs_11_, ...), custom_call_target="tpu_custom_call" | custom-call | flops 1024 | bytes 1024 | tf_op jit(solution)/shard_map/finish/pallas_call | solution.py:306
  102.8 1.0 collective-permute-start.9
  103.8 2.5 %collective-permute-start.8 = (bf16[2,320,128]{2,1,0:T(8,128)(2,1)S(1)}, bf16[2,320,128]{2,1,0:T(8,128)(2,1)S(1)}, u32[]{:S(2)}, u32[]{:S(2)}) collective-permute-start(bf16[2,320,128]{2,1,0:T(8,128)(2,1)S(1)} %get-tuple-element.40), channel_id=1, source_target_pairs={{15,15},{0,0},{1,2},{2,1},{3,4},{4,3},{5,6},{6,5},{7,8},{8,7},{9,1... | collective-permute-start | bytes 491528 | tf_op jit(solution)/shard_map/ppermute | solution.py:517
  106.3 1.1 collective-permute-start.10
  107.4 7.9 %inner_jacobian.1 = (bf16[8,320,128]{2,1,0:T(8,128)(2,1)}, f32[4,2,320,128]{3,2,1,0:T(8,128)S(1)}, bf16[4,320,320]{2,1,0:T(8,128)(2,1)S(1)}, bf16[4,320,320]{2,1,0:T(8,128)(2,1)S(1)}) custom-call(s32[2,4]{1,0:T(2,128)S(1)} %copy-done, bf16[8,320,320]{2,1,0:T(8,128)(2,1)} %bitcast.49, bf16[8,320,320]{2,1,0:T(8,128)(2,1)} %bitcast.21, ...), custom_call_target="tpu_custom_call" | custom-call | flops 1024 | bytes 1024 | tf_op jit(solution)/shard_map/inner_jacobian/pallas_call | solution.py:398
  115.3 2.1 %edge_jacobian.1 = bf16[8,320,128]{2,1,0:T(8,128)(2,1)} custom-call(s32[2,4]{1,0:T(2,128)S(1)} %copy-done, s32[5]{0:T(128)S(1)} %stack.19.place, bf16[2,320,128]{2,1,0:T(8,128)(2,1)S(1)} %collective-permute-done.8.beside, bf16[4,320,128]{2,1,0:T(8,128)(2,1)S(1)} %collective-permute-done.9.below, bf16[2,320,128]{2,1,0:T(8,128)(2,1)S(1)} %collective-permute-done.10.within, ...), custom_call_target="tpu_custom_call" | custom-call | flops 1024 | bytes 1024 | tf_op jit(solution)/shard_map/edge_jacobian/pallas_call | solution.py:306
  (15 shorter events, 2.6 us)
Async XLA Ops:
  0.7 0.7 copy-start
  5.0 22.8 %collective-permute-start = (bf16[3040,128]{1,0:T(8,128)(2,1)S(1)}, bf16[3040,128]{1,0:T(8,128)(2,1)S(1)}, u32[]{:S(2)}, u32[]{:S(2)}) collective-permute-start(bf16[3040,128]{1,0:T(8,128)(2,1)S(1)} %local_map.3), channel_id=1, source_target_pairs={{0,48},{16,32},{32,16},{48,0},{64,112},{80,96},{96,80},{112,64},{1... | collective-permute-start | bytes 2334728 | tf_op jit(solution)/shard_map/ppermute | solution.py:469
  12.4 30.9 %collective-permute-start.1 = (bf16[3040,128]{1,0:T(8,128)(2,1)S(1)}, bf16[3040,128]{1,0:T(8,128)(2,1)S(1)}, u32[]{:S(2)}, u32[]{:S(2)}) collective-permute-start(bf16[3040,128]{1,0:T(8,128)(2,1)S(1)} %local_map.4), channel_id=1, source_target_pairs={{0,16},{16,0},{32,48},{48,32},{64,80},{80,64},{96,112},{112,96},{1... | collective-permute-start | bytes 2334728 | tf_op jit(solution)/shard_map/ppermute | solution.py:469
  17.3 26.0 %collective-permute-start.2 = (bf16[3040,128]{1,0:T(8,128)(2,1)S(1)}, bf16[3040,128]{1,0:T(8,128)(2,1)S(1)}, u32[]{:S(2)}, u32[]{:S(2)}) collective-permute-start(bf16[3040,128]{1,0:T(8,128)(2,1)S(1)} %local_map.5), channel_id=1, source_target_pairs={{0,32},{16,48},{32,0},{48,16},{64,96},{80,112},{96,64},{112,80},{1... | collective-permute-start | bytes 2334728 | tf_op jit(solution)/shard_map/ppermute | solution.py:469
  44.7 10.1 %collective-permute-start.3 = (bf16[320,128]{1,0:T(8,128)(2,1)S(1)}, bf16[320,128]{1,0:T(8,128)(2,1)S(1)}, u32[]{:S(2)}, u32[]{:S(2)}) collective-permute-start(bf16[320,128]{1,0:T(8,128)(2,1)S(1)} %group_front.1), channel_id=1, source_target_pairs={{0,64},{16,80},{32,96},{48,112},{64,0},{80,16},{96,32},{112,48},{1... | collective-permute-start | bytes 245768 | tf_op jit(solution)/shard_map/ppermute | solution.py:466
  54.1 1.8 %collective-permute-start.5 = (bf16[1120,128]{1,0:T(8,128)(2,1)S(1)}, bf16[1120,128]{1,0:T(8,128)(2,1)S(1)}, u32[]{:S(2)}, u32[]{:S(2)}) collective-permute-start(bf16[1120,128]{1,0:T(8,128)(2,1)S(1)} %get-tuple-element.27), channel_id=1, source_target_pairs={{0,0},{16,16},{32,32},{48,48},{64,64},{80,80},{96,96},{112,112},{1... | collective-permute-start | bytes 860168 | tf_op jit(solution)/shard_map/ppermute | solution.py:466
  55.0 0.9 collective-permute-start.4
  56.8 0.7 collective-permute-start.6
  58.3 25.6 %collective-permute-start.7 = (bf16[320,128]{1,0:T(8,128)(2,1)S(1)}, bf16[320,128]{1,0:T(8,128)(2,1)S(1)}, u32[]{:S(2)}, u32[]{:S(2)}) collective-permute-start(bf16[320,128]{1,0:T(8,128)(2,1)S(1)} %backward_one.1), channel_id=1, source_target_pairs={{0,64},{16,80},{32,96},{48,112},{64,0},{80,16},{96,32},{112,48},{1... | collective-permute-start | bytes 245768 | tf_op jit(solution)/shard_map/ppermute | solution.py:466
  102.8 12.5 %collective-permute-start.9 = (bf16[4,320,128]{2,1,0:T(8,128)(2,1)S(1)}, bf16[4,320,128]{2,1,0:T(8,128)(2,1)S(1)}, u32[]{:S(2)}, u32[]{:S(2)}) collective-permute-start(bf16[4,320,128]{2,1,0:T(8,128)(2,1)S(1)} %get-tuple-element.41), channel_id=1, source_target_pairs={{0,16},{16,32},{32,48},{48,64},{64,80},{80,96},{96,112},{112,128},... | collective-permute-start | bytes 983048 | tf_op jit(solution)/shard_map/ppermute | solution.py:518
  103.8 11.5 %collective-permute-start.8 = (bf16[2,320,128]{2,1,0:T(8,128)(2,1)S(1)}, bf16[2,320,128]{2,1,0:T(8,128)(2,1)S(1)}, u32[]{:S(2)}, u32[]{:S(2)}) collective-permute-start(bf16[2,320,128]{2,1,0:T(8,128)(2,1)S(1)} %get-tuple-element.40), channel_id=1, source_target_pairs={{15,15},{0,0},{1,2},{2,1},{3,4},{4,3},{5,6},{6,5},{7,8},{8,7},{9,1... | collective-permute-start | bytes 491528 | tf_op jit(solution)/shard_map/ppermute | solution.py:517
  106.3 9.0 %collective-permute-start.10 = (bf16[2,320,128]{2,1,0:T(8,128)(2,1)S(1)}, bf16[2,320,128]{2,1,0:T(8,128)(2,1)S(1)}, u32[]{:S(2)}, u32[]{:S(2)}) collective-permute-start(bf16[2,320,128]{2,1,0:T(8,128)(2,1)S(1)} %get-tuple-element.42), channel_id=1, source_target_pairs={{0,1},{1,0},{2,3},{3,2},{4,5},{5,4},{6,7},{7,6},{8,9},{9,8},{10,11... | collective-permute-start | bytes 491528 | tf_op jit(solution)/shard_map/ppermute | solution.py:519

commit v6 on v5

--- a/solution.py
+++ b/solution.py
@@ -123,10 +123,28 @@
     return top, (x - top.astype(F32)).astype(BF)
 
 
-def prepare_kernel(
-    slots, place, d0, d1, l0, l1, u0, u1, r0, r1, out, first_ops, second_ops, c_out, y_out
-):
+def prepare_kernel(slots, place, *refs):
+    d0, d1, l0, l1, u0, u1, r0, r1 = refs[0:8]
+    diags, minuses, pluses = refs[8:10], refs[10:12], refs[12:14]
+    out, first_ops, second_ops, c_out, y_out, rows_out, lowers, sides = refs[14:]
     n = d0.shape[0]
+    pencil = pl.program_id(0)
+    for s in range(2):
+        row = (diags[s], (l0, l1)[s], (u0, u1)[s], minuses[s], pluses[s])
+        for t, block in enumerate(row):
+            rows_out[s, :, t * n : (t + 1) * n] = block[...]
+    lowers[...] = l0[...]
+
+    @pl.when(pencil == 0)
+    def _():
+        for s in range(2):
+            sides[s] = minuses[s][...]
+
+    @pl.when(pencil == GROUP - 1)
+    def _():
+        for s in range(2):
+            sides[s + 2] = pluses[s][...]
+
     rows = packed_rows(n)
     inv0, inv1 = d0[...], d1[...]
     e0 = mm(inv0, l0[...])
@@ -145,7 +163,7 @@
     c_out[...] = c
     y_out[...] = y0
 
-    @pl.when(pl.program_id(0) == place[3])
+    @pl.when(pencil == place[3])
     def _():
         pack(out, 0, a_top)
         pack(out, rows, mm(h0_top, h1_top).astype(BF))
@@ -154,7 +172,7 @@
         out[3 * rows + n : 3 * rows + 2 * n, :] = (y0 - mm_fine(h0_top, c)).astype(BF)
 
 
-def prepare(slots, place, diag_inv, lower, upper, source):
+def prepare(slots, place, diag_inv, lower, upper, source, diagonal, minus, plus):
     n, cols = source.shape[1:]
 
     def block(slab, width):
@@ -169,10 +187,15 @@
         grid_spec=pltpu.PrefetchScalarGridSpec(
             num_scalar_prefetch=2,
             grid=(GROUP,),
-            in_specs=[block(s, n) for s in (0, 1, 0, 1, 0, 1)] + [block(s, cols) for s in (0, 1)],
+            in_specs=[block(s, n) for s in (0, 1) * 3]
+            + [block(s, cols) for s in (0, 1)]
+            + [block(s, n) for s in (0, 1) * 3],
             out_specs=[
                 pl.BlockSpec((map_rows(n), cols), lambda p, sl, at: (0, 0)),
                 per(4 * n), per(5 * n), per(cols), per(cols),
+                pl.BlockSpec((None, 2, n, 5 * n), lambda p, sl, at: (p, 0, 0, 0)),
+                per(n),
+                pl.BlockSpec((4, n, n), lambda p, sl, at: (0, 0, 0)),
             ],
         ),
         out_shape=[
@@ -181,11 +204,17 @@
             shape((GROUP, n, 5 * n), BF),
             shape((GROUP, n, cols), F32),
             shape((GROUP, n, cols), F32),
+            shape((GROUP, 2, n, 5 * n), BF),
+            shape((GROUP, n, n), BF),
+            shape((4, n, n), BF),
         ],
         compiler_params=pltpu.CompilerParams(vmem_limit_bytes=VMEM_LIMIT),
         cost_estimate=SHORT,
         name="prepare",
-    )(slots, place, diag_inv, diag_inv, lower, lower, upper, upper, source, source)
+    )(
+        slots, place, diag_inv, diag_inv, lower, lower, upper, upper, source, source,
+        diagonal, diagonal, minus, minus, plus, plus,
+    )
 
 
 def per_owner(place, pieces, body):
@@ -194,31 +223,6 @@
         @pl.when(place[3] == owned)
         def _(owned=owned):
             body([pieces[owned ^ j] for j in range(GROUP)])
-
-
-def group_front_kernel(place, across, near, next_one, own, send):
-    n = send.shape[0]
-    rows = packed_rows(n)
-
-    def body(maps):
-        front = maps[0][3 * rows : 3 * rows + n, :].astype(F32)
-        for one in maps[1:]:
-            shift = one[3 * rows : 3 * rows + n, :].astype(F32)
-            front = mm_fine(unpack(one, 0, n), front) + shift
-        send[...] = front.astype(BF)
-
-    per_owner(place, (own, near, next_one, across), body)
-
-
-def joined(left, right):
-    a_l, b_l, g_l, c_l, h_l = left
-    a_r, b_r, g_r, c_r, h_r = right
-    a = mm(a_r, a_l).astype(BF)
-    b = mm(b_l, b_r).astype(BF)
-    g = (mm(b_l, mm(g_r, a_l).astype(BF)) + g_l.astype(F32)).astype(BF)
-    c = mm_fine(a_r, c_l) + c_r
-    h = mm_fine(b_l, mm_fine(g_r, c_l) + h_r) + h_l
-    return a, b, g, c, h
 
 
 def segment(one, n):
@@ -232,21 +236,48 @@
     )
 
 
-def group_map_kernel(
-    place, across, near, next_one, own, a_out, b_out, g_out, c_out, h_out, send_far
+def group_back_kernel(
+    place, across, near, next_one, own, a_low, b_low, c_low, g_out, h_out, send_far
 ):
-    n = a_out.shape[0]
+    n = a_low.shape[0]
 
     def body(maps):
-        segments = [segment(one, n) for one in maps]
-        a, b, g, c, h = joined(joined(*segments[:2]), joined(*segments[2:]))
-        a_out[...] = a
-        b_out[...] = b
+        (a0, b0, g0, c0, h0), (a1, b1, g1, c1, h1), (a2, b2, g2, c2, h2), (_, _, g3, _, h3) = (
+            segment(one, n) for one in maps
+        )
+        a = mm(a1, a0).astype(BF)
+        b = mm(b0, b1).astype(BF)
+        c = mm_fine(a1, c0) + c1
+        low_g = mm(b0, mm(g1, a0).astype(BF)) + g0.astype(F32)
+        high_g = (mm(b2, mm(g3, a2).astype(BF)) + g2.astype(F32)).astype(BF)
+        g = (mm(b, mm(high_g, a).astype(BF)) + low_g).astype(BF)
+        low_h = mm_fine(b0, mm_fine(g1, c0) + h1) + h0
+        high_h = mm_fine(b2, mm_fine(g3, c2) + h3) + h2
+        h = mm_fine(b, mm_fine(high_g, c) + high_h) + low_h
+        a_low[...] = a
+        b_low[...] = b
+        c_low[...] = c
         g_out[...] = g
-        c_out[...] = c
         h_out[...] = h
         send_far[0:n, :] = h.astype(BF)
         pack(send_far, n, g)
+
+    per_owner(place, (own, near, next_one, across), body)
+
+
+def group_front_kernel(
+    place, across, near, next_one, own, a_low, b_low, c_low, send, a_out, b_out, c_out
+):
+    n = a_low.shape[0]
+
+    def body(maps):
+        (a2, b2, _, c2, _), (a3, b3, _, c3, _) = (segment(one, n) for one in maps[2:])
+        a = mm(a3, a2).astype(BF)
+        c = mm_fine(a, c_low[...]) + (mm_fine(a3, c2) + c3)
+        send[...] = c.astype(BF)
+        c_out[...] = c
+        a_out[...] = mm(a, a_low[...]).astype(BF)
+        b_out[...] = mm(b_low[...], mm(b2, b3).astype(BF)).astype(BF)
 
     per_owner(place, (own, near, next_one, across), body)
 
@@ -314,7 +345,7 @@
     )(*scalars, *operands)
 
 
-def finish_kernel(place, ends, first_ops, second_ops, c, y0, within, beside, tops, solved):
+def finish_kernel(place, ends, first_ops, second_ops, c, y0, beside, tops, solved):
     n = c.shape[1]
     every = range(GROUP)
     fronts = [ends[p, 0:n, :] for p in every]
@@ -333,95 +364,39 @@
         tops[p] = top
     even = lax.rem(place[1], 2) == 0
     for s in range(2):
-        first, last = solved[0, s], solved[GROUP - 1, s]
-        within[s] = jnp.where(even, last, first)
-        beside[s] = jnp.where(even, first, last)
-
-
-def inner_jacobian_kernel(slots, *refs):
-    blocks, (solved, ends) = refs[0:10], refs[10:12]
-    precond, partial, lowers, sides, vals = refs[12:]
+        beside[s] = jnp.where(even, solved[0, s], solved[GROUP - 1, s])
+
+
+def row_products(chosen, rows, solved, ends, partial):
     n = solved.shape[2]
-    pencil = pl.program_id(0)
-
-    @pl.when(pencil == 0)
-    def _():
-        zero = jnp.zeros(solved.shape[2:], BF)
+    zero = jnp.zeros(solved.shape[2:], BF)
+
+    def value(s, p):
+        if p < 0 or p >= GROUP or s < 0:
+            return zero
+        return ends[p, n : 2 * n, :] if s == 2 else solved[p, s]
+
+    for i, p in enumerate(chosen):
+        for s in range(2):
+            around = [value(s, p), value(s - 1, p), value(s + 1, p), value(s, p - 1), value(s, p + 1)]
+            partial[i, s] = mm(rows[p, s], jnp.concatenate(around, axis=0))
+
+
+def first_rows_kernel(place, rows, solved, ends, within, partial):
+    even = lax.rem(place[1], 2) == 0
+    row_products((0, 1), rows, solved, ends, partial)
+    for s in range(2):
+        within[s] = jnp.where(even, solved[GROUP - 1, s], solved[0, s])
+
+
+def second_rows_kernel(slots, rows, solved, ends, precond, partial):
+    row_products((2, 3), rows, solved, ends, partial)
+    for s in range(2):
         for p in range(GROUP):
-            vals[0, p + 1] = zero
-            vals[1, p + 1] = solved[p, 0]
-            vals[2, p + 1] = solved[p, 1]
-            vals[3, p + 1] = ends[p, n : 2 * n, :]
-        for s in range(2):
-            vals[s + 1, 0] = zero
-            vals[s + 1, GROUP + 1] = zero
-
-    both = range(2)
-    near = [
-        [
-            vals[s + 1, pencil + 1], vals[s, pencil + 1], vals[s + 2, pencil + 1],
-            vals[s + 1, pencil], vals[s + 1, pencil + 2],
-        ]
-        for s in both
-    ]
-    totals = [mm(blocks[5 * s][...], near[s][0]) for s in both]
-    for t in range(1, 5):
-        totals = [totals[s] + mm(blocks[5 * s + t][...], near[s][t]) for s in both]
-    for s in both:
-        precond[slots[s, pencil]] = near[s][0]
-        partial[s] = totals[s]
-    lowers[...] = blocks[1][...]
-
-    @pl.when(pencil == 0)
-    def _():
-        for s in both:
-            sides[s] = blocks[5 * s + 3][...]
-
-    @pl.when(pencil == GROUP - 1)
-    def _():
-        for s in both:
-            sides[s + 2] = blocks[5 * s + 4][...]
-
-
-def inner_jacobian(slots, blocks, vectors):
-    n, cols = vectors[0].shape[2:]
-
-    def whole(shape):
-        return pl.BlockSpec(shape, lambda p, sl: (0,) * len(shape))
-
-    specs = [
-        pl.BlockSpec((None, n, n), lambda p, sl, s=s: (sl[s, p], 0, 0))
-        for s in range(2)
-        for _ in blocks
-    ]
-    stored_shape = (2 * GROUP, n, cols)
-    return pl.pallas_call(
-        inner_jacobian_kernel,
-        grid_spec=pltpu.PrefetchScalarGridSpec(
-            num_scalar_prefetch=1,
-            grid=(GROUP,),
-            in_specs=specs + [whole(v.shape) for v in vectors],
-            out_specs=[
-                whole(stored_shape),
-                pl.BlockSpec((None, 2, n, cols), lambda p, sl: (p, 0, 0, 0)),
-                pl.BlockSpec((None, n, n), lambda p, sl: (p, 0, 0)),
-                whole((4, n, n)),
-            ],
-            scratch_shapes=[pltpu.VMEM((4, GROUP + 2, n, cols), BF)],
-        ),
-        out_shape=[
-            jax.ShapeDtypeStruct(stored_shape, BF),
-            jax.ShapeDtypeStruct((GROUP, 2, n, cols), F32),
-            jax.ShapeDtypeStruct((GROUP, n, n), BF),
-            jax.ShapeDtypeStruct((4, n, n), BF),
-        ],
-        compiler_params=pltpu.CompilerParams(vmem_limit_bytes=VMEM_LIMIT),
-        cost_estimate=SHORT,
-        name="inner_jacobian",
-    )(slots, *blocks, *blocks, *vectors)
-
-
-def edge_jacobian_kernel(slots, place, beside, below, within, partial, lowers, sides, jac):
+            precond[slots[s, p]] = solved[p, s]
+
+
+def edge_jacobian_kernel(slots, place, beside, below, within, partial_a, partial_b, lowers, sides, jac):
     even = lax.rem(place[1], 2) == 0
     low = [jnp.where(even, beside[s], within[s]) for s in range(2)]
     high = [jnp.where(even, within[s], beside[s]) for s in range(2)]
@@ -430,7 +405,7 @@
     start = jnp.where(place[0] == 0, 0.0, 1.0).astype(F32)
     for s in range(2):
         for p in range(GROUP):
-            total = partial[p, s]
+            total = partial_a[p, s] if p < 2 else partial_b[p - 2, s]
             if s == 0:
                 total = total + start * mm(lowers[p], below[p])
             if p == 0:
@@ -469,28 +444,27 @@
         return lax.ppermute(values, "sweep", [(i, i ^ distance) for i in range(count)])
 
     low_pair, high_pair, outer, inner = (1, 0, 2, 3), (0, 1, 3, 2), (1, 0, 3, 2), (0, 2, 1, 3)
-    vec = ((n, cols), BF)
+    vec, vec32, mat = ((n, cols), BF), ((n, cols), F32), ((n, n), BF)
     maps = [None] * GROUP
     for distance in (3, 1, 2):
         piece = local_map(elem_slot, place, inverse, lower, upper, source, distance)
         maps[distance] = to_peer(piece, distance)
-    maps[0], first_ops, second_ops, c_own, y_own = prepare(
-        elem_slot, place, inverse, lower, upper, source
+    maps[0], first_ops, second_ops, c_own, y_own, rows, lowers, sides = prepare(
+        elem_slot, place, inverse, lower, upper, source, diagonal, minus, plus
     )
     pieces = (maps[3], maps[1], maps[2], maps[0])
 
-    (send,) = whole_call(group_front_kernel, [vec], [place], *pieces, name="group_front")
+    a_low, b_low, c_low, g, h, send_far = whole_call(
+        group_back_kernel, [mat, mat, vec32, mat, vec32, ((n + packed_rows(n), cols), BF)],
+        [place], *pieces, name="group_back",
+    )
+    far = swap(send_far, high_pair)
+    send, a, b, c = whole_call(
+        group_front_kernel, [vec, mat, mat, vec32], [place],
+        *pieces, a_low, b_low, c_low, name="group_front",
+    )
     hop1 = swap(send, low_pair)
-    a, b, g, c, h, send_far = whole_call(
-        group_map_kernel,
-        [
-            ((n, n), BF), ((n, n), BF), ((n, n), BF), ((n, cols), F32), ((n, cols), F32),
-            ((n + packed_rows(n), cols), BF),
-        ],
-        [place], *pieces, name="group_map",
-    )
-    far = swap(send_far, high_pair)
-    (send,) = whole_call(forward_one_kernel, [vec], [], hop1, a, c, name="forward_one", cost=LONG)
+    (send,) = whole_call(forward_one_kernel, [vec], [], hop1, a, c, name="forward_one")
     hop2 = swap(send, inner)
     send, ahead, back2 = whole_call(
         turn_kernel, [vec, vec, vec], [], hop2, far, a, b, g, c, h, name="turn"
@@ -507,8 +481,8 @@
     ends = lax.all_to_all(ends, "sweep", 0, 0, axis_index_groups=groups)
 
     pair = ((2, n, cols), BF)
-    within, beside, tops, solved = whole_call(
-        finish_kernel, [pair, pair, ((GROUP, n, cols), BF), ((GROUP, 2, n, cols), BF)], [place],
+    beside, tops, solved = whole_call(
+        finish_kernel, [pair, ((GROUP, n, cols), BF), ((GROUP, 2, n, cols), BF)], [place],
         ends, first_ops, second_ops, c_own, y_own, name="finish",
     )
     aside = [(across - 1, across - 1), (0, 0)]
@@ -516,13 +490,18 @@
         aside += [(i, i + 1), (i + 1, i)]
     beside = lax.ppermute(beside, "cross", aside)
     below = lax.ppermute(tops, "sweep", [(i, (i + 1) % count) for i in range(count)])
+    part = ((2, 2, n, cols), F32)
+    within, partial_a = whole_call(
+        first_rows_kernel, [pair, part], [place], rows, solved, ends, name="first_rows"
+    )
     within = lax.ppermute(within, "cross", [(i, i ^ 1) for i in range(across)])
-    precond, partial, lowers, sides = inner_jacobian(
-        elem_slot, (diagonal, lower, upper, minus, plus), (solved, ends)
+    every = ((2 * GROUP, n, cols), BF)
+    precond, partial_b = whole_call(
+        second_rows_kernel, [every, part], [elem_slot], rows, solved, ends, name="second_rows"
     )
     (jac,) = whole_call(
-        edge_jacobian_kernel, [((2 * GROUP, n, cols), BF)], [elem_slot, place],
-        beside, below, within, partial, lowers, sides, name="edge_jacobian",
+        edge_jacobian_kernel, [every], [elem_slot, place],
+        beside, below, within, partial_a, partial_b, lowers, sides, name="edge_jacobian",
     )
     return precond.reshape(right_side.shape), jac.reshape(right_side.shape)
 

time: 120 us -> 119 us (level)
  starting transfers between devices: 40.4 us -> 33.6 us
  blocking collectives: 13.9 us -> 18.1 us
  waiting for transfers between devices: 19 us -> 22.1 us
    pallas_call x1 -> x0, Pallas kernels: 7.88 us -> none  [inner_jacobian(): pl.pallas_call(inner_jacobian_kernel, grid_spec=pltpu.PrefetchScalarGridS...]
    ppermute x5, starting transfers between devices: 30.6 us -> 23.8 us  [swap(): return lax.ppermute(values, 'sweep', pairs)]
    ppermute x5, waiting for transfers between devices: 2.43 us -> 6.8 us  [swap(): return lax.ppermute(values, 'sweep', pairs)]
    all_to_all x1, blocking collectives: 13.9 us -> 18.1 us  [local(): ends = lax.all_to_all(ends, 'sweep', 0, 0, axis_index_groups=groups)]
    pallas_call x8 -> x10, Pallas kernels: 14.5 us -> 18.7 us  [whole_call(): pl.pallas_call(kernel, in_specs=specs, out_specs=[pl.BlockSpec(memory_spa...]
    ppermute x3, waiting for transfers between devices: 16.5 us -> 13.6 us  [to_peer(): lax.ppermute(values, 'sweep', [(i, i ^ distance) for i in range(count)])]
    pallas_call x1, Pallas kernels: 9.22 us -> 12.2 us  [prepare(): pl.pallas_call(prepare_kernel, grid_spec=pltpu.PrefetchScalarGridSpec(num...]
  transfers between devices with their start and end apart: 11 -> 11, of which waited for: 3 -> 5; matrix products, arithmetic and copies ran while one was open for 0% -> 0% of each run, Pallas kernels for 25% -> 22%
where the time goes in v6:
time: 119 us; the launch traced here: 117 us
  Pallas kernels  41.7 us (35%)
  starting transfers between devices  33.6 us (28%)
  waiting for transfers between devices  22.1 us (19%)
  blocking collectives  18.1 us (15%)
    ppermute x5, starting transfers between devices, swap(): return lax.ppermute(values, 'sweep', pairs)  23.8 us
    pallas_call x10, Pallas kernels, whole_call(): pl.pallas_call(kernel, in_specs=specs, out_specs=[pl.BlockSpec(memory_spa...  18.7 us
    all_to_all x1, blocking collectives, local(): ends = lax.all_to_all(ends, 'sweep', 0, 0, axis_index_groups=groups)  18.1 us
    ppermute x3, waiting for transfers between devices, to_peer(): lax.ppermute(values, 'sweep', [(i, i ^ distance) for i in range(count)])  13.6 us
    pallas_call x1, Pallas kernels, prepare(): pl.pallas_call(prepare_kernel, grid_spec=pltpu.PrefetchScalarGridSpec(num...  12.2 us
    pallas_call x3, Pallas kernels, element_call(): pl.pallas_call(kernel, grid_spec=pltpu.PrefetchScalarGridSpec(num_scalar_...  10.9 us
    ppermute x5, waiting for transfers between devices, swap(): return lax.ppermute(values, 'sweep', pairs)  6.8 us
    ppermute x3, starting transfers between devices, to_peer(): lax.ppermute(values, 'sweep', [(i, i ^ distance) for i in range(count)])  5.26 us
  transfers between devices with their start and end apart: 11, of which 5 were waited for; matrix products, arithmetic and copies ran while one was open for 0% of the time, Pallas kernels for 22%

profile of v6, /device:TPU:8, one launch (start us, length us, event | category | flops | bytes accessed | tf_op | source)
XLA Modules:
  0.0 117.1 jit_solution(4192770277655392653)
XLA Ops:
  1.4 3.6 %local_map.3 = bf16[3040,128]{1,0:T(8,128)(2,1)S(1)} custom-call(s32[2,4]{1,0:T(2,128)S(1)} %copy-done, s32[5]{0:T(128)S(1)} %stack.19.place, bf16[8,320,320]{2,1,0:T(8,128)(2,1)} %bitcast.13, bf16[8,320,320]{2,1,0:T(8,128)(2,1)} %bitcast.14, bf16[8,320,320]{2,1,0:T(8,128)(2,1)} %bitcast.21, bf16[8,320,320]{2,1,0:T(8,128)(2,1)} %bitcast.22, ...), custom_call_target="tpu_custom_call" | custom-call | flops 1024 | bytes 1024 | tf_op jit(solution)/shard_map/local_map/pallas_call | solution.py:89
  5.0 3.7 %collective-permute-start = (bf16[3040,128]{1,0:T(8,128)(2,1)S(1)}, bf16[3040,128]{1,0:T(8,128)(2,1)S(1)}, u32[]{:S(2)}, u32[]{:S(2)}) collective-permute-start(bf16[3040,128]{1,0:T(8,128)(2,1)S(1)} %local_map.3), channel_id=1, source_target_pairs={{0,48},{16,32},{32,16},{48,0},{64,112},{80,96},{96,80},{112,64},{1... | collective-permute-start | bytes 2334728 | tf_op jit(solution)/shard_map/ppermute | solution.py:444
  8.8 3.6 %local_map.4 = bf16[3040,128]{1,0:T(8,128)(2,1)S(1)} custom-call(s32[2,4]{1,0:T(2,128)S(1)} %copy-done, s32[5]{0:T(128)S(1)} %stack.19.place, bf16[8,320,320]{2,1,0:T(8,128)(2,1)} %bitcast.15, bf16[8,320,320]{2,1,0:T(8,128)(2,1)} %bitcast.16, bf16[8,320,320]{2,1,0:T(8,128)(2,1)} %bitcast.23, bf16[8,320,320]{2,1,0:T(8,128)(2,1)} %bitcast.24, ...), custom_call_target="tpu_custom_call" | custom-call | flops 1024 | bytes 1024 | tf_op jit(solution)/shard_map/local_map/pallas_call | solution.py:89
  12.4 1.3 %collective-permute-start.1 = (bf16[3040,128]{1,0:T(8,128)(2,1)S(1)}, bf16[3040,128]{1,0:T(8,128)(2,1)S(1)}, u32[]{:S(2)}, u32[]{:S(2)}) collective-permute-start(bf16[3040,128]{1,0:T(8,128)(2,1)S(1)} %local_map.4), channel_id=1, source_target_pairs={{0,16},{16,0},{32,48},{48,32},{64,80},{80,64},{96,112},{112,96},{1... | collective-permute-start | bytes 2334728 | tf_op jit(solution)/shard_map/ppermute | solution.py:444
  13.7 3.6 %local_map.5 = bf16[3040,128]{1,0:T(8,128)(2,1)S(1)} custom-call(s32[2,4]{1,0:T(2,128)S(1)} %copy-done, s32[5]{0:T(128)S(1)} %stack.19.place, bf16[8,320,320]{2,1,0:T(8,128)(2,1)} %bitcast.17, bf16[8,320,320]{2,1,0:T(8,128)(2,1)} %bitcast.18, bf16[8,320,320]{2,1,0:T(8,128)(2,1)} %bitcast.25, bf16[8,320,320]{2,1,0:T(8,128)(2,1)} %bitcast.26, ...), custom_call_target="tpu_custom_call" | custom-call | flops 1024 | bytes 1024 | tf_op jit(solution)/shard_map/local_map/pallas_call | solution.py:89
  17.6 12.2 %prepare.1 = (bf16[3040,128]{1,0:T(8,128)(2,1)S(1)}, bf16[4,320,1280]{2,1,0:T(8,128)(2,1)S(1)}, bf16[4,320,1600]{2,1,0:T(8,128)(2,1)S(1)}, f32[4,320,128]{2,1,0:...) custom-call(s32[2,4]{1,0:T(2,128)S(1)} %copy-done, ...), custom_call_target="tpu_custom_call" | custom-call | flops 1024 | bytes 1024 | tf_op jit(solution)/shard_map/prepare/pallas_call | solution.py:185
  29.7 13.6 %collective-permute-done.1.near = bf16[3040,128]{1,0:T(8,128)(2,1)S(1)} collective-permute-done((bf16[3040,128]{1,0:T(8,128)(2,1)S(1)}, bf16[3040,128]{1,0:T(8,128)(2,1)S(1)}, u32[]{:S(2)}, u32[]{:S(2)}) %collective-permute-start.1) | collective-permute-done | bytes 778272 | tf_op jit(solution)/shard_map/ppermute | solution.py:444
  43.3 3.5 %group_back.1 = (bf16[320,320]{1,0:T(8,128)(2,1)S(1)}, bf16[320,320]{1,0:T(8,128)(2,1)S(1)}, f32[320,128]{1,0:T(8,128)S(1)}, bf16[320,320]{1,0:T(8,128)(2,1)S(1)...) custom-call(s32[5]{0:T(128)S(1)} %stack.19.place, bf16[3040,128]{1,0:T(8,128)(2,1)S(1)} %collective-permute-done.across, ...), custom_call_target="tpu_custom_call" | custom-call | flops 1024 | bytes 1024 | tf_op jit(solution)/shard_map/group_back/pallas_call | solution.py:337
  47.5 1.6 %group_front.1 = (bf16[320,128]{1,0:T(8,128)(2,1)S(1)}, bf16[320,320]{1,0:T(8,128)(2,1)S(1)}, bf16[320,320]{1,0:T(8,128)(2,1)S(1)}, f32[320,128]{1,0:T(8,128)S(1)}) custom-call(s32[5]{0:T(128)S(1)} %stack.19.place, bf16[3040,128]{1,0:T(8,128)(2,1)S(1)} %collective-permute-done.across, bf16[3040,128]{1,0:T(8,128)(2,1)S(1)} %collective-permute-done.1.near, ...), custom_call_target="tpu_custom_call" | custom-call | flops 1024 | bytes 1024 | tf_op jit(solution)/shard_map/group_front/pallas_call | solution.py:337
  49.1 5.2 %collective-permute-start.3 = (bf16[320,128]{1,0:T(8,128)(2,1)S(1)}, bf16[320,128]{1,0:T(8,128)(2,1)S(1)}, u32[]{:S(2)}, u32[]{:S(2)}) collective-permute-start(bf16[320,128]{1,0:T(8,128)(2,1)S(1)} %get-tuple-element.35), channel_id=1, source_target_pairs={{0,64},{16,80},{32,96},{48,112},{64,0},{80,16},{96,32},{112,48},{1... | collective-permute-start | bytes 245768 | tf_op jit(solution)/shard_map/ppermute | solution.py:441
  54.3 4.4 %collective-permute-done.3.incoming.hop1 = bf16[320,128]{1,0:T(8,128)(2,1)S(1)} collective-permute-done((bf16[320,128]{1,0:T(8,128)(2,1)S(1)}, bf16[320,128]{1,0:T(8,128)(2,1)S(1)}, u32[]{:S(2)}, u32[]{:S(2)}) %collective-permute-start.3) | collective-permute-done | bytes 81952 | tf_op jit(solution)/shard_map/ppermute | solution.py:441
  59.6 0.8 turn.1
  61.9 16.6 %collective-permute-start.7 = (bf16[320,128]{1,0:T(8,128)(2,1)S(1)}, bf16[320,128]{1,0:T(8,128)(2,1)S(1)}, u32[]{:S(2)}, u32[]{:S(2)}) collective-permute-start(bf16[320,128]{1,0:T(8,128)(2,1)S(1)} %backward_one.1), channel_id=1, source_target_pairs={{0,64},{16,80},{32,96},{48,112},{64,0},{80,16},{96,32},{112,48},{1... | collective-permute-start | bytes 245768 | tf_op jit(solution)/shard_map/ppermute | solution.py:441
  78.5 2.4 %collective-permute-done.7.hop4 = bf16[320,128]{1,0:T(8,128)(2,1)S(1)} collective-permute-done((bf16[320,128]{1,0:T(8,128)(2,1)S(1)}, bf16[320,128]{1,0:T(8,128)(2,1)S(1)}, u32[]{:S(2)}, u32[]{:S(2)}) %collective-permute-start.7) | collective-permute-done | bytes 81952 | tf_op jit(solution)/shard_map/ppermute | solution.py:441
  80.9 2.5 %interfaces.1 = bf16[4,640,128]{2,1,0:T(8,128)(2,1)S(1)} custom-call(s32[5]{0:T(128)S(1)} %stack.19.place, bf16[3040,128]{1,0:T(8,128)(2,1)S(1)} %collective-permute-done.across, bf16[3040,128]{1,0:T(8,128)(2,1)S(1)} %collective-permute-done.1.near, bf16[3040,128]{1,0:T(8,128)(2,1)S(1)} %collective-permute-done.2.next_one, ...), custom_call_target="tpu_custom_call" | custom-call | flops 1024 | bytes 1024 | tf_op jit(solution)/shard_map/interfaces/pallas_call | solution.py:337
  83.4 18.1 %all_to_all.5.ends = bf16[4,640,128]{2,1,0:T(8,128)(2,1)S(1)} all-to-all(bf16[4,640,128]{2,1,0:T(8,128)(2,1)S(1)} %interfaces.1), channel_id=1, replica_groups={{0,16,32,48},{64,80,96,112},{128,144,160,176},{192,208,224,240},{1,17,3..., dimensions={0} | all-to-all | bytes 1310720 | tf_op jit(solution)/shard_map/all_to_all | solution.py:481
  101.5 2.8 %finish.1 = (bf16[2,320,128]{2,1,0:T(8,128)(2,1)S(1)}, bf16[4,320,128]{2,1,0:T(8,128)(2,1)S(1)}, bf16[4,2,320,128]{3,2,1,0:T(8,128)(2,1)S(1)}) custom-call(s32[5]{0:T(128)S(1)} %stack.19.place, bf16[4,640,128]{2,1,0:T(8,128)(2,1)S(1)} %all_to_all.5.ends, bf16[4,320,1280]{2,1,0:T(8,128)(2,1)S(1)} %get-tuple-element.45.first_ops, ...), custom_call_target="tpu_custom_call" | custom-call | flops 1024 | bytes 1024 | tf_op jit(solution)/shard_map/finish/pallas_call | solution.py:337
  104.2 1.0 collective-permute-start.9
  105.2 1.9 %collective-permute-start.8 = (bf16[2,320,128]{2,1,0:T(8,128)(2,1)S(1)}, bf16[2,320,128]{2,1,0:T(8,128)(2,1)S(1)}, u32[]{:S(2)}, u32[]{:S(2)}) collective-permute-start(bf16[2,320,128]{2,1,0:T(8,128)(2,1)S(1)} %get-tuple-element.51), channel_id=1, source_target_pairs={{15,15},{0,0},{1,2},{2,1},{3,4},{4,3},{5,6},{6,5},{7,8},{8,7},{9,1... | collective-permute-start | bytes 491528 | tf_op jit(solution)/shard_map/ppermute | solution.py:491
  107.2 1.8 %first_rows.1 = (bf16[2,320,128]{2,1,0:T(8,128)(2,1)S(1)}, f32[2,2,320,128]{3,2,1,0:T(8,128)S(1)}) custom-call(s32[5]{0:T(128)S(1)} %stack.19.place, bf16[4,2,320,1600]{3,2,1,0:T(8,128)(2,1)S(1)} %get-tuple-element.30.rows, bf16[4,2,320,128]{3,2,1,0:T(8,128)(2,1)S(1)} %get-tuple-element.49.solved, bf16[4,640,128]{2,1,0:T(8,128)(2,1)S(1)} %all_to_all.5.ends), custom_call_target="tpu_custom_call" | custom-call | flops 1024 | bytes 1024 | tf_op jit(solution)/shard_map/first_rows/pallas_call | solution.py:337
  109.0 1.7 %collective-permute-start.10 = (bf16[2,320,128]{2,1,0:T(8,128)(2,1)S(1)}, bf16[2,320,128]{2,1,0:T(8,128)(2,1)S(1)}, u32[]{:S(2)}, u32[]{:S(2)}) collective-permute-start(bf16[2,320,128]{2,1,0:T(8,128)(2,1)S(1)} %get-tuple-element.53), channel_id=1, source_target_pairs={{0,1},{1,0},{2,3},{3,2},{4,5},{5,4},{6,7},{7,6},{8,9},{9,8},{10,11... | collective-permute-start | bytes 491528 | tf_op jit(solution)/shard_map/ppermute | solution.py:497
  110.6 2.6 %second_rows.1 = (bf16[8,320,128]{2,1,0:T(8,128)(2,1)}, f32[2,2,320,128]{3,2,1,0:T(8,128)S(1)}) custom-call(s32[2,4]{1,0:T(2,128)S(1)} %copy-done.1, bf16[4,2,320,1600]{3,2,1,0:T(8,128)(2,1)S(1)} %get-tuple-element.30.rows, bf16[4,2,320,128]{3,2,1,0:T(8,128)(2,1)S(1)} %get-tuple-element.49.solved, bf16[4,640,128]{2,1,0:T(8,128)(2,1)S(1)} %all_to_all.5.ends), custom_call_target="tpu_custom_call" | custom-call | flops 1024 | bytes 1024 | tf_op jit(solution)/shard_map/second_rows/pallas_call | solution.py:337
  114.0 1.0 collective-permute-done.9.below
  115.0 2.1 %edge_jacobian.1 = bf16[8,320,128]{2,1,0:T(8,128)(2,1)} custom-call(s32[2,4]{1,0:T(2,128)S(1)} %copy-done.1, s32[5]{0:T(128)S(1)} %stack.19.place, bf16[2,320,128]{2,1,0:T(8,128)(2,1)S(1)} %collective-permute-done.8.beside, bf16[4,320,128]{2,1,0:T(8,128)(2,1)S(1)} %collective-permute-done.9.below, bf16[2,320,128]{2,1,0:T(8,128)(2,1)S(1)} %collective-permute-done.10.within, ...), custom_call_target="tpu_custom_call" | custom-call | flops 1024 | bytes 1024 | tf_op jit(solution)/shard_map/edge_jacobian/pallas_call | solution.py:337
  (18 shorter events, 4.8 us)
Async XLA Ops:
  0.7 0.7 copy-start
  5.0 24.7 %collective-permute-start = (bf16[3040,128]{1,0:T(8,128)(2,1)S(1)}, bf16[3040,128]{1,0:T(8,128)(2,1)S(1)}, u32[]{:S(2)}, u32[]{:S(2)}) collective-permute-start(bf16[3040,128]{1,0:T(8,128)(2,1)S(1)} %local_map.3), channel_id=1, source_target_pairs={{0,48},{16,32},{32,16},{48,0},{64,112},{80,96},{96,80},{112,64},{1... | collective-permute-start | bytes 2334728 | tf_op jit(solution)/shard_map/ppermute | solution.py:444
  12.4 30.9 %collective-permute-start.1 = (bf16[3040,128]{1,0:T(8,128)(2,1)S(1)}, bf16[3040,128]{1,0:T(8,128)(2,1)S(1)}, u32[]{:S(2)}, u32[]{:S(2)}) collective-permute-start(bf16[3040,128]{1,0:T(8,128)(2,1)S(1)} %local_map.4), channel_id=1, source_target_pairs={{0,16},{16,0},{32,48},{48,32},{64,80},{80,64},{96,112},{112,96},{1... | collective-permute-start | bytes 2334728 | tf_op jit(solution)/shard_map/ppermute | solution.py:444
  17.3 26.0 %collective-permute-start.2 = (bf16[3040,128]{1,0:T(8,128)(2,1)S(1)}, bf16[3040,128]{1,0:T(8,128)(2,1)S(1)}, u32[]{:S(2)}, u32[]{:S(2)}) collective-permute-start(bf16[3040,128]{1,0:T(8,128)(2,1)S(1)} %local_map.5), channel_id=1, source_target_pairs={{0,32},{16,48},{32,0},{48,16},{64,96},{80,112},{96,64},{112,80},{1... | collective-permute-start | bytes 2334728 | tf_op jit(solution)/shard_map/ppermute | solution.py:444
  46.8 12.8 %collective-permute-start.5 = (bf16[1120,128]{1,0:T(8,128)(2,1)S(1)}, bf16[1120,128]{1,0:T(8,128)(2,1)S(1)}, u32[]{:S(2)}, u32[]{:S(2)}) collective-permute-start(bf16[1120,128]{1,0:T(8,128)(2,1)S(1)} %get-tuple-element.38), channel_id=1, source_target_pairs={{0,0},{16,16},{32,32},{48,48},{64,64},{80,80},{96,96},{112,112},{1... | collective-permute-start | bytes 860168 | tf_op jit(solution)/shard_map/ppermute | solution.py:441
  49.1 9.6 %collective-permute-start.3 = (bf16[320,128]{1,0:T(8,128)(2,1)S(1)}, bf16[320,128]{1,0:T(8,128)(2,1)S(1)}, u32[]{:S(2)}, u32[]{:S(2)}) collective-permute-start(bf16[320,128]{1,0:T(8,128)(2,1)S(1)} %get-tuple-element.35), channel_id=1, source_target_pairs={{0,64},{16,80},{32,96},{48,112},{64,0},{80,16},{96,32},{112,48},{1... | collective-permute-start | bytes 245768 | tf_op jit(solution)/shard_map/ppermute | solution.py:441
  58.9 0.7 collective-permute-start.4
  60.4 0.7 collective-permute-start.6
  61.9 19.0 %collective-permute-start.7 = (bf16[320,128]{1,0:T(8,128)(2,1)S(1)}, bf16[320,128]{1,0:T(8,128)(2,1)S(1)}, u32[]{:S(2)}, u32[]{:S(2)}) collective-permute-start(bf16[320,128]{1,0:T(8,128)(2,1)S(1)} %backward_one.1), channel_id=1, source_target_pairs={{0,64},{16,80},{32,96},{48,112},{64,0},{80,16},{96,32},{112,48},{1... | collective-permute-start | bytes 245768 | tf_op jit(solution)/shard_map/ppermute | solution.py:441
  104.2 10.8 %collective-permute-start.9 = (bf16[4,320,128]{2,1,0:T(8,128)(2,1)S(1)}, bf16[4,320,128]{2,1,0:T(8,128)(2,1)S(1)}, u32[]{:S(2)}, u32[]{:S(2)}) collective-permute-start(bf16[4,320,128]{2,1,0:T(8,128)(2,1)S(1)} %get-tuple-element.52), channel_id=1, source_target_pairs={{0,16},{16,32},{32,48},{48,64},{64,80},{80,96},{96,112},{112,128},... | collective-permute-start | bytes 983048 | tf_op jit(solution)/shard_map/ppermute | solution.py:492
  105.2 8.7 %collective-permute-start.8 = (bf16[2,320,128]{2,1,0:T(8,128)(2,1)S(1)}, bf16[2,320,128]{2,1,0:T(8,128)(2,1)S(1)}, u32[]{:S(2)}, u32[]{:S(2)}) collective-permute-start(bf16[2,320,128]{2,1,0:T(8,128)(2,1)S(1)} %get-tuple-element.51), channel_id=1, source_target_pairs={{15,15},{0,0},{1,2},{2,1},{3,4},{4,3},{5,6},{6,5},{7,8},{8,7},{9,1... | collective-permute-start | bytes 491528 | tf_op jit(solution)/shard_map/ppermute | solution.py:491
  107.2 3.5 %copy-start.1 = (s32[2,4]{1,0:T(2,128)S(1)}, s32[2,4]{1,0:T(2,128)}, u32[]{:S(2)}) copy-start(s32[2,4]{1,0:T(2,128)} %slots.11) | copy-start | bytes 100
  109.0 5.0 %collective-permute-start.10 = (bf16[2,320,128]{2,1,0:T(8,128)(2,1)S(1)}, bf16[2,320,128]{2,1,0:T(8,128)(2,1)S(1)}, u32[]{:S(2)}, u32[]{:S(2)}) collective-permute-start(bf16[2,320,128]{2,1,0:T(8,128)(2,1)S(1)} %get-tuple-element.53), channel_id=1, source_target_pairs={{0,1},{1,0},{2,3},{3,2},{4,5},{5,4},{6,7},{7,6},{8,9},{9,8},{10,11... | collective-permute-start | bytes 491528 | tf_op jit(solution)/shard_map/ppermute | solution.py:497

commit v7 on v6

--- a/solution.py
+++ b/solution.py
@@ -345,36 +345,35 @@
     )(*scalars, *operands)
 
 
-def finish_kernel(place, ends, first_ops, second_ops, c, y0, beside, tops, solved):
+def finish_second_kernel(ends, first_ops, c, tops, rests):
     n = c.shape[1]
-    every = range(GROUP)
-    fronts = [ends[p, 0:n, :] for p in every]
-    backs = [ends[p, n : 2 * n, :] for p in every]
-    x1 = [
-        c[p] + mm(first_ops[p], jnp.concatenate([fronts[p], fronts[p], backs[p], backs[p]], axis=0))
-        for p in every
-    ]
-    for p in every:
-        top, rest = halves(x1[p])
-        x0 = y0[p] + mm(
-            second_ops[p], jnp.concatenate([fronts[p], fronts[p], top, top, rest], axis=0)
-        )
-        solved[p, 0] = x0.astype(BF)
-        solved[p, 1] = top
-        tops[p] = top
+    for p in range(GROUP):
+        front = ends[p, 0:n, :]
+        back = ends[p, n : 2 * n, :]
+        x1 = c[p] + mm(first_ops[p], jnp.concatenate([front, front, back, back], axis=0))
+        tops[p], rests[p] = halves(x1)
+
+
+def finish_first_kernel(place, ends, second_ops, y0, tops, rests, beside, firsts):
+    n = y0.shape[1]
+    for p in range(GROUP):
+        front = ends[p, 0:n, :]
+        top = tops[p]
+        around = jnp.concatenate([front, front, top, top, rests[p]], axis=0)
+        firsts[p] = (y0[p] + mm(second_ops[p], around)).astype(BF)
     even = lax.rem(place[1], 2) == 0
-    for s in range(2):
-        beside[s] = jnp.where(even, solved[0, s], solved[GROUP - 1, s])
-
-
-def row_products(chosen, rows, solved, ends, partial):
-    n = solved.shape[2]
-    zero = jnp.zeros(solved.shape[2:], BF)
+    for s, values in enumerate((firsts, tops)):
+        beside[s] = jnp.where(even, values[0], values[GROUP - 1])
+
+
+def row_products(chosen, rows, firsts, tops, ends, partial):
+    n = tops.shape[1]
+    zero = jnp.zeros(tops.shape[1:], BF)
 
     def value(s, p):
         if p < 0 or p >= GROUP or s < 0:
             return zero
-        return ends[p, n : 2 * n, :] if s == 2 else solved[p, s]
+        return ends[p, n : 2 * n, :] if s == 2 else (firsts, tops)[s][p]
 
     for i, p in enumerate(chosen):
         for s in range(2):
@@ -382,18 +381,18 @@
             partial[i, s] = mm(rows[p, s], jnp.concatenate(around, axis=0))
 
 
-def first_rows_kernel(place, rows, solved, ends, within, partial):
+def first_rows_kernel(place, rows, firsts, tops, ends, within, partial):
     even = lax.rem(place[1], 2) == 0
-    row_products((0, 1), rows, solved, ends, partial)
-    for s in range(2):
-        within[s] = jnp.where(even, solved[GROUP - 1, s], solved[0, s])
-
-
-def second_rows_kernel(slots, rows, solved, ends, precond, partial):
-    row_products((2, 3), rows, solved, ends, partial)
+    row_products((0, 1), rows, firsts, tops, ends, partial)
+    for s, values in enumerate((firsts, tops)):
+        within[s] = jnp.where(even, values[GROUP - 1], values[0])
+
+
+def second_rows_kernel(slots, rows, firsts, tops, ends, precond, partial):
+    row_products((2, 3), rows, firsts, tops, ends, partial)
     for s in range(2):
         for p in range(GROUP):
-            precond[slots[s, p]] = solved[p, s]
+            precond[slots[s, p]] = (firsts, tops)[s][p]
 
 
 def edge_jacobian_kernel(slots, place, beside, below, within, partial_a, partial_b, lowers, sides, jac):
@@ -436,14 +435,13 @@
     ).astype(jnp.int32)
     groups = [list(range(g, g + GROUP)) for g in range(0, count, GROUP)]
 
-    def swap(values, order):
-        pairs = [(g * GROUP + k, order[g] * GROUP + k) for g in range(GROUP) for k in range(GROUP)]
+    def hop(values, *moves):
+        pairs = [(a * GROUP + k, b * GROUP + k) for a, b in moves for k in range(GROUP)]
         return lax.ppermute(values, "sweep", pairs)
 
     def to_peer(values, distance):
         return lax.ppermute(values, "sweep", [(i, i ^ distance) for i in range(count)])
 
-    low_pair, high_pair, outer, inner = (1, 0, 2, 3), (0, 1, 3, 2), (1, 0, 3, 2), (0, 2, 1, 3)
     vec, vec32, mat = ((n, cols), BF), ((n, cols), F32), ((n, n), BF)
     maps = [None] * GROUP
     for distance in (3, 1, 2):
@@ -458,22 +456,22 @@
         group_back_kernel, [mat, mat, vec32, mat, vec32, ((n + packed_rows(n), cols), BF)],
         [place], *pieces, name="group_back",
     )
-    far = swap(send_far, high_pair)
+    far = hop(send_far, (3, 2))
     send, a, b, c = whole_call(
         group_front_kernel, [vec, mat, mat, vec32], [place],
         *pieces, a_low, b_low, c_low, name="group_front",
     )
-    hop1 = swap(send, low_pair)
+    hop1 = hop(send, (0, 1))
     (send,) = whole_call(forward_one_kernel, [vec], [], hop1, a, c, name="forward_one")
-    hop2 = swap(send, inner)
+    hop2 = hop(send, (1, 2))
     send, ahead, back2 = whole_call(
         turn_kernel, [vec, vec, vec], [], hop2, far, a, b, g, c, h, name="turn"
     )
-    hop3 = swap(send, inner)
+    hop3 = hop(send, (2, 1))
     (send,) = whole_call(
         backward_one_kernel, [vec], [place], b, g, h, hop1, hop3, ahead, name="backward_one"
     )
-    hop4 = swap(send, outer)
+    hop4 = hop(send, (1, 0), (2, 3))
     (ends,) = whole_call(
         interfaces_kernel, [((GROUP, 2 * n, cols), BF)], [place],
         *pieces, hop1, hop2, hop3, back2, hop4, name="interfaces",
@@ -481,23 +479,27 @@
     ends = lax.all_to_all(ends, "sweep", 0, 0, axis_index_groups=groups)
 
     pair = ((2, n, cols), BF)
-    beside, tops, solved = whole_call(
-        finish_kernel, [pair, ((GROUP, n, cols), BF), ((GROUP, 2, n, cols), BF)], [place],
-        ends, first_ops, second_ops, c_own, y_own, name="finish",
-    )
-    aside = [(across - 1, across - 1), (0, 0)]
+    four = ((GROUP, n, cols), BF)
+    tops, rests = whole_call(
+        finish_second_kernel, [four, four], [], ends, first_ops, c_own, name="finish_second"
+    )
+    below = lax.ppermute(tops, "sweep", [(i, (i + 1) % count) for i in range(count)])
+    beside, firsts = whole_call(
+        finish_first_kernel, [pair, four], [place],
+        ends, second_ops, y_own, tops, rests, name="finish_first",
+    )
+    aside = []
     for i in range(1, across - 1, 2):
         aside += [(i, i + 1), (i + 1, i)]
     beside = lax.ppermute(beside, "cross", aside)
-    below = lax.ppermute(tops, "sweep", [(i, (i + 1) % count) for i in range(count)])
     part = ((2, 2, n, cols), F32)
     within, partial_a = whole_call(
-        first_rows_kernel, [pair, part], [place], rows, solved, ends, name="first_rows"
+        first_rows_kernel, [pair, part], [place], rows, firsts, tops, ends, name="first_rows"
     )
     within = lax.ppermute(within, "cross", [(i, i ^ 1) for i in range(across)])
     every = ((2 * GROUP, n, cols), BF)
     precond, partial_b = whole_call(
-        second_rows_kernel, [every, part], [elem_slot], rows, solved, ends, name="second_rows"
+        second_rows_kernel, [every, part], [elem_slot], rows, firsts, tops, ends, name="second_rows"
     )
     (jac,) = whole_call(
         edge_jacobian_kernel, [every], [elem_slot, place],

time: 119 us -> 114 us (0.958)
  starting transfers between devices: 33.6 us -> 18.3 us
  waiting for transfers between devices: 22.1 us -> 36.9 us
  blocking collectives: 18.1 us -> 13.9 us
    ppermute x5, waiting for transfers between devices: 6.8 us -> 22.6 us  [hop(): return lax.ppermute(values, 'sweep', pairs)]
    ppermute x5, starting transfers between devices: 23.8 us -> 8.48 us  [hop(): return lax.ppermute(values, 'sweep', pairs)]
    all_to_all x1, blocking collectives: 18.1 us -> 13.9 us  [local(): ends = lax.all_to_all(ends, 'sweep', 0, 0, axis_index_groups=groups)]
    pallas_call x10 -> x11, Pallas kernels: 18.7 us -> 18.8 us  [whole_call(): pl.pallas_call(kernel, in_specs=specs, out_specs=[pl.BlockSpec(memory_spa...]
  transfers between devices with their start and end apart: 11 -> 11, of which waited for: 5 -> 4; matrix products, arithmetic and copies ran while one was open for 0% -> 0% of each run, Pallas kernels for 22% -> 24%
where the time goes in v7:
time: 114 us; the launch traced here: 113 us
  Pallas kernels  41.8 us (37%)
  waiting for transfers between devices  36.9 us (32%)
  starting transfers between devices  18.3 us (16%)
  blocking collectives  13.9 us (12%)
    ppermute x5, waiting for transfers between devices, hop(): return lax.ppermute(values, 'sweep', pairs)  22.6 us
    pallas_call x11, Pallas kernels, whole_call(): pl.pallas_call(kernel, in_specs=specs, out_specs=[pl.BlockSpec(memory_spa...  18.8 us
    all_to_all x1, blocking collectives, local(): ends = lax.all_to_all(ends, 'sweep', 0, 0, axis_index_groups=groups)  13.9 us
    ppermute x3, waiting for transfers between devices, to_peer(): lax.ppermute(values, 'sweep', [(i, i ^ distance) for i in range(count)])  13.6 us
    pallas_call x1, Pallas kernels, prepare(): pl.pallas_call(prepare_kernel, grid_spec=pltpu.PrefetchScalarGridSpec(num...  12.2 us
    pallas_call x3, Pallas kernels, element_call(): pl.pallas_call(kernel, grid_spec=pltpu.PrefetchScalarGridSpec(num_scalar_...  10.9 us
    ppermute x5, starting transfers between devices, hop(): return lax.ppermute(values, 'sweep', pairs)  8.48 us
    ppermute x3, starting transfers between devices, to_peer(): lax.ppermute(values, 'sweep', [(i, i ^ distance) for i in range(count)])  5.26 us
  transfers between devices with their start and end apart: 11, of which 4 were waited for; matrix products, arithmetic and copies ran while one was open for 0% of the time, Pallas kernels for 24%

profile of v7, /device:TPU:8, one launch (start us, length us, event | category | flops | bytes accessed | tf_op | source)
XLA Modules:
  0.0 112.5 jit_solution(7276068408649054426)
XLA Ops:
  1.4 3.6 %local_map.3 = bf16[3040,128]{1,0:T(8,128)(2,1)S(1)} custom-call(s32[2,4]{1,0:T(2,128)S(1)} %copy-done, s32[5]{0:T(128)S(1)} %stack.19.place, bf16[8,320,320]{2,1,0:T(8,128)(2,1)} %bitcast.13, bf16[8,320,320]{2,1,0:T(8,128)(2,1)} %bitcast.14, bf16[8,320,320]{2,1,0:T(8,128)(2,1)} %bitcast.21, bf16[8,320,320]{2,1,0:T(8,128)(2,1)} %bitcast.22, ...), custom_call_target="tpu_custom_call" | custom-call | flops 1024 | bytes 1024 | tf_op jit(solution)/shard_map/local_map/pallas_call | solution.py:89
  5.0 3.7 %collective-permute-start = (bf16[3040,128]{1,0:T(8,128)(2,1)S(1)}, bf16[3040,128]{1,0:T(8,128)(2,1)S(1)}, u32[]{:S(2)}, u32[]{:S(2)}) collective-permute-start(bf16[3040,128]{1,0:T(8,128)(2,1)S(1)} %local_map.3), channel_id=1, source_target_pairs={{0,48},{16,32},{32,16},{48,0},{64,112},{80,96},{96,80},{112,64},{1... | collective-permute-start | bytes 2334728 | tf_op jit(solution)/shard_map/ppermute | solution.py:443
  8.8 3.6 %local_map.4 = bf16[3040,128]{1,0:T(8,128)(2,1)S(1)} custom-call(s32[2,4]{1,0:T(2,128)S(1)} %copy-done, s32[5]{0:T(128)S(1)} %stack.19.place, bf16[8,320,320]{2,1,0:T(8,128)(2,1)} %bitcast.15, bf16[8,320,320]{2,1,0:T(8,128)(2,1)} %bitcast.16, bf16[8,320,320]{2,1,0:T(8,128)(2,1)} %bitcast.23, bf16[8,320,320]{2,1,0:T(8,128)(2,1)} %bitcast.24, ...), custom_call_target="tpu_custom_call" | custom-call | flops 1024 | bytes 1024 | tf_op jit(solution)/shard_map/local_map/pallas_call | solution.py:89
  12.4 1.3 %collective-permute-start.1 = (bf16[3040,128]{1,0:T(8,128)(2,1)S(1)}, bf16[3040,128]{1,0:T(8,128)(2,1)S(1)}, u32[]{:S(2)}, u32[]{:S(2)}) collective-permute-start(bf16[3040,128]{1,0:T(8,128)(2,1)S(1)} %local_map.4), channel_id=1, source_target_pairs={{0,16},{16,0},{32,48},{48,32},{64,80},{80,64},{96,112},{112,96},{1... | collective-permute-start | bytes 2334728 | tf_op jit(solution)/shard_map/ppermute | solution.py:443
  13.7 3.6 %local_map.5 = bf16[3040,128]{1,0:T(8,128)(2,1)S(1)} custom-call(s32[2,4]{1,0:T(2,128)S(1)} %copy-done, s32[5]{0:T(128)S(1)} %stack.19.place, bf16[8,320,320]{2,1,0:T(8,128)(2,1)} %bitcast.17, bf16[8,320,320]{2,1,0:T(8,128)(2,1)} %bitcast.18, bf16[8,320,320]{2,1,0:T(8,128)(2,1)} %bitcast.25, bf16[8,320,320]{2,1,0:T(8,128)(2,1)} %bitcast.26, ...), custom_call_target="tpu_custom_call" | custom-call | flops 1024 | bytes 1024 | tf_op jit(solution)/shard_map/local_map/pallas_call | solution.py:89
  17.6 12.2 %prepare.1 = (bf16[3040,128]{1,0:T(8,128)(2,1)S(1)}, bf16[4,320,1280]{2,1,0:T(8,128)(2,1)S(1)}, bf16[4,320,1600]{2,1,0:T(8,128)(2,1)S(1)}, f32[4,320,128]{2,1,0:...) custom-call(s32[2,4]{1,0:T(2,128)S(1)} %copy-done, ...), custom_call_target="tpu_custom_call" | custom-call | flops 1024 | bytes 1024 | tf_op jit(solution)/shard_map/prepare/pallas_call | solution.py:185
  29.7 13.6 %collective-permute-done.1.near = bf16[3040,128]{1,0:T(8,128)(2,1)S(1)} collective-permute-done((bf16[3040,128]{1,0:T(8,128)(2,1)S(1)}, bf16[3040,128]{1,0:T(8,128)(2,1)S(1)}, u32[]{:S(2)}, u32[]{:S(2)}) %collective-permute-start.1) | collective-permute-done | bytes 778272 | tf_op jit(solution)/shard_map/ppermute | solution.py:443
  43.3 3.5 %group_back.1 = (bf16[320,320]{1,0:T(8,128)(2,1)S(1)}, bf16[320,320]{1,0:T(8,128)(2,1)S(1)}, f32[320,128]{1,0:T(8,128)S(1)}, bf16[320,320]{1,0:T(8,128)(2,1)S(1)...) custom-call(s32[5]{0:T(128)S(1)} %stack.19.place, bf16[3040,128]{1,0:T(8,128)(2,1)S(1)} %collective-permute-done.across, ...), custom_call_target="tpu_custom_call" | custom-call | flops 1024 | bytes 1024 | tf_op jit(solution)/shard_map/group_back/pallas_call | solution.py:337
  47.5 1.6 %group_front.1 = (bf16[320,128]{1,0:T(8,128)(2,1)S(1)}, bf16[320,320]{1,0:T(8,128)(2,1)S(1)}, bf16[320,320]{1,0:T(8,128)(2,1)S(1)}, f32[320,128]{1,0:T(8,128)S(1)}) custom-call(s32[5]{0:T(128)S(1)} %stack.19.place, bf16[3040,128]{1,0:T(8,128)(2,1)S(1)} %collective-permute-done.across, bf16[3040,128]{1,0:T(8,128)(2,1)S(1)} %collective-permute-done.1.near, ...), custom_call_target="tpu_custom_call" | custom-call | flops 1024 | bytes 1024 | tf_op jit(solution)/shard_map/group_front/pallas_call | solution.py:337
  49.1 5.2 %collective-permute-start.3 = (bf16[320,128]{1,0:T(8,128)(2,1)S(1)}, bf16[320,128]{1,0:T(8,128)(2,1)S(1)}, u32[]{:S(2)}, u32[]{:S(2)}) collective-permute-start(bf16[320,128]{1,0:T(8,128)(2,1)S(1)} %get-tuple-element.36), channel_id=1, source_target_pairs={{0,64},{16,80},{32,96},{48,112},{1,65},{17,81},{33,97},{49,113},{2... | collective-permute-start | bytes 245768 | tf_op jit(solution)/shard_map/ppermute | solution.py:440
  54.3 2.0 %collective-permute-done.3.incoming.hop1 = bf16[320,128]{1,0:T(8,128)(2,1)S(1)} collective-permute-done((bf16[320,128]{1,0:T(8,128)(2,1)S(1)}, bf16[320,128]{1,0:T(8,128)(2,1)S(1)}, u32[]{:S(2)}, u32[]{:S(2)}) %collective-permute-start.3) | collective-permute-done | bytes 81952 | tf_op jit(solution)/shard_map/ppermute | solution.py:440
  57.3 0.8 turn.1
  59.6 1.3 %collective-permute-start.7 = (bf16[320,128]{1,0:T(8,128)(2,1)S(1)}, bf16[320,128]{1,0:T(8,128)(2,1)S(1)}, u32[]{:S(2)}, u32[]{:S(2)}) collective-permute-start(bf16[320,128]{1,0:T(8,128)(2,1)S(1)} %backward_one.1), channel_id=1, source_target_pairs={{64,0},{80,16},{96,32},{112,48},{128,192},{144,208},{160,224},{176... | collective-permute-start | bytes 245768 | tf_op jit(solution)/shard_map/ppermute | solution.py:440
  60.9 20.6 %collective-permute-done.7.hop4 = bf16[320,128]{1,0:T(8,128)(2,1)S(1)} collective-permute-done((bf16[320,128]{1,0:T(8,128)(2,1)S(1)}, bf16[320,128]{1,0:T(8,128)(2,1)S(1)}, u32[]{:S(2)}, u32[]{:S(2)}) %collective-permute-start.7) | collective-permute-done | bytes 81952 | tf_op jit(solution)/shard_map/ppermute | solution.py:440
  81.5 2.5 %interfaces.1 = bf16[4,640,128]{2,1,0:T(8,128)(2,1)S(1)} custom-call(s32[5]{0:T(128)S(1)} %stack.19.place, bf16[3040,128]{1,0:T(8,128)(2,1)S(1)} %collective-permute-done.across, bf16[3040,128]{1,0:T(8,128)(2,1)S(1)} %collective-permute-done.1.near, bf16[3040,128]{1,0:T(8,128)(2,1)S(1)} %collective-permute-done.2.next_one, ...), custom_call_target="tpu_custom_call" | custom-call | flops 1024 | bytes 1024 | tf_op jit(solution)/shard_map/interfaces/pallas_call | solution.py:337
  84.0 13.9 %all_to_all.5.ends = bf16[4,640,128]{2,1,0:T(8,128)(2,1)S(1)} all-to-all(bf16[4,640,128]{2,1,0:T(8,128)(2,1)S(1)} %interfaces.1), channel_id=1, replica_groups={{0,16,32,48},{64,80,96,112},{128,144,160,176},{192,208,224,240},{1,17,3..., dimensions={0} | all-to-all | bytes 1310720 | tf_op jit(solution)/shard_map/all_to_all | solution.py:479
  97.8 1.0 finish_second.1
  98.9 1.0 collective-permute-start.9
  99.9 1.8 %finish_first.1 = (bf16[2,320,128]{2,1,0:T(8,128)(2,1)S(1)}, bf16[4,320,128]{2,1,0:T(8,128)(2,1)S(1)}) custom-call(s32[5]{0:T(128)S(1)} %stack.19.place, bf16[4,640,128]{2,1,0:T(8,128)(2,1)S(1)} %all_to_all.5.ends, bf16[4,320,1600]{2,1,0:T(8,128)(2,1)S(1)} %get-tuple-element.46.second_ops, f32[4,320,128]{2,1,0:T(8,128)S(1)} %get-tuple-element.47.y0, ...), custom_call_target="tpu_custom_call" | custom-call | flops 1024 | bytes 1024 | tf_op jit(solution)/shard_map/finish_first/pallas_call | solution.py:337
  101.7 2.5 %collective-permute-start.8 = (bf16[2,320,128]{2,1,0:T(8,128)(2,1)S(1)}, bf16[2,320,128]{2,1,0:T(8,128)(2,1)S(1)}, u32[]{:S(2)}, u32[]{:S(2)}) collective-permute-start(bf16[2,320,128]{2,1,0:T(8,128)(2,1)S(1)} %get-tuple-element.54), channel_id=1, source_target_pairs={{1,2},{2,1},{3,4},{4,3},{5,6},{6,5},{7,8},{8,7},{9,10},{10,9},{11,... | collective-permute-start | bytes 491528 | tf_op jit(solution)/shard_map/ppermute | solution.py:494
  104.2 1.8 %first_rows.1 = (bf16[2,320,128]{2,1,0:T(8,128)(2,1)S(1)}, f32[2,2,320,128]{3,2,1,0:T(8,128)S(1)}) custom-call(s32[5]{0:T(128)S(1)} %stack.19.place, bf16[4,2,320,1600]{3,2,1,0:T(8,128)(2,1)S(1)} %get-tuple-element.31.rows, bf16[4,320,128]{2,1,0:T(8,128)(2,1)S(1)} %get-tuple-element.52.firsts, bf16[4,320,128]{2,1,0:T(8,128)(2,1)S(1)} %get-tuple-element.50.tops, ...), custom_call_target="tpu_custom_call" | custom-call | flops 1024 | bytes 1024 | tf_op jit(solution)/shard_map/first_rows/pallas_call | solution.py:337
  106.0 1.1 collective-permute-start.10
  107.1 2.6 %second_rows.1 = (bf16[8,320,128]{2,1,0:T(8,128)(2,1)}, f32[2,2,320,128]{3,2,1,0:T(8,128)S(1)}) custom-call(s32[2,4]{1,0:T(2,128)S(1)} %copy-done.1, bf16[4,2,320,1600]{3,2,1,0:T(8,128)(2,1)S(1)} %get-tuple-element.31.rows, bf16[4,320,128]{2,1,0:T(8,128)(2,1)S(1)} %get-tuple-element.52.firsts, bf16[4,320,128]{2,1,0:T(8,128)(2,1)S(1)} %get-tuple-element.50.tops, ...), custom_call_target="tpu_custom_call" | custom-call | flops 1024 | bytes 1024 | tf_op jit(solution)/shard_map/second_rows/pallas_call | solution.py:337
  110.5 2.1 %edge_jacobian.1 = bf16[8,320,128]{2,1,0:T(8,128)(2,1)} custom-call(s32[2,4]{1,0:T(2,128)S(1)} %copy-done.1, s32[5]{0:T(128)S(1)} %stack.19.place, bf16[2,320,128]{2,1,0:T(8,128)(2,1)S(1)} %collective-permute-done.8.beside, bf16[4,320,128]{2,1,0:T(8,128)(2,1)S(1)} %collective-permute-done.9.below, bf16[2,320,128]{2,1,0:T(8,128)(2,1)S(1)} %collective-permute-done.10.within, ...), custom_call_target="tpu_custom_call" | custom-call | flops 1024 | bytes 1024 | tf_op jit(solution)/shard_map/edge_jacobian/pallas_call | solution.py:337
  (19 shorter events, 4.7 us)
Async XLA Ops:
  0.7 0.7 copy-start
  5.0 24.7 %collective-permute-start = (bf16[3040,128]{1,0:T(8,128)(2,1)S(1)}, bf16[3040,128]{1,0:T(8,128)(2,1)S(1)}, u32[]{:S(2)}, u32[]{:S(2)}) collective-permute-start(bf16[3040,128]{1,0:T(8,128)(2,1)S(1)} %local_map.3), channel_id=1, source_target_pairs={{0,48},{16,32},{32,16},{48,0},{64,112},{80,96},{96,80},{112,64},{1... | collective-permute-start | bytes 2334728 | tf_op jit(solution)/shard_map/ppermute | solution.py:443
  12.4 30.9 %collective-permute-start.1 = (bf16[3040,128]{1,0:T(8,128)(2,1)S(1)}, bf16[3040,128]{1,0:T(8,128)(2,1)S(1)}, u32[]{:S(2)}, u32[]{:S(2)}) collective-permute-start(bf16[3040,128]{1,0:T(8,128)(2,1)S(1)} %local_map.4), channel_id=1, source_target_pairs={{0,16},{16,0},{32,48},{48,32},{64,80},{80,64},{96,112},{112,96},{1... | collective-permute-start | bytes 2334728 | tf_op jit(solution)/shard_map/ppermute | solution.py:443
  17.3 26.0 %collective-permute-start.2 = (bf16[3040,128]{1,0:T(8,128)(2,1)S(1)}, bf16[3040,128]{1,0:T(8,128)(2,1)S(1)}, u32[]{:S(2)}, u32[]{:S(2)}) collective-permute-start(bf16[3040,128]{1,0:T(8,128)(2,1)S(1)} %local_map.5), channel_id=1, source_target_pairs={{0,32},{16,48},{32,0},{48,16},{64,96},{80,112},{96,64},{112,80},{1... | collective-permute-start | bytes 2334728 | tf_op jit(solution)/shard_map/ppermute | solution.py:443
  46.8 10.5 %collective-permute-start.5 = (bf16[1120,128]{1,0:T(8,128)(2,1)S(1)}, bf16[1120,128]{1,0:T(8,128)(2,1)S(1)}, u32[]{:S(2)}, u32[]{:S(2)}) collective-permute-start(bf16[1120,128]{1,0:T(8,128)(2,1)S(1)} %get-tuple-element.39), channel_id=1, source_target_pairs={{192,128},{208,144},{224,160},{240,176},{193,129},{209,145},{225,1... | collective-permute-start | bytes 860168 | tf_op jit(solution)/shard_map/ppermute | solution.py:440
  49.1 7.2 %collective-permute-start.3 = (bf16[320,128]{1,0:T(8,128)(2,1)S(1)}, bf16[320,128]{1,0:T(8,128)(2,1)S(1)}, u32[]{:S(2)}, u32[]{:S(2)}) collective-permute-start(bf16[320,128]{1,0:T(8,128)(2,1)S(1)} %get-tuple-element.36), channel_id=1, source_target_pairs={{0,64},{16,80},{32,96},{48,112},{1,65},{17,81},{33,97},{49,113},{2... | collective-permute-start | bytes 245768 | tf_op jit(solution)/shard_map/ppermute | solution.py:440
  56.6 0.7 collective-permute-start.4
  58.1 0.7 collective-permute-start.6
  59.6 21.9 %collective-permute-start.7 = (bf16[320,128]{1,0:T(8,128)(2,1)S(1)}, bf16[320,128]{1,0:T(8,128)(2,1)S(1)}, u32[]{:S(2)}, u32[]{:S(2)}) collective-permute-start(bf16[320,128]{1,0:T(8,128)(2,1)S(1)} %backward_one.1), channel_id=1, source_target_pairs={{64,0},{80,16},{96,32},{112,48},{128,192},{144,208},{160,224},{176... | collective-permute-start | bytes 245768 | tf_op jit(solution)/shard_map/ppermute | solution.py:440
  98.9 11.6 %collective-permute-start.9 = (bf16[4,320,128]{2,1,0:T(8,128)(2,1)S(1)}, bf16[4,320,128]{2,1,0:T(8,128)(2,1)S(1)}, u32[]{:S(2)}, u32[]{:S(2)}) collective-permute-start(bf16[4,320,128]{2,1,0:T(8,128)(2,1)S(1)} %get-tuple-element.50.tops), channel_id=1, source_target_pairs={{0,16},{16,32},{32,48},{48,64},{64,80},{80,96},{96,112},{112,128},... | collective-permute-start | bytes 983048 | tf_op jit(solution)/shard_map/ppermute | solution.py:486
  101.7 8.7 %collective-permute-start.8 = (bf16[2,320,128]{2,1,0:T(8,128)(2,1)S(1)}, bf16[2,320,128]{2,1,0:T(8,128)(2,1)S(1)}, u32[]{:S(2)}, u32[]{:S(2)}) collective-permute-start(bf16[2,320,128]{2,1,0:T(8,128)(2,1)S(1)} %get-tuple-element.54), channel_id=1, source_target_pairs={{1,2},{2,1},{3,4},{4,3},{5,6},{6,5},{7,8},{8,7},{9,10},{10,9},{11,... | collective-permute-start | bytes 491528 | tf_op jit(solution)/shard_map/ppermute | solution.py:494
  104.2 2.9 %copy-start.1 = (s32[2,4]{1,0:T(2,128)S(1)}, s32[2,4]{1,0:T(2,128)}, u32[]{:S(2)}) copy-start(s32[2,4]{1,0:T(2,128)} %slots.11) | copy-start | bytes 100
  106.0 4.4 %collective-permute-start.10 = (bf16[2,320,128]{2,1,0:T(8,128)(2,1)S(1)}, bf16[2,320,128]{2,1,0:T(8,128)(2,1)S(1)}, u32[]{:S(2)}, u32[]{:S(2)}) collective-permute-start(bf16[2,320,128]{2,1,0:T(8,128)(2,1)S(1)} %get-tuple-element.55), channel_id=1, source_target_pairs={{0,1},{1,0},{2,3},{3,2},{4,5},{5,4},{6,7},{7,6},{8,9},{9,8},{10,11... | collective-permute-start | bytes 491528 | tf_op jit(solution)/shard_map/ppermute | solution.py:499
